TPU v7x, 32 devices: a whole 2x2x4 slice. The times are simulated.
32 devices in a mesh: leaf: 4 (over z), row: 8 (over y, x, core).
Axes of the slice: x: 2, y: 2, z: 4, core: 2. Of those that a mesh axis runs over, the one named last changes fastest.
Arguments:
- sep_inverse: bfloat16 [4, 6144, 6144], P('leaf', 'row'), may hold values from -8 to 8, as said below
- rhs_block: bfloat16 [4, 6144, 512], P('leaf', 'row'), may hold values from -6 to 6
- coupling: bfloat16 [4, 4096, 6144], P('leaf', 'row'), may hold values from -0.078125 to 0.078125
- ancestor_rows: int32 [4, 4096], P('leaf', 'row'), may hold values from 0 to 4095, as said below
- ancestor_rhs: float32 [4096, 512], P('row', 'leaf'), may hold values from -12 to 12
Outputs:
- solution: bfloat16 [4, 6144, 512], P('leaf', 'row')
- ancestor_out: float32 [4096, 512], P('row', 'leaf')
Inputs may be any that keep to these rules, and one draw needn't show every extreme that they name: Each block sep_inverse[g] is exactly symmetric. For each subtree, ancestor_rows is a one-to-one map of the 4096 coupling rows onto the ancestor rows that keeps every aligned block of 512 rows within itself.
All inputs are finite; a program needn't handle non-finite values.
Results may differ from a plain program's by a relative error of at most 0.014.
Values may be sent and summed in bfloat16 or wider, within the bound.
No kernel may reach another device: no remote copies, remote signals or barrier semaphores. Data moves between devices by JAX's collectives and lax.ppermute only.
A program may use at most 64 MiB of HBM per device.

v0:
```python
import functools

import jax
import jax.numpy as jnp
from jax import lax
from jax.experimental import pallas as pl
from jax.experimental.pallas import tpu as pltpu
from jax.sharding import PartitionSpec as P

VMEM = pl.BlockSpec(memory_space=pltpu.VMEM)
F32 = jnp.float32
BF16 = jnp.bfloat16


def pick_kernel(n, order, src, out, sem):
    width = out.shape[1] // n

    def copy(j):
        start = pl.multiple_of(order[j] * width, 128)
        return pltpu.make_async_copy(
            src.at[:, pl.ds(start, width)], out.at[:, pl.ds(j * width, width)], sem.at[j]
        )

    for j in range(n):
        copy(j).start()
    for j in range(n):
        copy(j).wait()


def column_block(src, start, width):
    return lax.dynamic_slice_in_dim(src, start * width, width, 1)


def pick(src, order, width):
    n = order.shape[0]
    if width % 128:
        return jnp.concatenate([column_block(src, order[j], width) for j in range(n)], axis=1)
    return pl.pallas_call(
        functools.partial(pick_kernel, n),
        out_shape=jax.ShapeDtypeStruct((src.shape[0], n * width), src.dtype),
        in_specs=[pl.BlockSpec(memory_space=pltpu.SMEM), pl.BlockSpec(memory_space=pltpu.HBM)],
        out_specs=VMEM,
        scratch_shapes=[pltpu.SemaphoreType.DMA((n,))],
        compiler_params=pltpu.CompilerParams(vmem_limit_bytes=8 << 20),
        name="pick",
    )(order, pltpu.with_memory_space_constraint(src, pltpu.HBM))


def select_kernel(n, order, places, src, out, buf, sem):
    rows, width = buf.shape[1:]

    def copy(j):
        start = pl.multiple_of(order[j] * width, 128)
        return pltpu.make_async_copy(src.at[:, pl.ds(start, width)], buf.at[j], sem.at[j])

    for j in range(n):
        copy(j).start()
    hot = lax.broadcasted_iota(jnp.int32, (rows, rows), 0) == places[...]
    hot = jnp.where(hot, 1.0, 0.0).astype(BF16)
    for j in range(n):
        copy(j).wait()
        out[:, j * width : (j + 1) * width] = jnp.dot(
            hot, buf[j], preferred_element_type=F32
        ).astype(BF16)


def select_rows(src, places, order, width):
    rows = src.shape[0]
    n = order.shape[0]
    if width % 128:
        hot = (lax.broadcasted_iota(jnp.int32, (rows, rows), 0) == places).astype(src.dtype)
        return hot @ pick(src, order, width)
    return pl.pallas_call(
        functools.partial(select_kernel, n),
        out_shape=jax.ShapeDtypeStruct((rows, n * width), src.dtype),
        in_specs=[
            pl.BlockSpec(memory_space=pltpu.SMEM),
            VMEM,
            pl.BlockSpec(memory_space=pltpu.HBM),
        ],
        out_specs=VMEM,
        scratch_shapes=[
            pltpu.VMEM((n, rows, width), src.dtype),
            pltpu.SemaphoreType.DMA((n,)),
        ],
        compiler_params=pltpu.CompilerParams(vmem_limit_bytes=12 << 20),
        name="select_rows",
    )(order, places, pltpu.with_memory_space_constraint(src, pltpu.HBM))


def partial_kernel(n, keep, swap, *refs):
    pieces, (own, other, joined) = refs[:n], refs[n:]
    depth = pieces[0].shape[0]
    for j in range(n):
        joined[j * depth : (j + 1) * depth, :] = pieces[j][...]
    other[...] = jnp.dot(swap[...], joined[...], preferred_element_type=F32).astype(BF16)
    own[...] = jnp.dot(keep[...], joined[...], preferred_element_type=F32)


def partials(keep, swap, pieces):
    n = len(pieces)
    rows, depth = keep.shape
    width = pieces[0].shape[1]
    return pl.pallas_call(
        functools.partial(partial_kernel, n),
        out_shape=(
            jax.ShapeDtypeStruct((rows, width), F32),
            jax.ShapeDtypeStruct((rows, width), BF16),
        ),
        in_specs=[VMEM] * (2 + n),
        out_specs=(VMEM, VMEM),
        scratch_shapes=[pltpu.VMEM((depth, width), BF16)],
        compiler_params=pltpu.CompilerParams(vmem_limit_bytes=12 << 20),
        name="partials",
    )(keep, swap, *pieces)


def on_device(sep_inverse, rhs_block, coupling, ancestor_rows, ancestor_rhs):
    inverse, rhs, couple = sep_inverse[0], rhs_block[0], coupling[0]
    leaves, n_row = lax.axis_size("leaf"), lax.axis_size("row")
    leaf, me = lax.axis_index("leaf"), lax.axis_index("row")
    core = me & 1
    rows = inverse.shape[0]
    anc = couple.shape[0]
    width = rhs.shape[1]
    narrow = width // leaves
    dims = [1 << b for b in range(1, n_row.bit_length() - 1)]
    routes = (dims, dims[::-1])
    masks = ([0], [0])
    for step in range(len(dims)):
        for k in (0, 1):
            masks[k].extend([m ^ routes[k][step] for m in masks[k]])

    def partner(x):
        return lax.ppermute(x, "row", [(i, i ^ 1) for i in range(n_row)])

    def gather(x):
        pieces = [x]
        for step in range(len(dims)):
            pairs = [(i, i ^ routes[i & 1][step]) for i in range(n_row)]
            for p in range(len(pieces)):
                pieces.append(lax.ppermute(pieces[p], "row", pairs))
        return pieces

    mask = jnp.where(core == 0, jnp.array(masks[0], jnp.int32), jnp.array(masks[1], jnp.int32))
    mask_other = jnp.where(core == 0, jnp.array(masks[1], jnp.int32), jnp.array(masks[0], jnp.int32))
    keep_order = me ^ mask
    send_order = (me ^ 1) ^ mask_other

    edge = leaves // 4
    inner = (leaf >= edge) & (leaf < leaves - edge)
    cut = edge * narrow

    def outer_cols(x):
        return jnp.concatenate([x[:, :cut], x[:, width - cut :]], axis=1)

    def inner_cols(x):
        return x[:, cut : width - cut]

    chunks = (
        (outer_cols(rhs), [j for j in range(leaves) if j < edge or j >= leaves - edge]),
        (inner_cols(rhs), [j for j in range(leaves) if edge <= j < leaves - edge]),
    )

    gathered = [gather(x) for x, _ in chunks]

    def swapped(block):
        sent = block(send_order)
        return partner(sent)

    def kept(block):
        return block(keep_order)

    places = (ancestor_rows - me * anc).astype(jnp.int32)
    cpl_block = lambda order: select_rows(couple, places, order, rows)
    a_swap = swapped(lambda order: pick(inverse, order, rows))
    a_keep = kept(lambda order: pick(inverse, order, rows))
    c_swap = swapped(cpl_block)
    c_keep = kept(cpl_block)

    solved = []
    for pieces in gathered:
        own, other = partials(a_keep, a_swap, pieces)
        other = partner(other)
        solved.append((own + other.astype(F32)).astype(BF16))

    shares = []
    for (_, dests), y in zip(chunks, solved):
        pieces = gather(y)
        own, other = partials(c_keep, c_swap, pieces)
        q = own + partner(other).astype(F32)

        def piece(target):
            place = sum(jnp.where(target == j, i, 0) for i, j in enumerate(dests))
            return lax.dynamic_slice_in_dim(q, place * narrow, narrow, 1)

        total = piece(leaf)
        for d in range(1, leaves):
            sent = piece(leaf ^ d).astype(BF16)
            got = lax.ppermute(sent, "leaf", [(j ^ d, j) for j in dests])
            total = total + got.astype(F32)
        shares.append(total)

    out = ancestor_rhs - jnp.where(inner, shares[1], shares[0])
    y_outer, y_inner = solved
    solution = jnp.concatenate([y_outer[:, :cut], y_inner, y_outer[:, cut:]], axis=1)
    return (solution[None], out)


def solution(mesh):
    return jax.shard_map(
        on_device,
        mesh=mesh,
        in_specs=(
            P("leaf", "row", None),
            P("leaf", "row", None),
            P("leaf", "row", None),
            P("leaf", "row"),
            P("row", "leaf"),
        ),
        out_specs=(P("leaf", "row", None), P("row", "leaf")),
        check_vma=False,
    )
```

profile of v0, /device:TPU:0, one launch (start us, length us, event | category | flops | bytes accessed | tf_op | source)
XLA Modules:
  0.0 104.5 jit_solution(3586568637921366050)
XLA Ops:
  0.6 0.7 fusion.1
  1.3 5.1 %pick.3 = bf16[768,3072]{1,0:T(8,128)(2,1)} custom-call(s32[4]{0:T(128)S(1)} %get-tuple-element.28.order, bf16[768,6144]{1,0:T(8,128)(2,1)} %bitcast.5), custom_call_target="tpu_custom_call" | custom-call | tf_op jit(solution)/shard_map/pick/pallas_call | solution.py:38
  6.4 0.6 collective-permute-start
  7.0 4.5 %select_rows.3 = bf16[512,3072]{1,0:T(8,128)(2,1)S(1)} custom-call(s32[4]{0:T(128)S(1)} %get-tuple-element.28.order, s32[1,512]{1,0:T(1,128)S(1)} %broadcast_subtract_fusion.places, bf16[512,6144]{1,0:T(8,128)(2,1)} %bitcast.7), custom_call_target="tpu_custom_call" | custom-call | tf_op jit(solution)/shard_map/select_rows/pallas_call | solution.py:73
  11.5 0.1 collective-permute-start.9
  11.7 3.0 %collective-permute-start.1 = (bf16[768,256]{1,0:T(8,128)(2,1)S(1)}, bf16[768,256]{1,0:T(8,128)(2,1)S(1)}, u32[]{:S(2)}, u32[]{:S(2)}) collective-permute-start(bf16[768,256]{1,0:T(8,128)(2,1)S(1)} %pad_maximum_fusion.refs_0_), channel_id=1, source_target_pairs={{0,2},{1,5},{2,0},{3,7},{4,6},{5,1},{6,4},{7,3},{8,10},{9,13},{10,... | collective-permute-start | bytes 1179656 | tf_op jit(solution)/shard_map/ppermute | solution.py:142
  14.7 1.5 %collective-permute-start.2 = (bf16[768,256]{1,0:T(8,128)(2,1)S(1)}, bf16[768,256]{1,0:T(8,128)(2,1)S(1)}, u32[]{:S(2)}, u32[]{:S(2)}) collective-permute-start(bf16[768,256]{1,0:T(8,128)(2,1)S(1)} %pad_maximum_fusion.refs_0_), channel_id=1, source_target_pairs={{0,4},{1,3},{2,6},{3,1},{4,0},{5,7},{6,2},{7,5},{8,12},{9,11},{10,... | collective-permute-start | bytes 1179656 | tf_op jit(solution)/shard_map/ppermute | solution.py:142
  16.2 0.6 collective-permute-start.5
  16.8 7.1 %collective-permute-done.1.refs_1_ = bf16[768,256]{1,0:T(8,128)(2,1)S(1)} collective-permute-done((bf16[768,256]{1,0:T(8,128)(2,1)S(1)}, bf16[768,256]{1,0:T(8,128)(2,1)S(1)}, u32[]{:S(2)}, u32[]{:S(2)}) %collective-permute-start.1) | collective-permute-done | bytes 393248 | tf_op jit(solution)/shard_map/ppermute | solution.py:142
  23.9 2.0 %collective-permute-start.3 = (bf16[768,256]{1,0:T(8,128)(2,1)S(1)}, bf16[768,256]{1,0:T(8,128)(2,1)S(1)}, u32[]{:S(2)}, u32[]{:S(2)}) collective-permute-start(bf16[768,256]{1,0:T(8,128)(2,1)S(1)} %collective-permute-done.1.refs_1_), channel_id=1, source_target_pairs={{0,4},{1,3},{2,6},{3,1},{4,0},{5,7},{6,2},{7,5},{8,12},{9,11},{10,... | collective-permute-start | bytes 1179656 | tf_op jit(solution)/shard_map/ppermute | solution.py:142
  25.8 0.8 collective-permute-done.2.refs_2_
  26.7 1.5 %collective-permute-start.6 = (bf16[768,256]{1,0:T(8,128)(2,1)S(1)}, bf16[768,256]{1,0:T(8,128)(2,1)S(1)}, u32[]{:S(2)}, u32[]{:S(2)}) collective-permute-start(bf16[768,256]{1,0:T(8,128)(2,1)S(1)} %slice.23.refs_0_), channel_id=1, source_target_pairs={{0,4},{1,3},{2,6},{3,1},{4,0},{5,7},{6,2},{7,5},{8,12},{9,11},{10,... | collective-permute-start | bytes 1179656 | tf_op jit(solution)/shard_map/ppermute | solution.py:142
  28.2 3.8 %collective-permute-done.5.refs_1_ = bf16[768,256]{1,0:T(8,128)(2,1)S(1)} collective-permute-done((bf16[768,256]{1,0:T(8,128)(2,1)S(1)}, bf16[768,256]{1,0:T(8,128)(2,1)S(1)}, u32[]{:S(2)}, u32[]{:S(2)}) %collective-permute-start.5) | collective-permute-done | bytes 393248 | tf_op jit(solution)/shard_map/ppermute | solution.py:142
  32.0 1.3 %collective-permute-start.7 = (bf16[768,256]{1,0:T(8,128)(2,1)S(1)}, bf16[768,256]{1,0:T(8,128)(2,1)S(1)}, u32[]{:S(2)}, u32[]{:S(2)}) collective-permute-start(bf16[768,256]{1,0:T(8,128)(2,1)S(1)} %collective-permute-done.5.refs_1_), channel_id=1, source_target_pairs={{0,4},{1,3},{2,6},{3,1},{4,0},{5,7},{6,2},{7,5},{8,12},{9,11},{10,... | collective-permute-start | bytes 1179656 | tf_op jit(solution)/shard_map/ppermute | solution.py:142
  33.4 2.9 %pick.2.keep = bf16[768,3072]{1,0:T(8,128)(2,1)S(1)} custom-call(s32[4]{0:T(128)S(1)} %get-tuple-element.29.order, bf16[768,6144]{1,0:T(8,128)(2,1)} %bitcast.6), custom_call_target="tpu_custom_call" | custom-call | tf_op jit(solution)/shard_map/pick/pallas_call | solution.py:38
  36.3 0.0 collective-permute-done.3.refs_3_
  36.3 0.0 collective-permute-done.swap
  36.3 4.9 %partials.4 = (f32[768,256]{1,0:T(8,128)S(1)}, bf16[768,256]{1,0:T(8,128)(2,1)S(1)}) custom-call(bf16[768,3072]{1,0:T(8,128)(2,1)S(1)} %pick.2.keep, bf16[768,3072]{1,0:T(8,128)(2,1)} %collective-permute-done.swap, bf16[768,256]{1,0:T(8,128)(2,1)S(1)} %pad_maximum_fusion.refs_0_, bf16[768,256]{1,0:T(8,128)(2,1)S(1)} %collective-permute-done.1.refs_1_, ...), custom_call_target="tpu_custom_call" | custom-call | tf_op jit(solution)/shard_map/partials/pallas_call | solution.py:104
  41.2 0.1 collective-permute-start.4
  41.3 0.0 collective-permute-done.6.refs_2_
  41.3 4.9 %partials.5 = (f32[768,256]{1,0:T(8,128)S(1)}, bf16[768,256]{1,0:T(8,128)(2,1)S(1)}) custom-call(bf16[768,3072]{1,0:T(8,128)(2,1)S(1)} %pick.2.keep, bf16[768,3072]{1,0:T(8,128)(2,1)} %collective-permute-done.swap, bf16[768,256]{1,0:T(8,128)(2,1)S(1)} %slice.23.refs_0_, bf16[768,256]{1,0:T(8,128)(2,1)S(1)} %collective-permute-done.5.refs_1_, ...), custom_call_target="tpu_custom_call" | custom-call | tf_op jit(solution)/shard_map/partials/pallas_call | solution.py:104
  46.3 0.5 collective-permute-start.8
  46.8 0.0 collective-permute-done.4
  46.8 0.1 add_convert_fusion.1.refs_0_
  46.9 1.6 %collective-permute-start.17 = (bf16[768,256]{1,0:T(8,128)(2,1)S(1)}, bf16[768,256]{1,0:T(8,128)(2,1)S(1)}, u32[]{:S(2)}, u32[]{:S(2)}) collective-permute-start(bf16[768,256]{1,0:T(8,128)(2,1)S(1)} %add_convert_fusion.1.refs_0_), channel_id=1, source_target_pairs={{0,2},{1,5},{2,0},{3,7},{4,6},{5,1},{6,4},{7,3},{8,10},{9,13},{10,... | collective-permute-start | bytes 1179656 | tf_op jit(solution)/shard_map/ppermute | solution.py:142
  48.5 0.0 collective-permute-done.8
  48.5 0.9 add_convert_fusion.refs_0_
  49.4 1.2 %collective-permute-start.10 = (bf16[768,256]{1,0:T(8,128)(2,1)}, bf16[768,256]{1,0:T(8,128)(2,1)}, u32[]{:S(2)}, u32[]{:S(2)}) collective-permute-start(bf16[768,256]{1,0:T(8,128)(2,1)} %add_convert_fusion.refs_0_), channel_id=1, source_target_pairs={{0,2},{1,5},{2,0},{3,7},{4,6},{5,1},{6,4},{7,3},{8,10},{9,13},{10,... | collective-permute-start | bytes 1179656 | tf_op jit(solution)/shard_map/ppermute | solution.py:142
  50.6 1.5 %collective-permute-start.18 = (bf16[768,256]{1,0:T(8,128)(2,1)S(1)}, bf16[768,256]{1,0:T(8,128)(2,1)S(1)}, u32[]{:S(2)}, u32[]{:S(2)}) collective-permute-start(bf16[768,256]{1,0:T(8,128)(2,1)S(1)} %add_convert_fusion.1.refs_0_), channel_id=1, source_target_pairs={{0,4},{1,3},{2,6},{3,1},{4,0},{5,7},{6,2},{7,5},{8,12},{9,11},{10,... | collective-permute-start | bytes 1179656 | tf_op jit(solution)/shard_map/ppermute | solution.py:142
  52.0 4.5 %collective-permute-done.17.refs_1_ = bf16[768,256]{1,0:T(8,128)(2,1)S(1)} collective-permute-done((bf16[768,256]{1,0:T(8,128)(2,1)S(1)}, bf16[768,256]{1,0:T(8,128)(2,1)S(1)}, u32[]{:S(2)}, u32[]{:S(2)}) %collective-permute-start.17) | collective-permute-done | bytes 393248 | tf_op jit(solution)/shard_map/ppermute | solution.py:142
  56.5 1.2 %collective-permute-start.19 = (bf16[768,256]{1,0:T(8,128)(2,1)S(1)}, bf16[768,256]{1,0:T(8,128)(2,1)S(1)}, u32[]{:S(2)}, u32[]{:S(2)}) collective-permute-start(bf16[768,256]{1,0:T(8,128)(2,1)S(1)} %collective-permute-done.17.refs_1_), channel_id=1, source_target_pairs={{0,4},{1,3},{2,6},{3,1},{4,0},{5,7},{6,2},{7,5},{8,12},{9,11},{10,... | collective-permute-start | bytes 1179656 | tf_op jit(solution)/shard_map/ppermute | solution.py:142
  57.7 0.8 collective-permute-start.11
  58.6 6.5 %collective-permute-done.10.refs_1_ = bf16[768,256]{1,0:T(8,128)(2,1)} collective-permute-done((bf16[768,256]{1,0:T(8,128)(2,1)}, bf16[768,256]{1,0:T(8,128)(2,1)}, u32[]{:S(2)}, u32[]{:S(2)}) %collective-permute-start.10) | collective-permute-done | bytes 393248 | tf_op jit(solution)/shard_map/ppermute | solution.py:142
  65.1 1.2 %collective-permute-start.12 = (bf16[768,256]{1,0:T(8,128)(2,1)}, bf16[768,256]{1,0:T(8,128)(2,1)}, u32[]{:S(2)}, u32[]{:S(2)}) collective-permute-start(bf16[768,256]{1,0:T(8,128)(2,1)} %collective-permute-done.10.refs_1_), channel_id=1, source_target_pairs={{0,4},{1,3},{2,6},{3,1},{4,0},{5,7},{6,2},{7,5},{8,12},{9,11},{10,... | collective-permute-start | bytes 1179656 | tf_op jit(solution)/shard_map/ppermute | solution.py:142
  66.3 4.5 %select_rows.2.keep = bf16[512,3072]{1,0:T(8,128)(2,1)S(1)} custom-call(s32[4]{0:T(128)S(1)} %get-tuple-element.29.order, s32[1,512]{1,0:T(1,128)S(1)} %broadcast_subtract_fusion.places, bf16[512,6144]{1,0:T(8,128)(2,1)} %bitcast.8), custom_call_target="tpu_custom_call" | custom-call | tf_op jit(solution)/shard_map/select_rows/pallas_call | solution.py:73
  70.8 0.0 collective-permute-done.9.swap
  70.8 0.0 collective-permute-done.19.refs_3_
  70.8 2.5 %partials.7 = (f32[512,256]{1,0:T(8,128)S(1)}, bf16[512,256]{1,0:T(8,128)(2,1)}) custom-call(bf16[512,3072]{1,0:T(8,128)(2,1)S(1)} %select_rows.2.keep, bf16[512,3072]{1,0:T(8,128)(2,1)S(1)} %collective-permute-done.9.swap, bf16[768,256]{1,0:T(8,128)(2,1)S(1)} %add_convert_fusion.1.refs_0_, bf16[768,256]{1,0:T(8,128)(2,1)S(1)} %collective-permute-done.17.refs_1_, ...), custom_call_target="tpu_custom_call" | custom-call | tf_op jit(solution)/shard_map/partials/pallas_call | solution.py:104
  73.3 0.8 copy-done.2
  74.2 0.0 collective-permute-done.11.refs_2_
  74.2 0.8 collective-permute-done.12.refs_3_
  75.0 1.9 %copy-done.1 = bf16[512,3072]{1,0:T(8,128)(2,1)S(1)} copy-done((bf16[512,3072]{1,0:T(8,128)(2,1)S(1)}, bf16[512,3072]{1,0:T(8,128)(2,1)}, u32[]{:S(2)}) %copy-start.1) | copy-done | bytes 3145752
  76.9 3.1 %partials.6 = (f32[512,256]{1,0:T(8,128)S(1)}, bf16[512,256]{1,0:T(8,128)(2,1)S(1)}) custom-call(bf16[512,3072]{1,0:T(8,128)(2,1)S(1)} %select_rows.2.keep, bf16[512,3072]{1,0:T(8,128)(2,1)S(1)} %copy-done.1, bf16[768,256]{1,0:T(8,128)(2,1)} %add_convert_fusion.refs_0_, bf16[768,256]{1,0:T(8,128)(2,1)} %collective-permute-done.10.refs_1_, ...), custom_call_target="tpu_custom_call" | custom-call | tf_op jit(solution)/shard_map/partials/pallas_call | solution.py:104
  80.0 0.0 copy-start.5
  80.0 0.8 collective-permute-start.13
  80.9 1.0 convert_add_fusion
  81.9 0.1 dynamic-slice_convert_fusion.2
  81.9 6.1 %collective-permute-start.23 = (bf16[512,128]{1,0:T(8,128)(2,1)S(1)}, bf16[512,128]{1,0:T(8,128)(2,1)S(1)}, u32[]{:S(2)}, u32[]{:S(2)}) collective-permute-start(bf16[512,128]{1,0:T(8,128)(2,1)S(1)} %get-tuple-element.24), channel_id=1, source_target_pairs={{24,0},{0,24},{25,1},{1,25},{26,2},{2,26},{27,3},{3,27},{28,4},{4,... | collective-permute-start | bytes 393224 | tf_op jit(solution)/shard_map/ppermute | solution.py:200
  88.1 1.3 %collective-permute-start.22 = (bf16[512,128]{1,0:T(8,128)(2,1)S(1)}, bf16[512,128]{1,0:T(8,128)(2,1)S(1)}, u32[]{:S(2)}, u32[]{:S(2)}) collective-permute-start(bf16[512,128]{1,0:T(8,128)(2,1)S(1)} %get-tuple-element.25), channel_id=1, source_target_pairs={{16,0},{8,24},{17,1},{9,25},{18,2},{10,26},{19,3},{11,27},{20,4},{... | collective-permute-start | bytes 393224 | tf_op jit(solution)/shard_map/ppermute | solution.py:200
  89.4 1.3 %collective-permute-start.21 = (bf16[512,128]{1,0:T(8,128)(2,1)S(1)}, bf16[512,128]{1,0:T(8,128)(2,1)S(1)}, u32[]{:S(2)}, u32[]{:S(2)}) collective-permute-start(bf16[512,128]{1,0:T(8,128)(2,1)S(1)} %get-tuple-element.23), channel_id=1, source_target_pairs={{8,0},{16,24},{9,1},{17,25},{10,2},{18,26},{11,3},{19,27},{12,4},{... | collective-permute-start | bytes 393224 | tf_op jit(solution)/shard_map/ppermute | solution.py:200
  90.7 0.0 collective-permute-done.13
  90.7 0.1 convert_add_fusion.1
  90.8 0.1 dynamic-slice_convert_fusion.5
  90.8 0.7 collective-permute-start.16
  91.5 7.3 %collective-permute-start.15 = (bf16[512,128]{1,0:T(8,128)(2,1)S(1)}, bf16[512,128]{1,0:T(8,128)(2,1)S(1)}, u32[]{:S(2)}, u32[]{:S(2)}) collective-permute-start(bf16[512,128]{1,0:T(8,128)(2,1)S(1)} %get-tuple-element.22), channel_id=1, source_target_pairs={{24,8},{0,16},{25,9},{1,17},{26,10},{2,18},{27,11},{3,19},{28,12},... | collective-permute-start | bytes 393224 | tf_op jit(solution)/shard_map/ppermute | solution.py:200
  98.8 0.0 collective-permute-done.23
  98.8 1.3 %collective-permute-start.14 = (bf16[512,128]{1,0:T(8,128)(2,1)S(1)}, bf16[512,128]{1,0:T(8,128)(2,1)S(1)}, u32[]{:S(2)}, u32[]{:S(2)}) collective-permute-start(bf16[512,128]{1,0:T(8,128)(2,1)S(1)} %get-tuple-element.20), channel_id=1, source_target_pairs={{0,8},{24,16},{1,9},{25,17},{2,10},{26,18},{3,11},{27,19},{4,12},{... | collective-permute-start | bytes 393224 | tf_op jit(solution)/shard_map/ppermute | solution.py:200
  100.1 2.0 %maximum_bitcast_fusion = bf16[1,768,512]{2,1,0:T(8,128)(2,1)} fusion(bf16[768,128]{1,0:T(8,128)(2,1)S(1)} %get-tuple-element.27, bf16[768,256]{1,0:T(8,128)(2,1)} %add_convert_fusion.refs_0_, bf16[768,128]{1,0:T(8,128)(2,1)S(1)} %get-tuple-element.26), kind=kLoop, calls=%fused_computation | loop fusion | flops 2359296 | bytes 1572864 | tf_op jit(solution)/shard_map/broadcast_in_dim | solution.py:207
  102.1 0.0 collective-permute-done.22
  102.1 0.0 collective-permute-done.21
  102.1 0.0 collective-permute-done.16
  102.1 0.2 collective-permute-done.15
  102.3 1.4 %collective-permute-done.14 = bf16[512,128]{1,0:T(8,128)(2,1)S(1)} collective-permute-done((bf16[512,128]{1,0:T(8,128)(2,1)S(1)}, bf16[512,128]{1,0:T(8,128)(2,1)S(1)}, u32[]{:S(2)}, u32[]{:S(2)}) %collective-permute-start.14) | collective-permute-done | bytes 131104 | tf_op jit(solution)/shard_map/ppermute | solution.py:200
  103.7 0.8 select_subtract_fusion
  (20 shorter events, 0.2 us)
Async XLA Ops:
  1.3 5.6 %copy-start.6 = (s32[1,512]{1,0:T(1,128)S(1)}, s32[1,512]{1,0:T(1,128)}, u32[]{:S(2)}) copy-start(s32[1,512]{1,0:T(1,128)} %param.12) | copy-start | bytes 6148
  6.4 29.9 %collective-permute-start = (bf16[768,3072]{1,0:T(8,128)(2,1)}, bf16[768,3072]{1,0:T(8,128)(2,1)}, u32[]{:S(2)}, u32[]{:S(2)}) collective-permute-start(bf16[768,3072]{1,0:T(8,128)(2,1)} %pick.3), channel_id=1, source_target_pairs={{0,1},{1,0},{2,3},{3,2},{4,5},{5,4},{6,7},{7,6},{8,9},{9,8},{10,11... | collective-permute-start | bytes 14155784 | tf_op jit(solution)/shard_map/ppermute | solution.py:135
  7.0 4.6 %copy-start.4 = (bf16[1,768,512]{2,1,0:T(8,128)(2,1)S(1)}, bf16[1,768,512]{2,1,0:T(8,128)(2,1)}, u32[]{:S(2)}) copy-start(bf16[1,768,512]{2,1,0:T(8,128)(2,1)} %param.10) | copy-start | bytes 2359300
  11.5 59.3 %collective-permute-start.9 = (bf16[512,3072]{1,0:T(8,128)(2,1)S(1)}, bf16[512,3072]{1,0:T(8,128)(2,1)S(1)}, u32[]{:S(2)}, u32[]{:S(2)}) collective-permute-start(bf16[512,3072]{1,0:T(8,128)(2,1)S(1)} %select_rows.3), channel_id=1, source_target_pairs={{0,1},{1,0},{2,3},{3,2},{4,5},{5,4},{6,7},{7,6},{8,9},{9,8},{10,11... | collective-permute-start | bytes 9437192 | tf_op jit(solution)/shard_map/ppermute | solution.py:135
  11.7 12.2 %collective-permute-start.1 = (bf16[768,256]{1,0:T(8,128)(2,1)S(1)}, bf16[768,256]{1,0:T(8,128)(2,1)S(1)}, u32[]{:S(2)}, u32[]{:S(2)}) collective-permute-start(bf16[768,256]{1,0:T(8,128)(2,1)S(1)} %pad_maximum_fusion.refs_0_), channel_id=1, source_target_pairs={{0,2},{1,5},{2,0},{3,7},{4,6},{5,1},{6,4},{7,3},{8,10},{9,13},{10,... | collective-permute-start | bytes 1179656 | tf_op jit(solution)/shard_map/ppermute | solution.py:142
  14.7 12.0 %collective-permute-start.2 = (bf16[768,256]{1,0:T(8,128)(2,1)S(1)}, bf16[768,256]{1,0:T(8,128)(2,1)S(1)}, u32[]{:S(2)}, u32[]{:S(2)}) collective-permute-start(bf16[768,256]{1,0:T(8,128)(2,1)S(1)} %pad_maximum_fusion.refs_0_), channel_id=1, source_target_pairs={{0,4},{1,3},{2,6},{3,1},{4,0},{5,7},{6,2},{7,5},{8,12},{9,11},{10,... | collective-permute-start | bytes 1179656 | tf_op jit(solution)/shard_map/ppermute | solution.py:142
  16.2 15.8 %collective-permute-start.5 = (bf16[768,256]{1,0:T(8,128)(2,1)S(1)}, bf16[768,256]{1,0:T(8,128)(2,1)S(1)}, u32[]{:S(2)}, u32[]{:S(2)}) collective-permute-start(bf16[768,256]{1,0:T(8,128)(2,1)S(1)} %slice.23.refs_0_), channel_id=1, source_target_pairs={{0,2},{1,5},{2,0},{3,7},{4,6},{5,1},{6,4},{7,3},{8,10},{9,13},{10,... | collective-permute-start | bytes 1179656 | tf_op jit(solution)/shard_map/ppermute | solution.py:142
  23.9 12.4 %collective-permute-start.3 = (bf16[768,256]{1,0:T(8,128)(2,1)S(1)}, bf16[768,256]{1,0:T(8,128)(2,1)S(1)}, u32[]{:S(2)}, u32[]{:S(2)}) collective-permute-start(bf16[768,256]{1,0:T(8,128)(2,1)S(1)} %collective-permute-done.1.refs_1_), channel_id=1, source_target_pairs={{0,4},{1,3},{2,6},{3,1},{4,0},{5,7},{6,2},{7,5},{8,12},{9,11},{10,... | collective-permute-start | bytes 1179656 | tf_op jit(solution)/shard_map/ppermute | solution.py:142
  26.7 14.7 %collective-permute-start.6 = (bf16[768,256]{1,0:T(8,128)(2,1)S(1)}, bf16[768,256]{1,0:T(8,128)(2,1)S(1)}, u32[]{:S(2)}, u32[]{:S(2)}) collective-permute-start(bf16[768,256]{1,0:T(8,128)(2,1)S(1)} %slice.23.refs_0_), channel_id=1, source_target_pairs={{0,4},{1,3},{2,6},{3,1},{4,0},{5,7},{6,2},{7,5},{8,12},{9,11},{10,... | collective-permute-start | bytes 1179656 | tf_op jit(solution)/shard_map/ppermute | solution.py:142
  32.0 9.3 %collective-permute-start.7 = (bf16[768,256]{1,0:T(8,128)(2,1)S(1)}, bf16[768,256]{1,0:T(8,128)(2,1)S(1)}, u32[]{:S(2)}, u32[]{:S(2)}) collective-permute-start(bf16[768,256]{1,0:T(8,128)(2,1)S(1)} %collective-permute-done.5.refs_1_), channel_id=1, source_target_pairs={{0,4},{1,3},{2,6},{3,1},{4,0},{5,7},{6,2},{7,5},{8,12},{9,11},{10,... | collective-permute-start | bytes 1179656 | tf_op jit(solution)/shard_map/ppermute | solution.py:142
  41.2 5.6 %collective-permute-start.4 = (bf16[768,256]{1,0:T(8,128)(2,1)S(1)}, bf16[768,256]{1,0:T(8,128)(2,1)S(1)}, u32[]{:S(2)}, u32[]{:S(2)}) collective-permute-start(bf16[768,256]{1,0:T(8,128)(2,1)S(1)} %get-tuple-element.11), channel_id=1, source_target_pairs={{0,1},{1,0},{2,3},{3,2},{4,5},{5,4},{6,7},{7,6},{8,9},{9,8},{10,11... | collective-permute-start | bytes 1179656 | tf_op jit(solution)/shard_map/ppermute | solution.py:135
  46.3 2.3 %collective-permute-start.8 = (bf16[768,256]{1,0:T(8,128)(2,1)S(1)}, bf16[768,256]{1,0:T(8,128)(2,1)S(1)}, u32[]{:S(2)}, u32[]{:S(2)}) collective-permute-start(bf16[768,256]{1,0:T(8,128)(2,1)S(1)} %get-tuple-element.13), channel_id=1, source_target_pairs={{0,1},{1,0},{2,3},{3,2},{4,5},{5,4},{6,7},{7,6},{8,9},{9,8},{10,11... | collective-permute-start | bytes 1179656 | tf_op jit(solution)/shard_map/ppermute | solution.py:135
  46.9 9.6 %collective-permute-start.17 = (bf16[768,256]{1,0:T(8,128)(2,1)S(1)}, bf16[768,256]{1,0:T(8,128)(2,1)S(1)}, u32[]{:S(2)}, u32[]{:S(2)}) collective-permute-start(bf16[768,256]{1,0:T(8,128)(2,1)S(1)} %add_convert_fusion.1.refs_0_), channel_id=1, source_target_pairs={{0,2},{1,5},{2,0},{3,7},{4,6},{5,1},{6,4},{7,3},{8,10},{9,13},{10,... | collective-permute-start | bytes 1179656 | tf_op jit(solution)/shard_map/ppermute | solution.py:142
  49.4 15.7 %collective-permute-start.10 = (bf16[768,256]{1,0:T(8,128)(2,1)}, bf16[768,256]{1,0:T(8,128)(2,1)}, u32[]{:S(2)}, u32[]{:S(2)}) collective-permute-start(bf16[768,256]{1,0:T(8,128)(2,1)} %add_convert_fusion.refs_0_), channel_id=1, source_target_pairs={{0,2},{1,5},{2,0},{3,7},{4,6},{5,1},{6,4},{7,3},{8,10},{9,13},{10,... | collective-permute-start | bytes 1179656 | tf_op jit(solution)/shard_map/ppermute | solution.py:142
  50.6 20.2 %collective-permute-start.18 = (bf16[768,256]{1,0:T(8,128)(2,1)S(1)}, bf16[768,256]{1,0:T(8,128)(2,1)S(1)}, u32[]{:S(2)}, u32[]{:S(2)}) collective-permute-start(bf16[768,256]{1,0:T(8,128)(2,1)S(1)} %add_convert_fusion.1.refs_0_), channel_id=1, source_target_pairs={{0,4},{1,3},{2,6},{3,1},{4,0},{5,7},{6,2},{7,5},{8,12},{9,11},{10,... | collective-permute-start | bytes 1179656 | tf_op jit(solution)/shard_map/ppermute | solution.py:142
  56.5 14.3 %collective-permute-start.19 = (bf16[768,256]{1,0:T(8,128)(2,1)S(1)}, bf16[768,256]{1,0:T(8,128)(2,1)S(1)}, u32[]{:S(2)}, u32[]{:S(2)}) collective-permute-start(bf16[768,256]{1,0:T(8,128)(2,1)S(1)} %collective-permute-done.17.refs_1_), channel_id=1, source_target_pairs={{0,4},{1,3},{2,6},{3,1},{4,0},{5,7},{6,2},{7,5},{8,12},{9,11},{10,... | collective-permute-start | bytes 1179656 | tf_op jit(solution)/shard_map/ppermute | solution.py:142
  57.7 16.4 %collective-permute-start.11 = (bf16[768,256]{1,0:T(8,128)(2,1)}, bf16[768,256]{1,0:T(8,128)(2,1)}, u32[]{:S(2)}, u32[]{:S(2)}) collective-permute-start(bf16[768,256]{1,0:T(8,128)(2,1)} %add_convert_fusion.refs_0_), channel_id=1, source_target_pairs={{0,4},{1,3},{2,6},{3,1},{4,0},{5,7},{6,2},{7,5},{8,12},{9,11},{10,... | collective-permute-start | bytes 1179656 | tf_op jit(solution)/shard_map/ppermute | solution.py:142
  65.1 9.9 %collective-permute-start.12 = (bf16[768,256]{1,0:T(8,128)(2,1)}, bf16[768,256]{1,0:T(8,128)(2,1)}, u32[]{:S(2)}, u32[]{:S(2)}) collective-permute-start(bf16[768,256]{1,0:T(8,128)(2,1)} %collective-permute-done.10.refs_1_), channel_id=1, source_target_pairs={{0,4},{1,3},{2,6},{3,1},{4,0},{5,7},{6,2},{7,5},{8,12},{9,11},{10,... | collective-permute-start | bytes 1179656 | tf_op jit(solution)/shard_map/ppermute | solution.py:142
  70.8 2.5 %copy-start = (bf16[512,3072]{1,0:T(8,128)(2,1)}, bf16[512,3072]{1,0:T(8,128)(2,1)S(1)}, u32[]{:S(2)}) copy-start(bf16[512,3072]{1,0:T(8,128)(2,1)S(1)} %collective-permute-done.9.swap) | copy-start | bytes 9437188
  73.3 0.8 copy-start.2
  74.1 6.7 %collective-permute-start.20 = (bf16[512,256]{1,0:T(8,128)(2,1)}, bf16[512,256]{1,0:T(8,128)(2,1)}, u32[]{:S(2)}, u32[]{:S(2)}) collective-permute-start(bf16[512,256]{1,0:T(8,128)(2,1)} %get-tuple-element.17), channel_id=1, source_target_pairs={{0,1},{1,0},{2,3},{3,2},{4,5},{5,4},{6,7},{7,6},{8,9},{9,8},{10,11... | collective-permute-start | bytes 786440 | tf_op jit(solution)/shard_map/ppermute | solution.py:135
  74.1 6.7 %copy-start.3 = (f32[512,256]{1,0:T(8,128)S(1)}, f32[512,256]{1,0:T(8,128)}, u32[]{:S(2)}) copy-start(f32[512,256]{1,0:T(8,128)} %copy-done.2) | copy-start | bytes 1572868
  75.0 1.9 %copy-start.1 = (bf16[512,3072]{1,0:T(8,128)(2,1)S(1)}, bf16[512,3072]{1,0:T(8,128)(2,1)}, u32[]{:S(2)}) copy-start(bf16[512,3072]{1,0:T(8,128)(2,1)} %copy-done) | copy-start | bytes 9437188
  80.0 23.7 %copy-start.5 = (f32[512,128]{1,0:T(8,128)S(1)}, f32[512,128]{1,0:T(8,128)}, u32[]{:S(2)}) copy-start(f32[512,128]{1,0:T(8,128)} %param.13) | copy-start | bytes 786436
  80.0 10.7 %collective-permute-start.13 = (bf16[512,256]{1,0:T(8,128)(2,1)S(1)}, bf16[512,256]{1,0:T(8,128)(2,1)S(1)}, u32[]{:S(2)}, u32[]{:S(2)}) collective-permute-start(bf16[512,256]{1,0:T(8,128)(2,1)S(1)} %get-tuple-element.15), channel_id=1, source_target_pairs={{0,1},{1,0},{2,3},{3,2},{4,5},{5,4},{6,7},{7,6},{8,9},{9,8},{10,11... | collective-permute-start | bytes 786440 | tf_op jit(solution)/shard_map/ppermute | solution.py:135
  81.9 16.8 %collective-permute-start.23 = (bf16[512,128]{1,0:T(8,128)(2,1)S(1)}, bf16[512,128]{1,0:T(8,128)(2,1)S(1)}, u32[]{:S(2)}, u32[]{:S(2)}) collective-permute-start(bf16[512,128]{1,0:T(8,128)(2,1)S(1)} %get-tuple-element.24), channel_id=1, source_target_pairs={{24,0},{0,24},{25,1},{1,25},{26,2},{2,26},{27,3},{3,27},{28,4},{4,... | collective-permute-start | bytes 393224 | tf_op jit(solution)/shard_map/ppermute | solution.py:200
  88.1 14.0 %collective-permute-start.22 = (bf16[512,128]{1,0:T(8,128)(2,1)S(1)}, bf16[512,128]{1,0:T(8,128)(2,1)S(1)}, u32[]{:S(2)}, u32[]{:S(2)}) collective-permute-start(bf16[512,128]{1,0:T(8,128)(2,1)S(1)} %get-tuple-element.25), channel_id=1, source_target_pairs={{16,0},{8,24},{17,1},{9,25},{18,2},{10,26},{19,3},{11,27},{20,4},{... | collective-permute-start | bytes 393224 | tf_op jit(solution)/shard_map/ppermute | solution.py:200
  89.4 12.7 %collective-permute-start.21 = (bf16[512,128]{1,0:T(8,128)(2,1)S(1)}, bf16[512,128]{1,0:T(8,128)(2,1)S(1)}, u32[]{:S(2)}, u32[]{:S(2)}) collective-permute-start(bf16[512,128]{1,0:T(8,128)(2,1)S(1)} %get-tuple-element.23), channel_id=1, source_target_pairs={{8,0},{16,24},{9,1},{17,25},{10,2},{18,26},{11,3},{19,27},{12,4},{... | collective-permute-start | bytes 393224 | tf_op jit(solution)/shard_map/ppermute | solution.py:200
  90.8 11.2 %collective-permute-start.16 = (bf16[512,128]{1,0:T(8,128)(2,1)S(1)}, bf16[512,128]{1,0:T(8,128)(2,1)S(1)}, u32[]{:S(2)}, u32[]{:S(2)}) collective-permute-start(bf16[512,128]{1,0:T(8,128)(2,1)S(1)} %get-tuple-element.21), channel_id=1, source_target_pairs={{16,8},{8,16},{17,9},{9,17},{18,10},{10,18},{19,11},{11,19},{20,12... | collective-permute-start | bytes 393224 | tf_op jit(solution)/shard_map/ppermute | solution.py:200
  91.5 10.8 %collective-permute-start.15 = (bf16[512,128]{1,0:T(8,128)(2,1)S(1)}, bf16[512,128]{1,0:T(8,128)(2,1)S(1)}, u32[]{:S(2)}, u32[]{:S(2)}) collective-permute-start(bf16[512,128]{1,0:T(8,128)(2,1)S(1)} %get-tuple-element.22), channel_id=1, source_target_pairs={{24,8},{0,16},{25,9},{1,17},{26,10},{2,18},{27,11},{3,19},{28,12},... | collective-permute-start | bytes 393224 | tf_op jit(solution)/shard_map/ppermute | solution.py:200
  98.8 4.9 %collective-permute-start.14 = (bf16[512,128]{1,0:T(8,128)(2,1)S(1)}, bf16[512,128]{1,0:T(8,128)(2,1)S(1)}, u32[]{:S(2)}, u32[]{:S(2)}) collective-permute-start(bf16[512,128]{1,0:T(8,128)(2,1)S(1)} %get-tuple-element.20), channel_id=1, source_target_pairs={{0,8},{24,16},{1,9},{25,17},{2,10},{26,18},{3,11},{27,19},{4,12},{... | collective-permute-start | bytes 393224 | tf_op jit(solution)/shard_map/ppermute | solution.py:200
where the time goes:
time: 105 us; the launch traced here: 104 us
  starting transfers between devices  37.5 us (36%)
  Pallas kernels  32.5 us (31%)
  waiting for transfers between devices  25.2 us (24%)
  other arithmetic  5.5 us (5%)
  local copies, waits for them, and re-layouts  2.91 us (3%)
    ppermute x12, waiting for transfers between devices, gather(): pieces.append(lax.ppermute(pieces[p], 'row', pairs))  23.6 us
    ppermute x6, starting transfers between devices, on_device(): got = lax.ppermute(sent, 'leaf', [(j ^ d, j) for j in dests])  18 us
    ppermute x12, starting transfers between devices, gather(): pieces.append(lax.ppermute(pieces[p], 'row', pairs))  17.4 us
    pallas_call x4, Pallas kernels, partials(): pl.pallas_call(functools.partial(partial_kernel, n), out_shape=(jax.Shape...  15.5 us
    pallas_call x2, Pallas kernels, select_rows(): pl.pallas_call(functools.partial(select_kernel, n), out_shape=jax.ShapeDt...  9.02 us
    pallas_call x2, Pallas kernels, pick(): pl.pallas_call(functools.partial(pick_kernel, n), out_shape=jax.ShapeDtyp...  8.01 us
    unnamed x14, local copies, waits for them, and re-layouts  2.7 us
    ppermute x6, starting transfers between devices, partner(): return lax.ppermute(x, 'row', [(i, i ^ 1) for i in range(n_row)])  2.11 us
  transfers between devices with their start and end apart: 24, of which 8 were waited for; matrix products, arithmetic and copies ran while one was open for 4% of the time, Pallas kernels for 26%

commit v1 on v0

v1 whole, which is shorter than its diff:
```python
import functools

import jax
import jax.numpy as jnp
import numpy as np
from jax import lax
from jax.experimental import pallas as pl
from jax.experimental.pallas import tpu as pltpu
from jax.sharding import PartitionSpec as P

VMEM = pl.BlockSpec(memory_space=pltpu.VMEM)
SMEM = pl.BlockSpec(memory_space=pltpu.SMEM)
SPLIT = 4
F32 = jnp.float32
BF16 = jnp.bfloat16


def block_copies(first, n, index, src, out, sem):
    width = out.shape[1] // n
    rows = out.shape[0] // SPLIT
    copies = []
    for j in range(n):
        start = pl.multiple_of(index[0, first + j] * width, 128)
        copies.append(
            [
                pltpu.make_async_copy(
                    src.at[pl.ds(r * rows, rows), pl.ds(start, width)],
                    out.at[pl.ds(r * rows, rows), pl.ds(j * width, width)],
                    sem.at[j, r],
                )
                for r in range(SPLIT)
            ]
        )
    return copies


def pick_kernel(first, n, index, src, out, sem):
    copies = block_copies(first, n, index, src, out, sem)
    for group in copies:
        for copy in group:
            copy.start()
    for group in copies:
        for copy in group:
            copy.wait()


def column_block(src, start, width):
    return lax.dynamic_slice_in_dim(src, start * width, width, 1)


def pick(index, first, n, src, width):
    if width % 128:
        blocks = [column_block(src, index[0, first + j], width) for j in range(n)]
        return jnp.concatenate(blocks, axis=1)
    return pl.pallas_call(
        functools.partial(pick_kernel, first, n),
        out_shape=jax.ShapeDtypeStruct((src.shape[0], n * width), src.dtype),
        in_specs=[SMEM, pl.BlockSpec(memory_space=pltpu.HBM)],
        out_specs=VMEM,
        scratch_shapes=[pltpu.SemaphoreType.DMA((n, SPLIT))],
        compiler_params=pltpu.CompilerParams(vmem_limit_bytes=8 << 20),
        name="pick",
    )(index, pltpu.with_memory_space_constraint(src, pltpu.HBM))


def select_kernel(first, n, base, index, places, src, out, buf, sem):
    rows, width = buf.shape[0], buf.shape[1] // n
    copies = block_copies(first, n, index, src, buf, sem)
    for group in copies:
        for copy in group:
            copy.start()
    hot = lax.broadcasted_iota(jnp.int32, (rows, rows), 0) + index[0, base] == places[...]
    hot = jnp.where(hot, 1.0, 0.0).astype(BF16)
    for j, group in enumerate(copies):
        for copy in group:
            copy.wait()
        block = slice(j * width, (j + 1) * width)
        out[:, block] = jnp.dot(hot, buf[:, block], preferred_element_type=F32).astype(BF16)


def select_rows(index, first, n, base, src, places, width):
    rows = src.shape[0]
    if width % 128:
        hot = lax.broadcasted_iota(jnp.int32, (rows, rows), 0) + index[0, base] == places
        return hot.astype(src.dtype) @ pick(index, first, n, src, width)
    return pl.pallas_call(
        functools.partial(select_kernel, first, n, base),
        out_shape=jax.ShapeDtypeStruct((rows, n * width), src.dtype),
        in_specs=[SMEM, VMEM, pl.BlockSpec(memory_space=pltpu.HBM)],
        out_specs=VMEM,
        scratch_shapes=[
            pltpu.VMEM((rows, n * width), src.dtype),
            pltpu.SemaphoreType.DMA((n, SPLIT)),
        ],
        compiler_params=pltpu.CompilerParams(vmem_limit_bytes=12 << 20),
        name="select_rows",
    )(index, places, pltpu.with_memory_space_constraint(src, pltpu.HBM))


def partial_kernel(n, keep, swap, *refs):
    pieces, (own, other, joined) = refs[:n], refs[n:]
    depth = pieces[0].shape[0]
    for j in range(n):
        joined[j * depth : (j + 1) * depth, :] = pieces[j][...]
    other[...] = jnp.dot(swap[...], joined[...], preferred_element_type=F32).astype(BF16)
    own[...] = jnp.dot(keep[...], joined[...], preferred_element_type=F32)


def partials(keep, swap, pieces):
    n = len(pieces)
    rows, depth = keep.shape
    width = pieces[0].shape[1]
    return pl.pallas_call(
        functools.partial(partial_kernel, n),
        out_shape=(
            jax.ShapeDtypeStruct((rows, width), F32),
            jax.ShapeDtypeStruct((rows, width), BF16),
        ),
        in_specs=[VMEM] * (2 + n),
        out_specs=(VMEM, VMEM),
        scratch_shapes=[pltpu.VMEM((depth, width), BF16)],
        compiler_params=pltpu.CompilerParams(vmem_limit_bytes=12 << 20),
        name="partials",
    )(keep, swap, *pieces)


def split_kernel(first, narrow, index, own, other, total, *pieces):
    for d in range(len(pieces) + 1):
        start = pl.multiple_of(index[0, first + d] * narrow, 128)
        piece = own[:, pl.ds(start, narrow)] + other[:, pl.ds(start, narrow)].astype(F32)
        if d == 0:
            total[...] = piece
        else:
            pieces[d - 1][...] = piece.astype(BF16)


def split(index, first, leaves, narrow, own, other):
    rows = own.shape[0]
    if narrow % 128:
        q = own + other.astype(F32)
        blocks = [column_block(q, index[0, first + d], narrow) for d in range(leaves)]
        return blocks[0], *[block.astype(BF16) for block in blocks[1:]]
    return pl.pallas_call(
        functools.partial(split_kernel, first, narrow),
        out_shape=[jax.ShapeDtypeStruct((rows, narrow), F32)]
        + [jax.ShapeDtypeStruct((rows, narrow), BF16)] * (leaves - 1),
        in_specs=[SMEM, VMEM, VMEM],
        out_specs=[VMEM] * leaves,
        compiler_params=pltpu.CompilerParams(vmem_limit_bytes=6 << 20),
        name="split",
    )(index, own, other)


def finish_kernel(which, index, rhs, *refs):
    groups, out = refs[:-1], refs[-1]
    n = len(groups) // 2
    for c in (0, 1):

        @pl.when(index[0, which] == c)
        def _():
            group = groups[c * n : (c + 1) * n]
            out[...] = rhs[...] - sum((g[...].astype(F32) for g in group[1:]), group[0][...])


def finish(index, which, rhs, groups):
    return pl.pallas_call(
        functools.partial(finish_kernel, which),
        out_shape=jax.ShapeDtypeStruct(rhs.shape, F32),
        in_specs=[SMEM] + [VMEM] * (1 + sum(len(g) for g in groups)),
        out_specs=VMEM,
        compiler_params=pltpu.CompilerParams(vmem_limit_bytes=8 << 20),
        name="finish",
    )(index, rhs, *[x for g in groups for x in g])


def on_device(sep_inverse, rhs_block, coupling, ancestor_rows, ancestor_rhs):
    inverse, rhs, couple = sep_inverse[0], rhs_block[0], coupling[0]
    leaves, n_row = lax.axis_size("leaf"), lax.axis_size("row")
    rows = inverse.shape[0]
    anc = couple.shape[0]
    width = rhs.shape[1]
    narrow = width // leaves
    dims = [1 << b for b in range(1, n_row.bit_length() - 1)]
    routes = (dims, dims[::-1])
    masks = ([0], [0])
    for step in range(len(dims)):
        for k in (0, 1):
            masks[k].extend([m ^ routes[k][step] for m in masks[k]])
    n = len(masks[0])
    edge = leaves // 4
    cut = edge * narrow
    is_inner = lambda j: edge <= j < leaves - edge
    dests = [[j for j in range(leaves) if is_inner(j) == bool(c)] for c in (0, 1)]

    table = []
    for leaf in range(leaves):
        for me in range(n_row):
            line = [(me ^ 1) ^ m for m in masks[1 - (me & 1)]]
            line += [me ^ m for m in masks[me & 1]]
            line.append(me * anc)
            for group in dests:
                line += [group.index(leaf ^ d) if leaf ^ d in group else 0 for d in range(leaves)]
            line.append(int(is_inner(leaf)))
            table.append(line)
    table = jnp.array(np.array(table, np.int32))
    device = lax.axis_index(("leaf", "row"))
    index = lax.dynamic_slice(table, (device, jnp.zeros_like(device)), (1, table.shape[1]))
    index, rhs = lax.optimization_barrier((index, rhs))
    base = 2 * n
    first_place = lambda c: base + 1 + c * leaves
    which = base + 1 + 2 * leaves

    def partner(x):
        return lax.ppermute(x, "row", [(i, i ^ 1) for i in range(n_row)])

    def gather(x):
        pieces = [x]
        for step in range(len(dims)):
            pairs = [(i, i ^ routes[i & 1][step]) for i in range(n_row)]
            for p in range(len(pieces)):
                pieces.append(lax.ppermute(pieces[p], "row", pairs))
        return pieces

    chunks = (
        jnp.concatenate([rhs[:, :cut], rhs[:, width - cut :]], axis=1),
        rhs[:, cut : width - cut],
    )
    gathered = [gather(x) for x in chunks]

    def inv_block(first):
        return pick(index, first, n, inverse, rows)

    def cpl_block(first):
        return select_rows(index, first, n, base, couple, ancestor_rows, rows)

    def both(block):
        sent = block(0)
        kept = block(n)
        return kept, partner(sent)

    inv = both(inv_block)
    cpl = both(cpl_block)

    solved = []
    for pieces in gathered:
        own, other = partials(*inv, pieces)
        other = partner(other)
        solved.append((own + other.astype(F32)).astype(BF16))

    shares = []
    for c, y in enumerate(solved):
        pieces = gather(y)
        own, other = partials(*cpl, pieces)
        other = partner(other)
        total, *sent = split(index, first_place(c), leaves, narrow, own, other)
        group = [total]
        for d in range(1, leaves):
            group.append(lax.ppermute(sent[d - 1], "leaf", [(j ^ d, j) for j in dests[c]]))
        shares.append(group)

    y_outer, y_inner = solved
    solution = jnp.concatenate([y_outer[:, :cut], y_inner, y_outer[:, cut:]], axis=1)
    out = finish(index, which, ancestor_rhs, shares)
    return (solution[None], out)


def solution(mesh):
    return jax.shard_map(
        on_device,
        mesh=mesh,
        in_specs=(
            P("leaf", "row", None),
            P("leaf", "row", None),
            P("leaf", "row", None),
            P("leaf", "row"),
            P("row", "leaf"),
        ),
        out_specs=(P("leaf", "row", None), P("row", "leaf")),
        check_vma=False,
    )
```

time: 105 us -> 93.6 us (0.89)
  Pallas kernels: 32.5 us -> 26.8 us
  starting transfers between devices: 37.5 us -> 32.8 us
  waiting for transfers between devices: 25.2 us -> 29.5 us
  other arithmetic: 5.5 us -> 1.26 us
  local copies, waits for them, and re-layouts: 2.91 us -> 0.79 us
    pallas_call x4, Pallas kernels: 15.5 us -> 8.76 us  [partials(): pl.pallas_call(functools.partial(partial_kernel, n), out_shape=(jax.Shape...]
    ppermute x6, starting transfers between devices: 18 us -> 12.5 us  [on_device(): lax.ppermute(sent[d - 1], 'leaf', [(j ^ d, j) for j in dests[c]])]
    ppermute x12, waiting for transfers between devices: 23.6 us -> 26.4 us  [gather(): pieces.append(lax.ppermute(pieces[p], 'row', pairs))]
    unnamed x14 -> x6, local copies, waits for them, and re-layouts: 2.7 us -> 0.01 us
    ppermute x6, waiting for transfers between devices: 1.61 us -> 3.1 us  [on_device(): lax.ppermute(sent[d - 1], 'leaf', [(j ^ d, j) for j in dests[c]])]
    add x2 -> x0, other arithmetic: 1.06 us -> none  [on_device(): q = own + partner(other).astype(F32)]
    pallas_call x4 -> x7, Pallas kernels: 17 us -> 18.1 us  [the longest x2 9.43 us: select_rows(): pl.pallas_call(functools.partial(select_kernel, first, n, base), out_shap...]
  transfers between devices with their start and end apart: 24 -> 24, of which waited for: 8 -> 9; matrix products, arithmetic and copies ran while one was open for 4% -> 1% of each run, Pallas kernels for 26% -> 24%
where the time goes in v1:
time: 93.6 us; the launch traced here: 92.1 us
  starting transfers between devices  32.8 us (35%)
  waiting for transfers between devices  29.5 us (32%)
  Pallas kernels  26.8 us (29%)
  other arithmetic  1.26 us (1%)
    ppermute x12, waiting for transfers between devices, gather(): pieces.append(lax.ppermute(pieces[p], 'row', pairs))  26.4 us
    ppermute x12, starting transfers between devices, gather(): pieces.append(lax.ppermute(pieces[p], 'row', pairs))  18.3 us
    ppermute x6, starting transfers between devices, on_device(): lax.ppermute(sent[d - 1], 'leaf', [(j ^ d, j) for j in dests[c]])  12.5 us
    pallas_call x2, Pallas kernels, select_rows(): pl.pallas_call(functools.partial(select_kernel, first, n, base), out_shap...  9.43 us
    pallas_call x4, Pallas kernels, partials(): pl.pallas_call(functools.partial(partial_kernel, n), out_shape=(jax.Shape...  8.76 us
    pallas_call x2, Pallas kernels, pick(): pl.pallas_call(functools.partial(pick_kernel, first, n), out_shape=jax.Sh...  6.01 us
    ppermute x6, waiting for transfers between devices, on_device(): lax.ppermute(sent[d - 1], 'leaf', [(j ^ d, j) for j in dests[c]])  3.1 us
    ppermute x6, starting transfers between devices, partner(): return lax.ppermute(x, 'row', [(i, i ^ 1) for i in range(n_row)])  2.1 us
  transfers between devices with their start and end apart: 24, of which 9 were waited for; matrix products, arithmetic and copies ran while one was open for 1% of the time, Pallas kernels for 24%

profile of v1, /device:TPU:0, one launch (start us, length us, event | category | flops | bytes accessed | tf_op | source)
XLA Modules:
  0.0 92.1 jit_solution(18362631247621738868)
XLA Ops:
  0.6 0.7 constant_dynamic-slice_fusion.index
  1.3 3.0 %pick.3 = bf16[768,3072]{1,0:T(8,128)(2,1)S(1)} custom-call(s32[1,18]{1,0:T(1,128)S(1)} %constant_dynamic-slice_fusion.index, bf16[768,6144]{1,0:T(8,128)(2,1)} %bitcast.5), custom_call_target="tpu_custom_call" | custom-call | tf_op jit(solution)/shard_map/pick/pallas_call | solution.py:55
  4.3 0.6 collective-permute-start
  4.9 4.7 %select_rows.3 = bf16[512,3072]{1,0:T(8,128)(2,1)S(1)} custom-call(s32[1,18]{1,0:T(1,128)S(1)} %constant_dynamic-slice_fusion.index, s32[1,512]{1,0:T(1,128)S(1)} %copy-done.1, bf16[512,6144]{1,0:T(8,128)(2,1)} %bitcast.7), custom_call_target="tpu_custom_call" | custom-call | tf_op jit(solution)/shard_map/select_rows/pallas_call | solution.py:86
  9.6 0.1 collective-permute-start.9
  9.8 3.0 %collective-permute-start.1 = (bf16[768,256]{1,0:T(8,128)(2,1)S(1)}, bf16[768,256]{1,0:T(8,128)(2,1)S(1)}, u32[]{:S(2)}, u32[]{:S(2)}) collective-permute-start(bf16[768,256]{1,0:T(8,128)(2,1)S(1)} %pad_maximum_fusion.refs_0_), channel_id=1, source_target_pairs={{0,2},{1,5},{2,0},{3,7},{4,6},{5,1},{6,4},{7,3},{8,10},{9,13},{10,... | collective-permute-start | bytes 1179656 | tf_op jit(solution)/shard_map/ppermute | solution.py:221
  12.8 1.5 %collective-permute-start.2 = (bf16[768,256]{1,0:T(8,128)(2,1)S(1)}, bf16[768,256]{1,0:T(8,128)(2,1)S(1)}, u32[]{:S(2)}, u32[]{:S(2)}) collective-permute-start(bf16[768,256]{1,0:T(8,128)(2,1)S(1)} %pad_maximum_fusion.refs_0_), channel_id=1, source_target_pairs={{0,4},{1,3},{2,6},{3,1},{4,0},{5,7},{6,2},{7,5},{8,12},{9,11},{10,... | collective-permute-start | bytes 1179656 | tf_op jit(solution)/shard_map/ppermute | solution.py:221
  14.4 0.6 collective-permute-start.5
  15.0 7.0 %collective-permute-done.1.refs_1_ = bf16[768,256]{1,0:T(8,128)(2,1)S(1)} collective-permute-done((bf16[768,256]{1,0:T(8,128)(2,1)S(1)}, bf16[768,256]{1,0:T(8,128)(2,1)S(1)}, u32[]{:S(2)}, u32[]{:S(2)}) %collective-permute-start.1) | collective-permute-done | bytes 393248 | tf_op jit(solution)/shard_map/ppermute | solution.py:221
  22.0 2.0 %collective-permute-start.3 = (bf16[768,256]{1,0:T(8,128)(2,1)S(1)}, bf16[768,256]{1,0:T(8,128)(2,1)S(1)}, u32[]{:S(2)}, u32[]{:S(2)}) collective-permute-start(bf16[768,256]{1,0:T(8,128)(2,1)S(1)} %collective-permute-done.1.refs_1_), channel_id=1, source_target_pairs={{0,4},{1,3},{2,6},{3,1},{4,0},{5,7},{6,2},{7,5},{8,12},{9,11},{10,... | collective-permute-start | bytes 1179656 | tf_op jit(solution)/shard_map/ppermute | solution.py:221
  24.0 0.8 collective-permute-done.2.refs_2_
  24.8 1.5 %collective-permute-start.6 = (bf16[768,256]{1,0:T(8,128)(2,1)S(1)}, bf16[768,256]{1,0:T(8,128)(2,1)S(1)}, u32[]{:S(2)}, u32[]{:S(2)}) collective-permute-start(bf16[768,256]{1,0:T(8,128)(2,1)S(1)} %slice.18.refs_0_), channel_id=1, source_target_pairs={{0,4},{1,3},{2,6},{3,1},{4,0},{5,7},{6,2},{7,5},{8,12},{9,11},{10,... | collective-permute-start | bytes 1179656 | tf_op jit(solution)/shard_map/ppermute | solution.py:221
  26.3 3.9 %collective-permute-done.5.refs_1_ = bf16[768,256]{1,0:T(8,128)(2,1)S(1)} collective-permute-done((bf16[768,256]{1,0:T(8,128)(2,1)S(1)}, bf16[768,256]{1,0:T(8,128)(2,1)S(1)}, u32[]{:S(2)}, u32[]{:S(2)}) %collective-permute-start.5) | collective-permute-done | bytes 393248 | tf_op jit(solution)/shard_map/ppermute | solution.py:221
  30.2 1.3 %collective-permute-start.7 = (bf16[768,256]{1,0:T(8,128)(2,1)S(1)}, bf16[768,256]{1,0:T(8,128)(2,1)S(1)}, u32[]{:S(2)}, u32[]{:S(2)}) collective-permute-start(bf16[768,256]{1,0:T(8,128)(2,1)S(1)} %collective-permute-done.5.refs_1_), channel_id=1, source_target_pairs={{0,4},{1,3},{2,6},{3,1},{4,0},{5,7},{6,2},{7,5},{8,12},{9,11},{10,... | collective-permute-start | bytes 1179656 | tf_op jit(solution)/shard_map/ppermute | solution.py:221
  31.5 3.0 %pick.2.keep = bf16[768,3072]{1,0:T(8,128)(2,1)S(1)} custom-call(s32[1,18]{1,0:T(1,128)S(1)} %constant_dynamic-slice_fusion.index, bf16[768,6144]{1,0:T(8,128)(2,1)} %bitcast.6), custom_call_target="tpu_custom_call" | custom-call | tf_op jit(solution)/shard_map/pick/pallas_call | solution.py:55
  34.5 0.0 collective-permute-done.3.refs_3_
  34.5 0.0 collective-permute-done.swap
  34.5 2.6 %partials.4 = (f32[768,256]{1,0:T(8,128)S(1)}, bf16[768,256]{1,0:T(8,128)(2,1)S(1)}) custom-call(bf16[768,3072]{1,0:T(8,128)(2,1)S(1)} %pick.2.keep, bf16[768,3072]{1,0:T(8,128)(2,1)S(1)} %collective-permute-done.swap, bf16[768,256]{1,0:T(8,128)(2,1)S(1)} %pad_maximum_fusion.refs_0_, bf16[768,256]{1,0:T(8,128)(2,1)S(1)} %collective-permute-done.1.refs_1_, ...), custom_call_target="tpu_custom_call" | custom-call | tf_op jit(solution)/shard_map/partials/pallas_call | solution.py:113
  37.2 0.1 collective-permute-start.4
  37.2 0.0 collective-permute-done.6.refs_2_
  37.2 1.8 %collective-permute-done.7.refs_3_ = bf16[768,256]{1,0:T(8,128)(2,1)S(1)} collective-permute-done((bf16[768,256]{1,0:T(8,128)(2,1)S(1)}, bf16[768,256]{1,0:T(8,128)(2,1)S(1)}, u32[]{:S(2)}, u32[]{:S(2)}) %collective-permute-start.7) | collective-permute-done | bytes 393248 | tf_op jit(solution)/shard_map/ppermute | solution.py:221
  39.0 2.6 %partials.5 = (f32[768,256]{1,0:T(8,128)S(1)}, bf16[768,256]{1,0:T(8,128)(2,1)S(1)}) custom-call(bf16[768,3072]{1,0:T(8,128)(2,1)S(1)} %pick.2.keep, bf16[768,3072]{1,0:T(8,128)(2,1)S(1)} %collective-permute-done.swap, bf16[768,256]{1,0:T(8,128)(2,1)S(1)} %slice.18.refs_0_, bf16[768,256]{1,0:T(8,128)(2,1)S(1)} %collective-permute-done.5.refs_1_, ...), custom_call_target="tpu_custom_call" | custom-call | tf_op jit(solution)/shard_map/partials/pallas_call | solution.py:113
  41.6 0.5 collective-permute-start.8
  42.1 0.0 collective-permute-done.4
  42.1 0.1 add_convert_fusion.1.refs_0_
  42.3 2.1 %collective-permute-start.10 = (bf16[768,256]{1,0:T(8,128)(2,1)S(1)}, bf16[768,256]{1,0:T(8,128)(2,1)S(1)}, u32[]{:S(2)}, u32[]{:S(2)}) collective-permute-start(bf16[768,256]{1,0:T(8,128)(2,1)S(1)} %add_convert_fusion.1.refs_0_), channel_id=1, source_target_pairs={{0,2},{1,5},{2,0},{3,7},{4,6},{5,1},{6,4},{7,3},{8,10},{9,13},{10,... | collective-permute-start | bytes 1179656 | tf_op jit(solution)/shard_map/ppermute | solution.py:221
  44.4 0.0 collective-permute-done.8
  44.4 0.1 add_convert_fusion.refs_0_
  44.5 1.2 %collective-permute-start.17 = (bf16[768,256]{1,0:T(8,128)(2,1)S(1)}, bf16[768,256]{1,0:T(8,128)(2,1)S(1)}, u32[]{:S(2)}, u32[]{:S(2)}) collective-permute-start(bf16[768,256]{1,0:T(8,128)(2,1)S(1)} %add_convert_fusion.refs_0_), channel_id=1, source_target_pairs={{0,2},{1,5},{2,0},{3,7},{4,6},{5,1},{6,4},{7,3},{8,10},{9,13},{10,... | collective-permute-start | bytes 1179656 | tf_op jit(solution)/shard_map/ppermute | solution.py:221
  45.7 1.1 %collective-permute-start.11 = (bf16[768,256]{1,0:T(8,128)(2,1)S(1)}, bf16[768,256]{1,0:T(8,128)(2,1)S(1)}, u32[]{:S(2)}, u32[]{:S(2)}) collective-permute-start(bf16[768,256]{1,0:T(8,128)(2,1)S(1)} %add_convert_fusion.1.refs_0_), channel_id=1, source_target_pairs={{0,4},{1,3},{2,6},{3,1},{4,0},{5,7},{6,2},{7,5},{8,12},{9,11},{10,... | collective-permute-start | bytes 1179656 | tf_op jit(solution)/shard_map/ppermute | solution.py:221
  46.8 5.6 %collective-permute-done.10.refs_1_ = bf16[768,256]{1,0:T(8,128)(2,1)S(1)} collective-permute-done((bf16[768,256]{1,0:T(8,128)(2,1)S(1)}, bf16[768,256]{1,0:T(8,128)(2,1)S(1)}, u32[]{:S(2)}, u32[]{:S(2)}) %collective-permute-start.10) | collective-permute-done | bytes 393248 | tf_op jit(solution)/shard_map/ppermute | solution.py:221
  52.5 1.9 %collective-permute-start.12 = (bf16[768,256]{1,0:T(8,128)(2,1)S(1)}, bf16[768,256]{1,0:T(8,128)(2,1)S(1)}, u32[]{:S(2)}, u32[]{:S(2)}) collective-permute-start(bf16[768,256]{1,0:T(8,128)(2,1)S(1)} %collective-permute-done.10.refs_1_), channel_id=1, source_target_pairs={{0,4},{1,3},{2,6},{3,1},{4,0},{5,7},{6,2},{7,5},{8,12},{9,11},{10,... | collective-permute-start | bytes 1179656 | tf_op jit(solution)/shard_map/ppermute | solution.py:221
  54.4 0.1 collective-permute-start.18
  54.5 6.4 %collective-permute-done.17.refs_1_ = bf16[768,256]{1,0:T(8,128)(2,1)S(1)} collective-permute-done((bf16[768,256]{1,0:T(8,128)(2,1)S(1)}, bf16[768,256]{1,0:T(8,128)(2,1)S(1)}, u32[]{:S(2)}, u32[]{:S(2)}) %collective-permute-start.17) | collective-permute-done | bytes 393248 | tf_op jit(solution)/shard_map/ppermute | solution.py:221
  60.9 1.9 %collective-permute-start.19 = (bf16[768,256]{1,0:T(8,128)(2,1)S(1)}, bf16[768,256]{1,0:T(8,128)(2,1)S(1)}, u32[]{:S(2)}, u32[]{:S(2)}) collective-permute-start(bf16[768,256]{1,0:T(8,128)(2,1)S(1)} %collective-permute-done.17.refs_1_), channel_id=1, source_target_pairs={{0,4},{1,3},{2,6},{3,1},{4,0},{5,7},{6,2},{7,5},{8,12},{9,11},{10,... | collective-permute-start | bytes 1179656 | tf_op jit(solution)/shard_map/ppermute | solution.py:221
  62.8 4.7 %select_rows.2.keep = bf16[512,3072]{1,0:T(8,128)(2,1)S(1)} custom-call(s32[1,18]{1,0:T(1,128)S(1)} %constant_dynamic-slice_fusion.index, s32[1,512]{1,0:T(1,128)S(1)} %copy-done.1, bf16[512,6144]{1,0:T(8,128)(2,1)} %bitcast.8), custom_call_target="tpu_custom_call" | custom-call | tf_op jit(solution)/shard_map/select_rows/pallas_call | solution.py:86
  67.5 0.0 collective-permute-done.9.swap
  67.5 0.0 collective-permute-done.11.refs_2_
  67.5 0.0 collective-permute-done.12.refs_3_
  67.5 1.8 %partials.6 = (f32[512,256]{1,0:T(8,128)S(1)}, bf16[512,256]{1,0:T(8,128)(2,1)S(1)}) custom-call(bf16[512,3072]{1,0:T(8,128)(2,1)S(1)} %select_rows.2.keep, bf16[512,3072]{1,0:T(8,128)(2,1)S(1)} %collective-permute-done.9.swap, bf16[768,256]{1,0:T(8,128)(2,1)S(1)} %add_convert_fusion.1.refs_0_, bf16[768,256]{1,0:T(8,128)(2,1)S(1)} %collective-permute-done.10.refs_1_, ...), custom_call_target="tpu_custom_call" | custom-call | tf_op jit(solution)/shard_map/partials/pallas_call | solution.py:113
  69.3 0.1 collective-permute-start.13
  69.4 0.0 collective-permute-done.18.refs_2_
  69.4 0.8 collective-permute-done.19.refs_3_
  70.3 1.8 %partials.7 = (f32[512,256]{1,0:T(8,128)S(1)}, bf16[512,256]{1,0:T(8,128)(2,1)S(1)}) custom-call(bf16[512,3072]{1,0:T(8,128)(2,1)S(1)} %select_rows.2.keep, bf16[512,3072]{1,0:T(8,128)(2,1)S(1)} %collective-permute-done.9.swap, bf16[768,256]{1,0:T(8,128)(2,1)S(1)} %add_convert_fusion.refs_0_, bf16[768,256]{1,0:T(8,128)(2,1)S(1)} %collective-permute-done.17.refs_1_, ...), custom_call_target="tpu_custom_call" | custom-call | tf_op jit(solution)/shard_map/partials/pallas_call | solution.py:113
  72.1 0.0 copy-start
  72.1 0.8 collective-permute-start.20
  72.9 0.0 collective-permute-done.13.other
  72.9 0.6 split.2
  73.5 1.3 %collective-permute-start.14 = (bf16[512,128]{1,0:T(8,128)(2,1)S(1)}, bf16[512,128]{1,0:T(8,128)(2,1)S(1)}, u32[]{:S(2)}, u32[]{:S(2)}) collective-permute-start(bf16[512,128]{1,0:T(8,128)(2,1)S(1)} %get-tuple-element.29), channel_id=1, source_target_pairs={{8,0},{16,24},{9,1},{17,25},{10,2},{18,26},{11,3},{19,27},{12,4},{... | collective-permute-start | bytes 393224 | tf_op jit(solution)/shard_map/ppermute | solution.py:258
  74.9 1.3 %collective-permute-start.15 = (bf16[512,128]{1,0:T(8,128)(2,1)S(1)}, bf16[512,128]{1,0:T(8,128)(2,1)S(1)}, u32[]{:S(2)}, u32[]{:S(2)}) collective-permute-start(bf16[512,128]{1,0:T(8,128)(2,1)S(1)} %get-tuple-element.30), channel_id=1, source_target_pairs={{16,0},{8,24},{17,1},{9,25},{18,2},{10,26},{19,3},{11,27},{20,4},{... | collective-permute-start | bytes 393224 | tf_op jit(solution)/shard_map/ppermute | solution.py:258
  76.2 6.0 %collective-permute-start.16 = (bf16[512,128]{1,0:T(8,128)(2,1)S(1)}, bf16[512,128]{1,0:T(8,128)(2,1)S(1)}, u32[]{:S(2)}, u32[]{:S(2)}) collective-permute-start(bf16[512,128]{1,0:T(8,128)(2,1)S(1)} %get-tuple-element.31), channel_id=1, source_target_pairs={{24,0},{0,24},{25,1},{1,25},{26,2},{2,26},{27,3},{3,27},{28,4},{4,... | collective-permute-start | bytes 393224 | tf_op jit(solution)/shard_map/ppermute | solution.py:258
  82.2 0.0 collective-permute-done.20.other
  82.2 0.7 split.3
  82.9 1.9 %collective-permute-start.21 = (bf16[512,128]{1,0:T(8,128)(2,1)S(1)}, bf16[512,128]{1,0:T(8,128)(2,1)S(1)}, u32[]{:S(2)}, u32[]{:S(2)}) collective-permute-start(bf16[512,128]{1,0:T(8,128)(2,1)S(1)} %get-tuple-element.35), channel_id=1, source_target_pairs={{0,8},{24,16},{1,9},{25,17},{2,10},{26,18},{3,11},{27,19},{4,12},{... | collective-permute-start | bytes 393224 | tf_op jit(solution)/shard_map/ppermute | solution.py:258
  84.7 1.3 %collective-permute-start.22 = (bf16[512,128]{1,0:T(8,128)(2,1)S(1)}, bf16[512,128]{1,0:T(8,128)(2,1)S(1)}, u32[]{:S(2)}, u32[]{:S(2)}) collective-permute-start(bf16[512,128]{1,0:T(8,128)(2,1)S(1)} %get-tuple-element.36), channel_id=1, source_target_pairs={{24,8},{0,16},{25,9},{1,17},{26,10},{2,18},{27,11},{3,19},{28,12},... | collective-permute-start | bytes 393224 | tf_op jit(solution)/shard_map/ppermute | solution.py:258
  86.1 0.0 collective-permute-done.14.refs_1_
  86.1 0.7 collective-permute-start.23
  86.7 1.0 %maximum_bitcast_fusion = bf16[1,768,512]{2,1,0:T(8,128)(2,1)} fusion(bf16[768,128]{1,0:T(8,128)(2,1)S(1)} %get-tuple-element.41, bf16[768,256]{1,0:T(8,128)(2,1)S(1)} %add_convert_fusion.refs_0_, bf16[768,128]{1,0:T(8,128)(2,1)S(1)} %get-tuple-element.40), kind=kLoop, calls=%fused_computation | loop fusion | flops 2359296 | bytes 1572864 | tf_op jit(solution)/shard_map/broadcast_in_dim | solution.py:264
  87.7 0.0 collective-permute-done.15.refs_2_
  87.7 0.0 collective-permute-done.16.refs_3_
  87.7 0.9 collective-permute-done.21.refs_5_
  88.6 2.2 %collective-permute-done.22.refs_6_ = bf16[512,128]{1,0:T(8,128)(2,1)S(1)} collective-permute-done((bf16[512,128]{1,0:T(8,128)(2,1)S(1)}, bf16[512,128]{1,0:T(8,128)(2,1)S(1)}, u32[]{:S(2)}, u32[]{:S(2)}) %collective-permute-start.22) | collective-permute-done | bytes 131104 | tf_op jit(solution)/shard_map/ppermute | solution.py:258
  90.8 0.0 collective-permute-done.23.refs_7_
  90.8 1.3 %finish.1 = f32[512,128]{1,0:T(8,128)} custom-call(s32[1,18]{1,0:T(1,128)S(1)} %constant_dynamic-slice_fusion.index, f32[512,128]{1,0:T(8,128)S(1)} %copy-done, f32[512,128]{1,0:T(8,128)S(1)} %get-tuple-element.28.refs_0_, bf16[512,128]{1,0:T(8,128)(2,1)S(1)} %collective-permute-done.14.refs_1_, bf16[512,128]{1,0:T(8,128)(2,1)S(1)} %collective-permute-done.15.refs_2_, ...), custom_call_target="tpu_custom_call" | custom-call | tf_op jit(solution)/shard_map/finish/pallas_call | solution.py:166
  (9 shorter events, 0.1 us)
Async XLA Ops:
  1.3 3.6 %copy-start.1 = (s32[1,512]{1,0:T(1,128)S(1)}, s32[1,512]{1,0:T(1,128)}, u32[]{:S(2)}) copy-start(s32[1,512]{1,0:T(1,128)} %places.3) | copy-start | bytes 6148
  4.3 30.2 %collective-permute-start = (bf16[768,3072]{1,0:T(8,128)(2,1)S(1)}, bf16[768,3072]{1,0:T(8,128)(2,1)S(1)}, u32[]{:S(2)}, u32[]{:S(2)}) collective-permute-start(bf16[768,3072]{1,0:T(8,128)(2,1)S(1)} %pick.3), channel_id=1, source_target_pairs={{0,1},{1,0},{2,3},{3,2},{4,5},{5,4},{6,7},{7,6},{8,9},{9,8},{10,11... | collective-permute-start | bytes 14155784 | tf_op jit(solution)/shard_map/ppermute | solution.py:214
  4.9 4.8 %copy-start.2 = (bf16[1,768,512]{2,1,0:T(8,128)(2,1)S(1)}, bf16[1,768,512]{2,1,0:T(8,128)(2,1)}, u32[]{:S(2)}) copy-start(bf16[1,768,512]{2,1,0:T(8,128)(2,1)} %param.7) | copy-start | bytes 2359300
  9.6 57.9 %collective-permute-start.9 = (bf16[512,3072]{1,0:T(8,128)(2,1)S(1)}, bf16[512,3072]{1,0:T(8,128)(2,1)S(1)}, u32[]{:S(2)}, u32[]{:S(2)}) collective-permute-start(bf16[512,3072]{1,0:T(8,128)(2,1)S(1)} %select_rows.3), channel_id=1, source_target_pairs={{0,1},{1,0},{2,3},{3,2},{4,5},{5,4},{6,7},{7,6},{8,9},{9,8},{10,11... | collective-permute-start | bytes 9437192 | tf_op jit(solution)/shard_map/ppermute | solution.py:214
  9.8 12.2 %collective-permute-start.1 = (bf16[768,256]{1,0:T(8,128)(2,1)S(1)}, bf16[768,256]{1,0:T(8,128)(2,1)S(1)}, u32[]{:S(2)}, u32[]{:S(2)}) collective-permute-start(bf16[768,256]{1,0:T(8,128)(2,1)S(1)} %pad_maximum_fusion.refs_0_), channel_id=1, source_target_pairs={{0,2},{1,5},{2,0},{3,7},{4,6},{5,1},{6,4},{7,3},{8,10},{9,13},{10,... | collective-permute-start | bytes 1179656 | tf_op jit(solution)/shard_map/ppermute | solution.py:221
  12.8 12.0 %collective-permute-start.2 = (bf16[768,256]{1,0:T(8,128)(2,1)S(1)}, bf16[768,256]{1,0:T(8,128)(2,1)S(1)}, u32[]{:S(2)}, u32[]{:S(2)}) collective-permute-start(bf16[768,256]{1,0:T(8,128)(2,1)S(1)} %pad_maximum_fusion.refs_0_), channel_id=1, source_target_pairs={{0,4},{1,3},{2,6},{3,1},{4,0},{5,7},{6,2},{7,5},{8,12},{9,11},{10,... | collective-permute-start | bytes 1179656 | tf_op jit(solution)/shard_map/ppermute | solution.py:221
  14.4 15.8 %collective-permute-start.5 = (bf16[768,256]{1,0:T(8,128)(2,1)S(1)}, bf16[768,256]{1,0:T(8,128)(2,1)S(1)}, u32[]{:S(2)}, u32[]{:S(2)}) collective-permute-start(bf16[768,256]{1,0:T(8,128)(2,1)S(1)} %slice.18.refs_0_), channel_id=1, source_target_pairs={{0,2},{1,5},{2,0},{3,7},{4,6},{5,1},{6,4},{7,3},{8,10},{9,13},{10,... | collective-permute-start | bytes 1179656 | tf_op jit(solution)/shard_map/ppermute | solution.py:221
  22.0 12.5 %collective-permute-start.3 = (bf16[768,256]{1,0:T(8,128)(2,1)S(1)}, bf16[768,256]{1,0:T(8,128)(2,1)S(1)}, u32[]{:S(2)}, u32[]{:S(2)}) collective-permute-start(bf16[768,256]{1,0:T(8,128)(2,1)S(1)} %collective-permute-done.1.refs_1_), channel_id=1, source_target_pairs={{0,4},{1,3},{2,6},{3,1},{4,0},{5,7},{6,2},{7,5},{8,12},{9,11},{10,... | collective-permute-start | bytes 1179656 | tf_op jit(solution)/shard_map/ppermute | solution.py:221
  24.8 12.4 %collective-permute-start.6 = (bf16[768,256]{1,0:T(8,128)(2,1)S(1)}, bf16[768,256]{1,0:T(8,128)(2,1)S(1)}, u32[]{:S(2)}, u32[]{:S(2)}) collective-permute-start(bf16[768,256]{1,0:T(8,128)(2,1)S(1)} %slice.18.refs_0_), channel_id=1, source_target_pairs={{0,4},{1,3},{2,6},{3,1},{4,0},{5,7},{6,2},{7,5},{8,12},{9,11},{10,... | collective-permute-start | bytes 1179656 | tf_op jit(solution)/shard_map/ppermute | solution.py:221
  30.2 8.8 %collective-permute-start.7 = (bf16[768,256]{1,0:T(8,128)(2,1)S(1)}, bf16[768,256]{1,0:T(8,128)(2,1)S(1)}, u32[]{:S(2)}, u32[]{:S(2)}) collective-permute-start(bf16[768,256]{1,0:T(8,128)(2,1)S(1)} %collective-permute-done.5.refs_1_), channel_id=1, source_target_pairs={{0,4},{1,3},{2,6},{3,1},{4,0},{5,7},{6,2},{7,5},{8,12},{9,11},{10,... | collective-permute-start | bytes 1179656 | tf_op jit(solution)/shard_map/ppermute | solution.py:221
  37.2 5.0 %collective-permute-start.4 = (bf16[768,256]{1,0:T(8,128)(2,1)S(1)}, bf16[768,256]{1,0:T(8,128)(2,1)S(1)}, u32[]{:S(2)}, u32[]{:S(2)}) collective-permute-start(bf16[768,256]{1,0:T(8,128)(2,1)S(1)} %get-tuple-element.23), channel_id=1, source_target_pairs={{0,1},{1,0},{2,3},{3,2},{4,5},{5,4},{6,7},{7,6},{8,9},{9,8},{10,11... | collective-permute-start | bytes 1179656 | tf_op jit(solution)/shard_map/ppermute | solution.py:214
  41.6 2.7 %collective-permute-start.8 = (bf16[768,256]{1,0:T(8,128)(2,1)S(1)}, bf16[768,256]{1,0:T(8,128)(2,1)S(1)}, u32[]{:S(2)}, u32[]{:S(2)}) collective-permute-start(bf16[768,256]{1,0:T(8,128)(2,1)S(1)} %get-tuple-element.25), channel_id=1, source_target_pairs={{0,1},{1,0},{2,3},{3,2},{4,5},{5,4},{6,7},{7,6},{8,9},{9,8},{10,11... | collective-permute-start | bytes 1179656 | tf_op jit(solution)/shard_map/ppermute | solution.py:214
  42.3 10.2 %collective-permute-start.10 = (bf16[768,256]{1,0:T(8,128)(2,1)S(1)}, bf16[768,256]{1,0:T(8,128)(2,1)S(1)}, u32[]{:S(2)}, u32[]{:S(2)}) collective-permute-start(bf16[768,256]{1,0:T(8,128)(2,1)S(1)} %add_convert_fusion.1.refs_0_), channel_id=1, source_target_pairs={{0,2},{1,5},{2,0},{3,7},{4,6},{5,1},{6,4},{7,3},{8,10},{9,13},{10,... | collective-permute-start | bytes 1179656 | tf_op jit(solution)/shard_map/ppermute | solution.py:221
  44.5 16.4 %collective-permute-start.17 = (bf16[768,256]{1,0:T(8,128)(2,1)S(1)}, bf16[768,256]{1,0:T(8,128)(2,1)S(1)}, u32[]{:S(2)}, u32[]{:S(2)}) collective-permute-start(bf16[768,256]{1,0:T(8,128)(2,1)S(1)} %add_convert_fusion.refs_0_), channel_id=1, source_target_pairs={{0,2},{1,5},{2,0},{3,7},{4,6},{5,1},{6,4},{7,3},{8,10},{9,13},{10,... | collective-permute-start | bytes 1179656 | tf_op jit(solution)/shard_map/ppermute | solution.py:221
  45.7 21.8 %collective-permute-start.11 = (bf16[768,256]{1,0:T(8,128)(2,1)S(1)}, bf16[768,256]{1,0:T(8,128)(2,1)S(1)}, u32[]{:S(2)}, u32[]{:S(2)}) collective-permute-start(bf16[768,256]{1,0:T(8,128)(2,1)S(1)} %add_convert_fusion.1.refs_0_), channel_id=1, source_target_pairs={{0,4},{1,3},{2,6},{3,1},{4,0},{5,7},{6,2},{7,5},{8,12},{9,11},{10,... | collective-permute-start | bytes 1179656 | tf_op jit(solution)/shard_map/ppermute | solution.py:221
  52.5 15.1 %collective-permute-start.12 = (bf16[768,256]{1,0:T(8,128)(2,1)S(1)}, bf16[768,256]{1,0:T(8,128)(2,1)S(1)}, u32[]{:S(2)}, u32[]{:S(2)}) collective-permute-start(bf16[768,256]{1,0:T(8,128)(2,1)S(1)} %collective-permute-done.10.refs_1_), channel_id=1, source_target_pairs={{0,4},{1,3},{2,6},{3,1},{4,0},{5,7},{6,2},{7,5},{8,12},{9,11},{10,... | collective-permute-start | bytes 1179656 | tf_op jit(solution)/shard_map/ppermute | solution.py:221
  54.4 15.1 %collective-permute-start.18 = (bf16[768,256]{1,0:T(8,128)(2,1)S(1)}, bf16[768,256]{1,0:T(8,128)(2,1)S(1)}, u32[]{:S(2)}, u32[]{:S(2)}) collective-permute-start(bf16[768,256]{1,0:T(8,128)(2,1)S(1)} %add_convert_fusion.refs_0_), channel_id=1, source_target_pairs={{0,4},{1,3},{2,6},{3,1},{4,0},{5,7},{6,2},{7,5},{8,12},{9,11},{10,... | collective-permute-start | bytes 1179656 | tf_op jit(solution)/shard_map/ppermute | solution.py:221
  60.9 9.4 %collective-permute-start.19 = (bf16[768,256]{1,0:T(8,128)(2,1)S(1)}, bf16[768,256]{1,0:T(8,128)(2,1)S(1)}, u32[]{:S(2)}, u32[]{:S(2)}) collective-permute-start(bf16[768,256]{1,0:T(8,128)(2,1)S(1)} %collective-permute-done.17.refs_1_), channel_id=1, source_target_pairs={{0,4},{1,3},{2,6},{3,1},{4,0},{5,7},{6,2},{7,5},{8,12},{9,11},{10,... | collective-permute-start | bytes 1179656 | tf_op jit(solution)/shard_map/ppermute | solution.py:221
  69.3 3.5 %collective-permute-start.13 = (bf16[512,256]{1,0:T(8,128)(2,1)S(1)}, bf16[512,256]{1,0:T(8,128)(2,1)S(1)}, u32[]{:S(2)}, u32[]{:S(2)}) collective-permute-start(bf16[512,256]{1,0:T(8,128)(2,1)S(1)} %get-tuple-element.27), channel_id=1, source_target_pairs={{0,1},{1,0},{2,3},{3,2},{4,5},{5,4},{6,7},{7,6},{8,9},{9,8},{10,11... | collective-permute-start | bytes 786440 | tf_op jit(solution)/shard_map/ppermute | solution.py:214
  72.1 18.7 %copy-start = (f32[512,128]{1,0:T(8,128)S(1)}, f32[512,128]{1,0:T(8,128)}, u32[]{:S(2)}) copy-start(f32[512,128]{1,0:T(8,128)} %rhs.1) | copy-start | bytes 786436
  72.1 10.1 %collective-permute-start.20 = (bf16[512,256]{1,0:T(8,128)(2,1)S(1)}, bf16[512,256]{1,0:T(8,128)(2,1)S(1)}, u32[]{:S(2)}, u32[]{:S(2)}) collective-permute-start(bf16[512,256]{1,0:T(8,128)(2,1)S(1)} %get-tuple-element.33), channel_id=1, source_target_pairs={{0,1},{1,0},{2,3},{3,2},{4,5},{5,4},{6,7},{7,6},{8,9},{9,8},{10,11... | collective-permute-start | bytes 786440 | tf_op jit(solution)/shard_map/ppermute | solution.py:214
  73.5 12.5 %collective-permute-start.14 = (bf16[512,128]{1,0:T(8,128)(2,1)S(1)}, bf16[512,128]{1,0:T(8,128)(2,1)S(1)}, u32[]{:S(2)}, u32[]{:S(2)}) collective-permute-start(bf16[512,128]{1,0:T(8,128)(2,1)S(1)} %get-tuple-element.29), channel_id=1, source_target_pairs={{8,0},{16,24},{9,1},{17,25},{10,2},{18,26},{11,3},{19,27},{12,4},{... | collective-permute-start | bytes 393224 | tf_op jit(solution)/shard_map/ppermute | solution.py:258
  74.9 12.8 %collective-permute-start.15 = (bf16[512,128]{1,0:T(8,128)(2,1)S(1)}, bf16[512,128]{1,0:T(8,128)(2,1)S(1)}, u32[]{:S(2)}, u32[]{:S(2)}) collective-permute-start(bf16[512,128]{1,0:T(8,128)(2,1)S(1)} %get-tuple-element.30), channel_id=1, source_target_pairs={{16,0},{8,24},{17,1},{9,25},{18,2},{10,26},{19,3},{11,27},{20,4},{... | collective-permute-start | bytes 393224 | tf_op jit(solution)/shard_map/ppermute | solution.py:258
  76.2 11.6 %collective-permute-start.16 = (bf16[512,128]{1,0:T(8,128)(2,1)S(1)}, bf16[512,128]{1,0:T(8,128)(2,1)S(1)}, u32[]{:S(2)}, u32[]{:S(2)}) collective-permute-start(bf16[512,128]{1,0:T(8,128)(2,1)S(1)} %get-tuple-element.31), channel_id=1, source_target_pairs={{24,0},{0,24},{25,1},{1,25},{26,2},{2,26},{27,3},{3,27},{28,4},{4,... | collective-permute-start | bytes 393224 | tf_op jit(solution)/shard_map/ppermute | solution.py:258
  82.9 5.7 %collective-permute-start.21 = (bf16[512,128]{1,0:T(8,128)(2,1)S(1)}, bf16[512,128]{1,0:T(8,128)(2,1)S(1)}, u32[]{:S(2)}, u32[]{:S(2)}) collective-permute-start(bf16[512,128]{1,0:T(8,128)(2,1)S(1)} %get-tuple-element.35), channel_id=1, source_target_pairs={{0,8},{24,16},{1,9},{25,17},{2,10},{26,18},{3,11},{27,19},{4,12},{... | collective-permute-start | bytes 393224 | tf_op jit(solution)/shard_map/ppermute | solution.py:258
  84.7 6.1 %collective-permute-start.22 = (bf16[512,128]{1,0:T(8,128)(2,1)S(1)}, bf16[512,128]{1,0:T(8,128)(2,1)S(1)}, u32[]{:S(2)}, u32[]{:S(2)}) collective-permute-start(bf16[512,128]{1,0:T(8,128)(2,1)S(1)} %get-tuple-element.36), channel_id=1, source_target_pairs={{24,8},{0,16},{25,9},{1,17},{26,10},{2,18},{27,11},{3,19},{28,12},... | collective-permute-start | bytes 393224 | tf_op jit(solution)/shard_map/ppermute | solution.py:258
  86.1 4.7 %collective-permute-start.23 = (bf16[512,128]{1,0:T(8,128)(2,1)S(1)}, bf16[512,128]{1,0:T(8,128)(2,1)S(1)}, u32[]{:S(2)}, u32[]{:S(2)}) collective-permute-start(bf16[512,128]{1,0:T(8,128)(2,1)S(1)} %get-tuple-element.37), channel_id=1, source_target_pairs={{16,8},{8,16},{17,9},{9,17},{18,10},{10,18},{19,11},{11,19},{20,12... | collective-permute-start | bytes 393224 | tf_op jit(solution)/shard_map/ppermute | solution.py:258

commit v2 on v1

--- a/solution.py
+++ b/solution.py
@@ -48,19 +48,21 @@
     return lax.dynamic_slice_in_dim(src, start * width, width, 1)
 
 
-def pick(index, first, n, src, width):
+def pick(index, first, n, src, width, space=None):
     if width % 128:
         blocks = [column_block(src, index[0, first + j], width) for j in range(n)]
         return jnp.concatenate(blocks, axis=1)
+    if space is not None:
+        src = pltpu.with_memory_space_constraint(src, space)
     return pl.pallas_call(
         functools.partial(pick_kernel, first, n),
         out_shape=jax.ShapeDtypeStruct((src.shape[0], n * width), src.dtype),
-        in_specs=[SMEM, pl.BlockSpec(memory_space=pltpu.HBM)],
+        in_specs=[SMEM, pl.BlockSpec(memory_space=pl.ANY)],
         out_specs=VMEM,
         scratch_shapes=[pltpu.SemaphoreType.DMA((n, SPLIT))],
         compiler_params=pltpu.CompilerParams(vmem_limit_bytes=8 << 20),
         name="pick",
-    )(index, pltpu.with_memory_space_constraint(src, pltpu.HBM))
+    )(index, src)
 
 
 def select_kernel(first, n, base, index, places, src, out, buf, sem):
@@ -86,7 +88,7 @@
     return pl.pallas_call(
         functools.partial(select_kernel, first, n, base),
         out_shape=jax.ShapeDtypeStruct((rows, n * width), src.dtype),
-        in_specs=[SMEM, VMEM, pl.BlockSpec(memory_space=pltpu.HBM)],
+        in_specs=[SMEM, VMEM, pl.BlockSpec(memory_space=pl.ANY)],
         out_specs=VMEM,
         scratch_shapes=[
             pltpu.VMEM((rows, n * width), src.dtype),
@@ -94,7 +96,7 @@
         ],
         compiler_params=pltpu.CompilerParams(vmem_limit_bytes=12 << 20),
         name="select_rows",
-    )(index, places, pltpu.with_memory_space_constraint(src, pltpu.HBM))
+    )(index, places, src)
 
 
 def partial_kernel(n, keep, swap, *refs):
@@ -227,15 +229,15 @@
     )
     gathered = [gather(x) for x in chunks]
 
-    def inv_block(first):
-        return pick(index, first, n, inverse, rows)
-
-    def cpl_block(first):
+    def inv_block(first, space):
+        return pick(index, first, n, inverse, rows, space)
+
+    def cpl_block(first, space):
         return select_rows(index, first, n, base, couple, ancestor_rows, rows)
 
     def both(block):
-        sent = block(0)
-        kept = block(n)
+        sent = block(0, pltpu.HBM)
+        kept = block(n, None)
         return kept, partner(sent)
 
     inv = both(inv_block)

time: 93.6 us -> 95.1 us (1.016)
  starting transfers between devices: 32.8 us -> 36.3 us
  Pallas kernels: 26.8 us -> 23.9 us
  local copies, waits for them, and re-layouts: 0.79 us -> 2.7 us
    ppermute x12, starting transfers between devices: 18.3 us -> 22.1 us  [gather(): pieces.append(lax.ppermute(pieces[p], 'row', pairs))]
    unnamed x6 -> x16, local copies, waits for them, and re-layouts: 0.01 us -> 1.92 us
    pallas_call x2, Pallas kernels: 6.01 us -> 4.28 us  [pick(): pl.pallas_call(functools.partial(pick_kernel, first, n), out_shape=jax.Sh...]
    pallas_call x2, Pallas kernels: 9.43 us -> 8.19 us  [select_rows(): pl.pallas_call(functools.partial(select_kernel, first, n, base), out_shap...]
  transfers between devices with their start and end apart: 24 -> 24, of which waited for: 9 -> 9; matrix products, arithmetic and copies ran while one was open for 1% -> 1% of each run, Pallas kernels for 24% -> 21%
where the time goes in v2:
time: 95.1 us; the launch traced here: 93.5 us
  starting transfers between devices  36.3 us (38%)
  waiting for transfers between devices  28.6 us (30%)
  Pallas kernels  23.9 us (25%)
  local copies, waits for them, and re-layouts  2.7 us (3%)
  other arithmetic  1.2 us (1%)
    ppermute x12, waiting for transfers between devices, gather(): pieces.append(lax.ppermute(pieces[p], 'row', pairs))  25.5 us
    ppermute x12, starting transfers between devices, gather(): pieces.append(lax.ppermute(pieces[p], 'row', pairs))  22.1 us
    ppermute x6, starting transfers between devices, on_device(): lax.ppermute(sent[d - 1], 'leaf', [(j ^ d, j) for j in dests[c]])  12.3 us
    pallas_call x4, Pallas kernels, partials(): pl.pallas_call(functools.partial(partial_kernel, n), out_shape=(jax.Shape...  8.77 us
    pallas_call x2, Pallas kernels, select_rows(): pl.pallas_call(functools.partial(select_kernel, first, n, base), out_shap...  8.19 us
    pallas_call x2, Pallas kernels, pick(): pl.pallas_call(functools.partial(pick_kernel, first, n), out_shape=jax.Sh...  4.28 us
    ppermute x6, waiting for transfers between devices, on_device(): lax.ppermute(sent[d - 1], 'leaf', [(j ^ d, j) for j in dests[c]])  3.1 us
    unnamed x16, local copies, waits for them, and re-layouts  1.92 us
  transfers between devices with their start and end apart: 24, of which 9 were waited for; matrix products, arithmetic and copies ran while one was open for 1% of the time, Pallas kernels for 21%

profile of v2, /device:TPU:0, one launch (start us, length us, event | category | flops | bytes accessed | tf_op | source)
XLA Modules:
  0.0 93.5 jit_solution(14471401735762856384)
XLA Ops:
  0.6 0.7 constant_dynamic-slice_fusion.index
  1.3 3.2 %pick.3 = bf16[768,3072]{1,0:T(8,128)(2,1)S(1)} custom-call(s32[1,18]{1,0:T(1,128)S(1)} %constant_dynamic-slice_fusion.index, bf16[768,6144]{1,0:T(8,128)(2,1)} %bitcast.5), custom_call_target="tpu_custom_call" | custom-call | tf_op jit(solution)/shard_map/pick/pallas_call | solution.py:57
  4.6 0.6 collective-permute-start
  5.1 0.4 copy-done
  5.6 1.5 %copy-done.2 = s32[1,512]{1,0:T(1,128)S(1)} copy-done((s32[1,512]{1,0:T(1,128)S(1)}, s32[1,512]{1,0:T(1,128)}, u32[]{:S(2)}) %copy-start.2) | copy-done | bytes 2072
  7.0 4.0 %select_rows.3 = bf16[512,3072]{1,0:T(8,128)(2,1)S(1)} custom-call(s32[1,18]{1,0:T(1,128)S(1)} %constant_dynamic-slice_fusion.index, s32[1,512]{1,0:T(1,128)S(1)} %copy-done.2, bf16[512,6144]{1,0:T(8,128)(2,1)S(1)} %bitcast.9), custom_call_target="tpu_custom_call" | custom-call | tf_op jit(solution)/shard_map/select_rows/pallas_call | solution.py:88
  11.1 0.5 collective-permute-start.9
  11.7 2.5 %collective-permute-start.1 = (bf16[768,256]{1,0:T(8,128)(2,1)S(1)}, bf16[768,256]{1,0:T(8,128)(2,1)S(1)}, u32[]{:S(2)}, u32[]{:S(2)}) collective-permute-start(bf16[768,256]{1,0:T(8,128)(2,1)S(1)} %pad_maximum_fusion.refs_0_), channel_id=1, source_target_pairs={{0,2},{1,5},{2,0},{3,7},{4,6},{5,1},{6,4},{7,3},{8,10},{9,13},{10,... | collective-permute-start | bytes 1179656 | tf_op jit(solution)/shard_map/ppermute | solution.py:223
  14.2 1.5 %collective-permute-start.2 = (bf16[768,256]{1,0:T(8,128)(2,1)S(1)}, bf16[768,256]{1,0:T(8,128)(2,1)S(1)}, u32[]{:S(2)}, u32[]{:S(2)}) collective-permute-start(bf16[768,256]{1,0:T(8,128)(2,1)S(1)} %pad_maximum_fusion.refs_0_), channel_id=1, source_target_pairs={{0,4},{1,3},{2,6},{3,1},{4,0},{5,7},{6,2},{7,5},{8,12},{9,11},{10,... | collective-permute-start | bytes 1179656 | tf_op jit(solution)/shard_map/ppermute | solution.py:223
  15.8 0.6 collective-permute-start.5
  16.4 6.6 %collective-permute-done.1.refs_1_ = bf16[768,256]{1,0:T(8,128)(2,1)S(1)} collective-permute-done((bf16[768,256]{1,0:T(8,128)(2,1)S(1)}, bf16[768,256]{1,0:T(8,128)(2,1)S(1)}, u32[]{:S(2)}, u32[]{:S(2)}) %collective-permute-start.1) | collective-permute-done | bytes 393248 | tf_op jit(solution)/shard_map/ppermute | solution.py:223
  23.0 2.9 %collective-permute-start.3 = (bf16[768,256]{1,0:T(8,128)(2,1)S(1)}, bf16[768,256]{1,0:T(8,128)(2,1)S(1)}, u32[]{:S(2)}, u32[]{:S(2)}) collective-permute-start(bf16[768,256]{1,0:T(8,128)(2,1)S(1)} %collective-permute-done.1.refs_1_), channel_id=1, source_target_pairs={{0,4},{1,3},{2,6},{3,1},{4,0},{5,7},{6,2},{7,5},{8,12},{9,11},{10,... | collective-permute-start | bytes 1179656 | tf_op jit(solution)/shard_map/ppermute | solution.py:223
  25.9 0.3 collective-permute-done.2.refs_2_
  26.2 1.5 %collective-permute-start.6 = (bf16[768,256]{1,0:T(8,128)(2,1)S(1)}, bf16[768,256]{1,0:T(8,128)(2,1)S(1)}, u32[]{:S(2)}, u32[]{:S(2)}) collective-permute-start(bf16[768,256]{1,0:T(8,128)(2,1)S(1)} %slice.18.refs_0_), channel_id=1, source_target_pairs={{0,4},{1,3},{2,6},{3,1},{4,0},{5,7},{6,2},{7,5},{8,12},{9,11},{10,... | collective-permute-start | bytes 1179656 | tf_op jit(solution)/shard_map/ppermute | solution.py:223
  27.7 3.0 %collective-permute-done.5.refs_1_ = bf16[768,256]{1,0:T(8,128)(2,1)S(1)} collective-permute-done((bf16[768,256]{1,0:T(8,128)(2,1)S(1)}, bf16[768,256]{1,0:T(8,128)(2,1)S(1)}, u32[]{:S(2)}, u32[]{:S(2)}) %collective-permute-start.5) | collective-permute-done | bytes 393248 | tf_op jit(solution)/shard_map/ppermute | solution.py:223
  30.7 2.3 %collective-permute-start.7 = (bf16[768,256]{1,0:T(8,128)(2,1)S(1)}, bf16[768,256]{1,0:T(8,128)(2,1)S(1)}, u32[]{:S(2)}, u32[]{:S(2)}) collective-permute-start(bf16[768,256]{1,0:T(8,128)(2,1)S(1)} %collective-permute-done.5.refs_1_), channel_id=1, source_target_pairs={{0,4},{1,3},{2,6},{3,1},{4,0},{5,7},{6,2},{7,5},{8,12},{9,11},{10,... | collective-permute-start | bytes 1179656 | tf_op jit(solution)/shard_map/ppermute | solution.py:223
  33.0 1.0 %pick.2.keep = bf16[768,3072]{1,0:T(8,128)(2,1)S(1)} custom-call(s32[1,18]{1,0:T(1,128)S(1)} %constant_dynamic-slice_fusion.index, bf16[768,6144]{1,0:T(8,128)(2,1)S(1)} %bitcast.8), custom_call_target="tpu_custom_call" | custom-call | tf_op jit(solution)/shard_map/pick/pallas_call | solution.py:57
  34.1 0.0 collective-permute-done.3.refs_3_
  34.1 0.0 collective-permute-done.swap
  34.1 2.6 %partials.4 = (f32[768,256]{1,0:T(8,128)S(1)}, bf16[768,256]{1,0:T(8,128)(2,1)S(1)}) custom-call(bf16[768,3072]{1,0:T(8,128)(2,1)S(1)} %pick.2.keep, bf16[768,3072]{1,0:T(8,128)(2,1)S(1)} %collective-permute-done.swap, bf16[768,256]{1,0:T(8,128)(2,1)S(1)} %pad_maximum_fusion.refs_0_, bf16[768,256]{1,0:T(8,128)(2,1)S(1)} %collective-permute-done.1.refs_1_, ...), custom_call_target="tpu_custom_call" | custom-call | tf_op jit(solution)/shard_map/partials/pallas_call | solution.py:115
  36.7 0.1 collective-permute-start.4
  36.8 0.0 collective-permute-done.6.refs_2_
  36.8 4.1 %collective-permute-done.7.refs_3_ = bf16[768,256]{1,0:T(8,128)(2,1)S(1)} collective-permute-done((bf16[768,256]{1,0:T(8,128)(2,1)S(1)}, bf16[768,256]{1,0:T(8,128)(2,1)S(1)}, u32[]{:S(2)}, u32[]{:S(2)}) %collective-permute-start.7) | collective-permute-done | bytes 393248 | tf_op jit(solution)/shard_map/ppermute | solution.py:223
  40.9 2.6 %partials.5 = (f32[768,256]{1,0:T(8,128)S(1)}, bf16[768,256]{1,0:T(8,128)(2,1)S(1)}) custom-call(bf16[768,3072]{1,0:T(8,128)(2,1)S(1)} %pick.2.keep, bf16[768,3072]{1,0:T(8,128)(2,1)S(1)} %collective-permute-done.swap, bf16[768,256]{1,0:T(8,128)(2,1)S(1)} %slice.18.refs_0_, bf16[768,256]{1,0:T(8,128)(2,1)S(1)} %collective-permute-done.5.refs_1_, ...), custom_call_target="tpu_custom_call" | custom-call | tf_op jit(solution)/shard_map/partials/pallas_call | solution.py:115
  43.5 0.0 copy-start.3
  43.5 0.2 collective-permute-start.8
  43.7 0.0 collective-permute-done.4
  43.7 0.1 add_convert_fusion.1.refs_0_
  43.8 1.9 %collective-permute-start.10 = (bf16[768,256]{1,0:T(8,128)(2,1)S(1)}, bf16[768,256]{1,0:T(8,128)(2,1)S(1)}, u32[]{:S(2)}, u32[]{:S(2)}) collective-permute-start(bf16[768,256]{1,0:T(8,128)(2,1)S(1)} %add_convert_fusion.1.refs_0_), channel_id=1, source_target_pairs={{0,2},{1,5},{2,0},{3,7},{4,6},{5,1},{6,4},{7,3},{8,10},{9,13},{10,... | collective-permute-start | bytes 1179656 | tf_op jit(solution)/shard_map/ppermute | solution.py:223
  45.7 0.0 collective-permute-done.8
  45.8 0.1 add_convert_fusion.refs_0_
  45.8 1.3 %collective-permute-start.17 = (bf16[768,256]{1,0:T(8,128)(2,1)S(1)}, bf16[768,256]{1,0:T(8,128)(2,1)S(1)}, u32[]{:S(2)}, u32[]{:S(2)}) collective-permute-start(bf16[768,256]{1,0:T(8,128)(2,1)S(1)} %add_convert_fusion.refs_0_), channel_id=1, source_target_pairs={{0,2},{1,5},{2,0},{3,7},{4,6},{5,1},{6,4},{7,3},{8,10},{9,13},{10,... | collective-permute-start | bytes 1179656 | tf_op jit(solution)/shard_map/ppermute | solution.py:223
  47.1 1.5 %collective-permute-start.11 = (bf16[768,256]{1,0:T(8,128)(2,1)S(1)}, bf16[768,256]{1,0:T(8,128)(2,1)S(1)}, u32[]{:S(2)}, u32[]{:S(2)}) collective-permute-start(bf16[768,256]{1,0:T(8,128)(2,1)S(1)} %add_convert_fusion.1.refs_0_), channel_id=1, source_target_pairs={{0,4},{1,3},{2,6},{3,1},{4,0},{5,7},{6,2},{7,5},{8,12},{9,11},{10,... | collective-permute-start | bytes 1179656 | tf_op jit(solution)/shard_map/ppermute | solution.py:223
  48.7 5.0 %collective-permute-done.10.refs_1_ = bf16[768,256]{1,0:T(8,128)(2,1)S(1)} collective-permute-done((bf16[768,256]{1,0:T(8,128)(2,1)S(1)}, bf16[768,256]{1,0:T(8,128)(2,1)S(1)}, u32[]{:S(2)}, u32[]{:S(2)}) %collective-permute-start.10) | collective-permute-done | bytes 393248 | tf_op jit(solution)/shard_map/ppermute | solution.py:223
  53.7 2.9 %collective-permute-start.12 = (bf16[768,256]{1,0:T(8,128)(2,1)S(1)}, bf16[768,256]{1,0:T(8,128)(2,1)S(1)}, u32[]{:S(2)}, u32[]{:S(2)}) collective-permute-start(bf16[768,256]{1,0:T(8,128)(2,1)S(1)} %collective-permute-done.10.refs_1_), channel_id=1, source_target_pairs={{0,4},{1,3},{2,6},{3,1},{4,0},{5,7},{6,2},{7,5},{8,12},{9,11},{10,... | collective-permute-start | bytes 1179656 | tf_op jit(solution)/shard_map/ppermute | solution.py:223
  56.6 0.0 collective-permute-start.18
  56.6 5.5 %collective-permute-done.17.refs_1_ = bf16[768,256]{1,0:T(8,128)(2,1)S(1)} collective-permute-done((bf16[768,256]{1,0:T(8,128)(2,1)S(1)}, bf16[768,256]{1,0:T(8,128)(2,1)S(1)}, u32[]{:S(2)}, u32[]{:S(2)}) %collective-permute-start.17) | collective-permute-done | bytes 393248 | tf_op jit(solution)/shard_map/ppermute | solution.py:223
  62.1 2.9 %collective-permute-start.19 = (bf16[768,256]{1,0:T(8,128)(2,1)S(1)}, bf16[768,256]{1,0:T(8,128)(2,1)S(1)}, u32[]{:S(2)}, u32[]{:S(2)}) collective-permute-start(bf16[768,256]{1,0:T(8,128)(2,1)S(1)} %collective-permute-done.17.refs_1_), channel_id=1, source_target_pairs={{0,4},{1,3},{2,6},{3,1},{4,0},{5,7},{6,2},{7,5},{8,12},{9,11},{10,... | collective-permute-start | bytes 1179656 | tf_op jit(solution)/shard_map/ppermute | solution.py:223
  65.0 4.2 %select_rows.2.keep = bf16[512,3072]{1,0:T(8,128)(2,1)S(1)} custom-call(s32[1,18]{1,0:T(1,128)S(1)} %constant_dynamic-slice_fusion.index, s32[1,512]{1,0:T(1,128)S(1)} %copy-done.3, bf16[512,6144]{1,0:T(8,128)(2,1)S(1)} %bitcast.10), custom_call_target="tpu_custom_call" | custom-call | tf_op jit(solution)/shard_map/select_rows/pallas_call | solution.py:88
  69.2 0.0 collective-permute-done.11.refs_2_
  69.2 1.8 %partials.6 = (f32[512,256]{1,0:T(8,128)S(1)}, bf16[512,256]{1,0:T(8,128)(2,1)S(1)}) custom-call(bf16[512,3072]{1,0:T(8,128)(2,1)S(1)} %select_rows.2.keep, bf16[512,3072]{1,0:T(8,128)(2,1)S(1)} %collective-permute-done.9.swap, bf16[768,256]{1,0:T(8,128)(2,1)S(1)} %add_convert_fusion.1.refs_0_, bf16[768,256]{1,0:T(8,128)(2,1)S(1)} %collective-permute-done.10.refs_1_, ...), custom_call_target="tpu_custom_call" | custom-call | tf_op jit(solution)/shard_map/partials/pallas_call | solution.py:115
  71.0 0.1 collective-permute-start.13
  71.1 0.0 collective-permute-done.18.refs_2_
  71.1 1.1 %collective-permute-done.19.refs_3_ = bf16[768,256]{1,0:T(8,128)(2,1)S(1)} collective-permute-done((bf16[768,256]{1,0:T(8,128)(2,1)S(1)}, bf16[768,256]{1,0:T(8,128)(2,1)S(1)}, u32[]{:S(2)}, u32[]{:S(2)}) %collective-permute-start.19) | collective-permute-done | bytes 393248 | tf_op jit(solution)/shard_map/ppermute | solution.py:223
  72.2 1.8 %partials.7 = (f32[512,256]{1,0:T(8,128)S(1)}, bf16[512,256]{1,0:T(8,128)(2,1)S(1)}) custom-call(bf16[512,3072]{1,0:T(8,128)(2,1)S(1)} %select_rows.2.keep, bf16[512,3072]{1,0:T(8,128)(2,1)S(1)} %collective-permute-done.9.swap, bf16[768,256]{1,0:T(8,128)(2,1)S(1)} %add_convert_fusion.refs_0_, bf16[768,256]{1,0:T(8,128)(2,1)S(1)} %collective-permute-done.17.refs_1_, ...), custom_call_target="tpu_custom_call" | custom-call | tf_op jit(solution)/shard_map/partials/pallas_call | solution.py:115
  73.9 0.0 copy-start.1
  74.0 0.5 collective-permute-start.20
  74.4 0.0 collective-permute-done.13.other
  74.4 0.6 split.2
  75.1 1.3 %collective-permute-start.14 = (bf16[512,128]{1,0:T(8,128)(2,1)S(1)}, bf16[512,128]{1,0:T(8,128)(2,1)S(1)}, u32[]{:S(2)}, u32[]{:S(2)}) collective-permute-start(bf16[512,128]{1,0:T(8,128)(2,1)S(1)} %get-tuple-element.29), channel_id=1, source_target_pairs={{8,0},{16,24},{9,1},{17,25},{10,2},{18,26},{11,3},{19,27},{12,4},{... | collective-permute-start | bytes 393224 | tf_op jit(solution)/shard_map/ppermute | solution.py:260
  76.4 1.3 %collective-permute-start.15 = (bf16[512,128]{1,0:T(8,128)(2,1)S(1)}, bf16[512,128]{1,0:T(8,128)(2,1)S(1)}, u32[]{:S(2)}, u32[]{:S(2)}) collective-permute-start(bf16[512,128]{1,0:T(8,128)(2,1)S(1)} %get-tuple-element.30), channel_id=1, source_target_pairs={{16,0},{8,24},{17,1},{9,25},{18,2},{10,26},{19,3},{11,27},{20,4},{... | collective-permute-start | bytes 393224 | tf_op jit(solution)/shard_map/ppermute | solution.py:260
  77.7 5.9 %collective-permute-start.16 = (bf16[512,128]{1,0:T(8,128)(2,1)S(1)}, bf16[512,128]{1,0:T(8,128)(2,1)S(1)}, u32[]{:S(2)}, u32[]{:S(2)}) collective-permute-start(bf16[512,128]{1,0:T(8,128)(2,1)S(1)} %get-tuple-element.31), channel_id=1, source_target_pairs={{24,0},{0,24},{25,1},{1,25},{26,2},{2,26},{27,3},{3,27},{28,4},{4,... | collective-permute-start | bytes 393224 | tf_op jit(solution)/shard_map/ppermute | solution.py:260
  83.6 0.0 collective-permute-done.20.other
  83.6 0.7 split.3
  84.3 1.9 %collective-permute-start.21 = (bf16[512,128]{1,0:T(8,128)(2,1)S(1)}, bf16[512,128]{1,0:T(8,128)(2,1)S(1)}, u32[]{:S(2)}, u32[]{:S(2)}) collective-permute-start(bf16[512,128]{1,0:T(8,128)(2,1)S(1)} %get-tuple-element.35), channel_id=1, source_target_pairs={{0,8},{24,16},{1,9},{25,17},{2,10},{26,18},{3,11},{27,19},{4,12},{... | collective-permute-start | bytes 393224 | tf_op jit(solution)/shard_map/ppermute | solution.py:260
  86.2 1.3 %collective-permute-start.22 = (bf16[512,128]{1,0:T(8,128)(2,1)S(1)}, bf16[512,128]{1,0:T(8,128)(2,1)S(1)}, u32[]{:S(2)}, u32[]{:S(2)}) collective-permute-start(bf16[512,128]{1,0:T(8,128)(2,1)S(1)} %get-tuple-element.36), channel_id=1, source_target_pairs={{24,8},{0,16},{25,9},{1,17},{26,10},{2,18},{27,11},{3,19},{28,12},... | collective-permute-start | bytes 393224 | tf_op jit(solution)/shard_map/ppermute | solution.py:260
  87.5 0.0 collective-permute-done.14.refs_1_
  87.5 0.7 collective-permute-start.23
  88.2 1.0 %maximum_bitcast_fusion = bf16[1,768,512]{2,1,0:T(8,128)(2,1)} fusion(bf16[768,128]{1,0:T(8,128)(2,1)S(1)} %get-tuple-element.41, bf16[768,256]{1,0:T(8,128)(2,1)S(1)} %add_convert_fusion.refs_0_, bf16[768,128]{1,0:T(8,128)(2,1)S(1)} %get-tuple-element.40), kind=kLoop, calls=%fused_computation | loop fusion | flops 2359296 | bytes 1572864 | tf_op jit(solution)/shard_map/broadcast_in_dim | solution.py:266
  89.1 0.0 collective-permute-done.15.refs_2_
  89.1 0.0 collective-permute-done.16.refs_3_
  89.1 0.9 collective-permute-done.21.refs_5_
  90.0 2.2 %collective-permute-done.22.refs_6_ = bf16[512,128]{1,0:T(8,128)(2,1)S(1)} collective-permute-done((bf16[512,128]{1,0:T(8,128)(2,1)S(1)}, bf16[512,128]{1,0:T(8,128)(2,1)S(1)}, u32[]{:S(2)}, u32[]{:S(2)}) %collective-permute-start.22) | collective-permute-done | bytes 131104 | tf_op jit(solution)/shard_map/ppermute | solution.py:260
  92.2 1.3 %finish.1 = f32[512,128]{1,0:T(8,128)} custom-call(s32[1,18]{1,0:T(1,128)S(1)} %constant_dynamic-slice_fusion.index, f32[512,128]{1,0:T(8,128)S(1)} %copy-done.1, f32[512,128]{1,0:T(8,128)S(1)} %get-tuple-element.28.refs_0_, bf16[512,128]{1,0:T(8,128)(2,1)S(1)} %collective-permute-done.14.refs_1_, bf16[512,128]{1,0:T(8,128)(2,1)S(1)} %collective-permute-done.15.refs_2_, ...), custom_call_target="tpu_custom_call" | custom-call | tf_op jit(solution)/shard_map/finish/pallas_call | solution.py:168
  (20 shorter events, 0.2 us)
Async XLA Ops:
  1.3 4.2 %copy-start = (bf16[1,512,6144]{2,1,0:T(8,128)(2,1)S(1)}, bf16[1,512,6144]{2,1,0:T(8,128)(2,1)}, u32[]{:S(2)}) copy-start(bf16[1,512,6144]{2,1,0:T(8,128)(2,1)} %param.8) | copy-start | bytes 18874372
  1.3 31.7 %slice-start = ((s8[9437184]{0:T(1024)(128)(4,1)}), s8[4194304]{0:T(1024)(128)(4,1)S(1)}, s32[]{:S(2)}) async-start(s8[9437184]{0:T(1024)(128)(4,1)} %bitcast.6), calls=%async_computation | async-start | bytes 8388608
  1.3 31.7 %slice-start.1 = ((s8[9437184]{0:T(1024)(128)(4,1)}), s8[4194304]{0:T(1024)(128)(4,1)S(1)}, s32[]{:S(2)}) async-start(s8[9437184]{0:T(1024)(128)(4,1)} %bitcast.6), calls=%async_computation.1 | async-start | bytes 8388608
  4.6 29.5 %collective-permute-start = (bf16[768,3072]{1,0:T(8,128)(2,1)S(1)}, bf16[768,3072]{1,0:T(8,128)(2,1)S(1)}, u32[]{:S(2)}, u32[]{:S(2)}) collective-permute-start(bf16[768,3072]{1,0:T(8,128)(2,1)S(1)} %pick.3), channel_id=1, source_target_pairs={{0,1},{1,0},{2,3},{3,2},{4,5},{5,4},{6,7},{7,6},{8,9},{9,8},{10,11... | collective-permute-start | bytes 14155784 | tf_op jit(solution)/shard_map/ppermute | solution.py:216
  5.6 1.5 %copy-start.2 = (s32[1,512]{1,0:T(1,128)S(1)}, s32[1,512]{1,0:T(1,128)}, u32[]{:S(2)}) copy-start(s32[1,512]{1,0:T(1,128)} %places.3) | copy-start | bytes 6148
  7.0 4.6 %copy-start.4 = (bf16[1,768,512]{2,1,0:T(8,128)(2,1)S(1)}, bf16[1,768,512]{2,1,0:T(8,128)(2,1)}, u32[]{:S(2)}) copy-start(bf16[1,768,512]{2,1,0:T(8,128)(2,1)} %param.7) | copy-start | bytes 2359300
  7.0 26.0 %slice-start.2 = ((s8[9437184]{0:T(1024)(128)(4,1)}), s8[1048576]{0:T(1024)(128)(4,1)S(1)}, s32[]{:S(2)}) async-start(s8[9437184]{0:T(1024)(128)(4,1)} %bitcast.6), calls=%async_computation.2 | async-start | bytes 2097152
  11.1 58.1 %collective-permute-start.9 = (bf16[512,3072]{1,0:T(8,128)(2,1)S(1)}, bf16[512,3072]{1,0:T(8,128)(2,1)S(1)}, u32[]{:S(2)}, u32[]{:S(2)}) collective-permute-start(bf16[512,3072]{1,0:T(8,128)(2,1)S(1)} %select_rows.3), channel_id=1, source_target_pairs={{0,1},{1,0},{2,3},{3,2},{4,5},{5,4},{6,7},{7,6},{8,9},{9,8},{10,11... | collective-permute-start | bytes 9437192 | tf_op jit(solution)/shard_map/ppermute | solution.py:216
  11.7 11.3 %collective-permute-start.1 = (bf16[768,256]{1,0:T(8,128)(2,1)S(1)}, bf16[768,256]{1,0:T(8,128)(2,1)S(1)}, u32[]{:S(2)}, u32[]{:S(2)}) collective-permute-start(bf16[768,256]{1,0:T(8,128)(2,1)S(1)} %pad_maximum_fusion.refs_0_), channel_id=1, source_target_pairs={{0,2},{1,5},{2,0},{3,7},{4,6},{5,1},{6,4},{7,3},{8,10},{9,13},{10,... | collective-permute-start | bytes 1179656 | tf_op jit(solution)/shard_map/ppermute | solution.py:223
  14.2 12.0 %collective-permute-start.2 = (bf16[768,256]{1,0:T(8,128)(2,1)S(1)}, bf16[768,256]{1,0:T(8,128)(2,1)S(1)}, u32[]{:S(2)}, u32[]{:S(2)}) collective-permute-start(bf16[768,256]{1,0:T(8,128)(2,1)S(1)} %pad_maximum_fusion.refs_0_), channel_id=1, source_target_pairs={{0,4},{1,3},{2,6},{3,1},{4,0},{5,7},{6,2},{7,5},{8,12},{9,11},{10,... | collective-permute-start | bytes 1179656 | tf_op jit(solution)/shard_map/ppermute | solution.py:223
  15.8 14.9 %collective-permute-start.5 = (bf16[768,256]{1,0:T(8,128)(2,1)S(1)}, bf16[768,256]{1,0:T(8,128)(2,1)S(1)}, u32[]{:S(2)}, u32[]{:S(2)}) collective-permute-start(bf16[768,256]{1,0:T(8,128)(2,1)S(1)} %slice.18.refs_0_), channel_id=1, source_target_pairs={{0,2},{1,5},{2,0},{3,7},{4,6},{5,1},{6,4},{7,3},{8,10},{9,13},{10,... | collective-permute-start | bytes 1179656 | tf_op jit(solution)/shard_map/ppermute | solution.py:223
  23.0 11.1 %collective-permute-start.3 = (bf16[768,256]{1,0:T(8,128)(2,1)S(1)}, bf16[768,256]{1,0:T(8,128)(2,1)S(1)}, u32[]{:S(2)}, u32[]{:S(2)}) collective-permute-start(bf16[768,256]{1,0:T(8,128)(2,1)S(1)} %collective-permute-done.1.refs_1_), channel_id=1, source_target_pairs={{0,4},{1,3},{2,6},{3,1},{4,0},{5,7},{6,2},{7,5},{8,12},{9,11},{10,... | collective-permute-start | bytes 1179656 | tf_op jit(solution)/shard_map/ppermute | solution.py:223
  26.2 10.6 %collective-permute-start.6 = (bf16[768,256]{1,0:T(8,128)(2,1)S(1)}, bf16[768,256]{1,0:T(8,128)(2,1)S(1)}, u32[]{:S(2)}, u32[]{:S(2)}) collective-permute-start(bf16[768,256]{1,0:T(8,128)(2,1)S(1)} %slice.18.refs_0_), channel_id=1, source_target_pairs={{0,4},{1,3},{2,6},{3,1},{4,0},{5,7},{6,2},{7,5},{8,12},{9,11},{10,... | collective-permute-start | bytes 1179656 | tf_op jit(solution)/shard_map/ppermute | solution.py:223
  30.7 10.2 %collective-permute-start.7 = (bf16[768,256]{1,0:T(8,128)(2,1)S(1)}, bf16[768,256]{1,0:T(8,128)(2,1)S(1)}, u32[]{:S(2)}, u32[]{:S(2)}) collective-permute-start(bf16[768,256]{1,0:T(8,128)(2,1)S(1)} %collective-permute-done.5.refs_1_), channel_id=1, source_target_pairs={{0,4},{1,3},{2,6},{3,1},{4,0},{5,7},{6,2},{7,5},{8,12},{9,11},{10,... | collective-permute-start | bytes 1179656 | tf_op jit(solution)/shard_map/ppermute | solution.py:223
  36.7 7.0 %collective-permute-start.4 = (bf16[768,256]{1,0:T(8,128)(2,1)S(1)}, bf16[768,256]{1,0:T(8,128)(2,1)S(1)}, u32[]{:S(2)}, u32[]{:S(2)}) collective-permute-start(bf16[768,256]{1,0:T(8,128)(2,1)S(1)} %get-tuple-element.23), channel_id=1, source_target_pairs={{0,1},{1,0},{2,3},{3,2},{4,5},{5,4},{6,7},{7,6},{8,9},{9,8},{10,11... | collective-permute-start | bytes 1179656 | tf_op jit(solution)/shard_map/ppermute | solution.py:216
  43.5 21.5 %copy-start.3 = (s32[1,512]{1,0:T(1,128)S(1)}, s32[1,512]{1,0:T(1,128)}, u32[]{:S(2)}) copy-start(s32[1,512]{1,0:T(1,128)} %places.3) | copy-start | bytes 6148
  43.5 2.2 %collective-permute-start.8 = (bf16[768,256]{1,0:T(8,128)(2,1)S(1)}, bf16[768,256]{1,0:T(8,128)(2,1)S(1)}, u32[]{:S(2)}, u32[]{:S(2)}) collective-permute-start(bf16[768,256]{1,0:T(8,128)(2,1)S(1)} %get-tuple-element.25), channel_id=1, source_target_pairs={{0,1},{1,0},{2,3},{3,2},{4,5},{5,4},{6,7},{7,6},{8,9},{9,8},{10,11... | collective-permute-start | bytes 1179656 | tf_op jit(solution)/shard_map/ppermute | solution.py:216
  43.8 9.8 %collective-permute-start.10 = (bf16[768,256]{1,0:T(8,128)(2,1)S(1)}, bf16[768,256]{1,0:T(8,128)(2,1)S(1)}, u32[]{:S(2)}, u32[]{:S(2)}) collective-permute-start(bf16[768,256]{1,0:T(8,128)(2,1)S(1)} %add_convert_fusion.1.refs_0_), channel_id=1, source_target_pairs={{0,2},{1,5},{2,0},{3,7},{4,6},{5,1},{6,4},{7,3},{8,10},{9,13},{10,... | collective-permute-start | bytes 1179656 | tf_op jit(solution)/shard_map/ppermute | solution.py:223
  45.8 16.2 %collective-permute-start.17 = (bf16[768,256]{1,0:T(8,128)(2,1)S(1)}, bf16[768,256]{1,0:T(8,128)(2,1)S(1)}, u32[]{:S(2)}, u32[]{:S(2)}) collective-permute-start(bf16[768,256]{1,0:T(8,128)(2,1)S(1)} %add_convert_fusion.refs_0_), channel_id=1, source_target_pairs={{0,2},{1,5},{2,0},{3,7},{4,6},{5,1},{6,4},{7,3},{8,10},{9,13},{10,... | collective-permute-start | bytes 1179656 | tf_op jit(solution)/shard_map/ppermute | solution.py:223
  47.1 22.0 %collective-permute-start.11 = (bf16[768,256]{1,0:T(8,128)(2,1)S(1)}, bf16[768,256]{1,0:T(8,128)(2,1)S(1)}, u32[]{:S(2)}, u32[]{:S(2)}) collective-permute-start(bf16[768,256]{1,0:T(8,128)(2,1)S(1)} %add_convert_fusion.1.refs_0_), channel_id=1, source_target_pairs={{0,4},{1,3},{2,6},{3,1},{4,0},{5,7},{6,2},{7,5},{8,12},{9,11},{10,... | collective-permute-start | bytes 1179656 | tf_op jit(solution)/shard_map/ppermute | solution.py:223
  53.7 15.5 %collective-permute-start.12 = (bf16[768,256]{1,0:T(8,128)(2,1)S(1)}, bf16[768,256]{1,0:T(8,128)(2,1)S(1)}, u32[]{:S(2)}, u32[]{:S(2)}) collective-permute-start(bf16[768,256]{1,0:T(8,128)(2,1)S(1)} %collective-permute-done.10.refs_1_), channel_id=1, source_target_pairs={{0,4},{1,3},{2,6},{3,1},{4,0},{5,7},{6,2},{7,5},{8,12},{9,11},{10,... | collective-permute-start | bytes 1179656 | tf_op jit(solution)/shard_map/ppermute | solution.py:223
  56.6 14.5 %collective-permute-start.18 = (bf16[768,256]{1,0:T(8,128)(2,1)S(1)}, bf16[768,256]{1,0:T(8,128)(2,1)S(1)}, u32[]{:S(2)}, u32[]{:S(2)}) collective-permute-start(bf16[768,256]{1,0:T(8,128)(2,1)S(1)} %add_convert_fusion.refs_0_), channel_id=1, source_target_pairs={{0,4},{1,3},{2,6},{3,1},{4,0},{5,7},{6,2},{7,5},{8,12},{9,11},{10,... | collective-permute-start | bytes 1179656 | tf_op jit(solution)/shard_map/ppermute | solution.py:223
  62.1 10.1 %collective-permute-start.19 = (bf16[768,256]{1,0:T(8,128)(2,1)S(1)}, bf16[768,256]{1,0:T(8,128)(2,1)S(1)}, u32[]{:S(2)}, u32[]{:S(2)}) collective-permute-start(bf16[768,256]{1,0:T(8,128)(2,1)S(1)} %collective-permute-done.17.refs_1_), channel_id=1, source_target_pairs={{0,4},{1,3},{2,6},{3,1},{4,0},{5,7},{6,2},{7,5},{8,12},{9,11},{10,... | collective-permute-start | bytes 1179656 | tf_op jit(solution)/shard_map/ppermute | solution.py:223
  71.0 3.4 %collective-permute-start.13 = (bf16[512,256]{1,0:T(8,128)(2,1)S(1)}, bf16[512,256]{1,0:T(8,128)(2,1)S(1)}, u32[]{:S(2)}, u32[]{:S(2)}) collective-permute-start(bf16[512,256]{1,0:T(8,128)(2,1)S(1)} %get-tuple-element.27), channel_id=1, source_target_pairs={{0,1},{1,0},{2,3},{3,2},{4,5},{5,4},{6,7},{7,6},{8,9},{9,8},{10,11... | collective-permute-start | bytes 786440 | tf_op jit(solution)/shard_map/ppermute | solution.py:216
  73.9 18.3 %copy-start.1 = (f32[512,128]{1,0:T(8,128)S(1)}, f32[512,128]{1,0:T(8,128)}, u32[]{:S(2)}) copy-start(f32[512,128]{1,0:T(8,128)} %rhs.1) | copy-start | bytes 786436
  74.0 9.7 %collective-permute-start.20 = (bf16[512,256]{1,0:T(8,128)(2,1)S(1)}, bf16[512,256]{1,0:T(8,128)(2,1)S(1)}, u32[]{:S(2)}, u32[]{:S(2)}) collective-permute-start(bf16[512,256]{1,0:T(8,128)(2,1)S(1)} %get-tuple-element.33), channel_id=1, source_target_pairs={{0,1},{1,0},{2,3},{3,2},{4,5},{5,4},{6,7},{7,6},{8,9},{9,8},{10,11... | collective-permute-start | bytes 786440 | tf_op jit(solution)/shard_map/ppermute | solution.py:216
  75.1 12.4 %collective-permute-start.14 = (bf16[512,128]{1,0:T(8,128)(2,1)S(1)}, bf16[512,128]{1,0:T(8,128)(2,1)S(1)}, u32[]{:S(2)}, u32[]{:S(2)}) collective-permute-start(bf16[512,128]{1,0:T(8,128)(2,1)S(1)} %get-tuple-element.29), channel_id=1, source_target_pairs={{8,0},{16,24},{9,1},{17,25},{10,2},{18,26},{11,3},{19,27},{12,4},{... | collective-permute-start | bytes 393224 | tf_op jit(solution)/shard_map/ppermute | solution.py:260
  76.4 12.7 %collective-permute-start.15 = (bf16[512,128]{1,0:T(8,128)(2,1)S(1)}, bf16[512,128]{1,0:T(8,128)(2,1)S(1)}, u32[]{:S(2)}, u32[]{:S(2)}) collective-permute-start(bf16[512,128]{1,0:T(8,128)(2,1)S(1)} %get-tuple-element.30), channel_id=1, source_target_pairs={{16,0},{8,24},{17,1},{9,25},{18,2},{10,26},{19,3},{11,27},{20,4},{... | collective-permute-start | bytes 393224 | tf_op jit(solution)/shard_map/ppermute | solution.py:260
  77.7 11.4 %collective-permute-start.16 = (bf16[512,128]{1,0:T(8,128)(2,1)S(1)}, bf16[512,128]{1,0:T(8,128)(2,1)S(1)}, u32[]{:S(2)}, u32[]{:S(2)}) collective-permute-start(bf16[512,128]{1,0:T(8,128)(2,1)S(1)} %get-tuple-element.31), channel_id=1, source_target_pairs={{24,0},{0,24},{25,1},{1,25},{26,2},{2,26},{27,3},{3,27},{28,4},{4,... | collective-permute-start | bytes 393224 | tf_op jit(solution)/shard_map/ppermute | solution.py:260
  84.3 5.7 %collective-permute-start.21 = (bf16[512,128]{1,0:T(8,128)(2,1)S(1)}, bf16[512,128]{1,0:T(8,128)(2,1)S(1)}, u32[]{:S(2)}, u32[]{:S(2)}) collective-permute-start(bf16[512,128]{1,0:T(8,128)(2,1)S(1)} %get-tuple-element.35), channel_id=1, source_target_pairs={{0,8},{24,16},{1,9},{25,17},{2,10},{26,18},{3,11},{27,19},{4,12},{... | collective-permute-start | bytes 393224 | tf_op jit(solution)/shard_map/ppermute | solution.py:260
  86.2 6.1 %collective-permute-start.22 = (bf16[512,128]{1,0:T(8,128)(2,1)S(1)}, bf16[512,128]{1,0:T(8,128)(2,1)S(1)}, u32[]{:S(2)}, u32[]{:S(2)}) collective-permute-start(bf16[512,128]{1,0:T(8,128)(2,1)S(1)} %get-tuple-element.36), channel_id=1, source_target_pairs={{24,8},{0,16},{25,9},{1,17},{26,10},{2,18},{27,11},{3,19},{28,12},... | collective-permute-start | bytes 393224 | tf_op jit(solution)/shard_map/ppermute | solution.py:260
  87.5 4.7 %collective-permute-start.23 = (bf16[512,128]{1,0:T(8,128)(2,1)S(1)}, bf16[512,128]{1,0:T(8,128)(2,1)S(1)}, u32[]{:S(2)}, u32[]{:S(2)}) collective-permute-start(bf16[512,128]{1,0:T(8,128)(2,1)S(1)} %get-tuple-element.37), channel_id=1, source_target_pairs={{16,8},{8,16},{17,9},{9,17},{18,10},{10,18},{19,11},{11,19},{20,12... | collective-permute-start | bytes 393224 | tf_op jit(solution)/shard_map/ppermute | solution.py:260

commit v3 on v1

v3 whole, which is shorter than its diff:
```python
import functools

import jax
import jax.numpy as jnp
from jax import lax
from jax.experimental import pallas as pl
from jax.experimental.pallas import tpu as pltpu
from jax.sharding import PartitionSpec as P

VMEM = pl.BlockSpec(memory_space=pltpu.VMEM)
SPLIT = 4
F32 = jnp.float32
BF16 = jnp.bfloat16


def block_of(masks, other, j):
    me = lax.axis_index("row")
    core = me & 1
    if other:
        me, core = me ^ 1, 1 - core
    return me ^ jnp.where(core == 0, masks[0][j], masks[1][j])


def block_copies(masks, other, src, out, sem):
    n = len(masks[0])
    width = out.shape[1] // n
    rows = out.shape[0] // SPLIT
    copies = []
    for j in range(n):
        start = pl.multiple_of(block_of(masks, other, j) * width, 128)
        copies.append(
            [
                pltpu.make_async_copy(
                    src.at[pl.ds(r * rows, rows), pl.ds(start, width)],
                    out.at[pl.ds(r * rows, rows), pl.ds(j * width, width)],
                    sem.at[j, r],
                )
                for r in range(SPLIT)
            ]
        )
    return copies


def pick_kernel(masks, other, src, out, sem):
    copies = block_copies(masks, other, src, out, sem)
    for group in copies:
        for copy in group:
            copy.start()
    for group in copies:
        for copy in group:
            copy.wait()


def column_block(src, start, width):
    return lax.dynamic_slice_in_dim(src, start * width, width, 1)


def pick(masks, other, src, width):
    n = len(masks[0])
    if width % 128:
        blocks = [column_block(src, block_of(masks, other, j), width) for j in range(n)]
        return jnp.concatenate(blocks, axis=1)
    if other:
        src = pltpu.with_memory_space_constraint(src, pltpu.HBM)
    return pl.pallas_call(
        functools.partial(pick_kernel, masks, other),
        out_shape=jax.ShapeDtypeStruct((src.shape[0], n * width), src.dtype),
        in_specs=[pl.BlockSpec(memory_space=pl.ANY)],
        out_specs=VMEM,
        scratch_shapes=[pltpu.SemaphoreType.DMA((n, SPLIT))],
        compiler_params=pltpu.CompilerParams(vmem_limit_bytes=8 << 20),
        name="pick",
    )(src)


def one_hot(places, rows):
    first = lax.axis_index("row") * rows
    return lax.broadcasted_iota(jnp.int32, (rows, rows), 0) + first == places


def select_kernel(masks, other, places, src, out, buf, sem):
    rows, n = buf.shape[0], len(masks[0])
    width = buf.shape[1] // n
    copies = block_copies(masks, other, src, buf, sem)
    for group in copies:
        for copy in group:
            copy.start()
    hot = jnp.where(one_hot(places[...], rows), 1.0, 0.0).astype(BF16)
    for j, group in enumerate(copies):
        for copy in group:
            copy.wait()
        block = slice(j * width, (j + 1) * width)
        out[:, block] = jnp.dot(hot, buf[:, block], preferred_element_type=F32).astype(BF16)


def select_rows(masks, other, src, places, width):
    rows, n = src.shape[0], len(masks[0])
    if width % 128:
        return one_hot(places, rows).astype(src.dtype) @ pick(masks, other, src, width)
    return pl.pallas_call(
        functools.partial(select_kernel, masks, other),
        out_shape=jax.ShapeDtypeStruct((rows, n * width), src.dtype),
        in_specs=[VMEM, pl.BlockSpec(memory_space=pl.ANY)],
        out_specs=VMEM,
        scratch_shapes=[
            pltpu.VMEM((rows, n * width), src.dtype),
            pltpu.SemaphoreType.DMA((n, SPLIT)),
        ],
        compiler_params=pltpu.CompilerParams(vmem_limit_bytes=12 << 20),
        name="select_rows",
    )(places, src)


def partial_kernel(n, first, had, keep, swap, *refs):
    pieces, sums, (own, other, joined) = refs[:n], refs[n : n + 2 * had], refs[n + 2 * had :]
    depth = pieces[0].shape[0]
    for j in range(n):
        joined[j * depth : (j + 1) * depth, :] = pieces[j][...]
    columns = slice(first * depth, (first + n) * depth)
    for k, (block, out) in enumerate(((keep, own), (swap, other))):
        value = jnp.dot(block[:, columns], joined[...], preferred_element_type=F32)
        if had:
            value = value + sums[k][...]
        out[...] = value.astype(out.dtype)


def partials(keep, swap, pieces, first=0, sums=(), other_type=BF16):
    n = len(pieces)
    rows = keep.shape[0]
    depth, width = pieces[0].shape
    return pl.pallas_call(
        functools.partial(partial_kernel, n, first, bool(sums)),
        out_shape=(
            jax.ShapeDtypeStruct((rows, width), F32),
            jax.ShapeDtypeStruct((rows, width), other_type),
        ),
        in_specs=[VMEM] * (2 + n + len(sums)),
        out_specs=(VMEM, VMEM),
        scratch_shapes=[pltpu.VMEM((n * depth, width), BF16)],
        compiler_params=pltpu.CompilerParams(vmem_limit_bytes=12 << 20),
        name="partials",
    )(keep, swap, *pieces, *sums)


def place_of(group, leaf):
    return sum(jnp.where(leaf == j, i, 0) for i, j in enumerate(group))


def member(group, leaf):
    return sum(jnp.where(leaf == j, 1.0, 0.0) for j in group)


def split_kernel(group, narrow, own, other, total, *pieces):
    leaf = lax.axis_index("leaf")
    for d in range(len(pieces) + 1):
        start = pl.multiple_of(place_of(group, leaf ^ d) * narrow, 128)
        piece = own[:, pl.ds(start, narrow)] + other[:, pl.ds(start, narrow)].astype(F32)
        if d == 0:
            total[...] = jnp.where(member(group, leaf) > 0, piece, 0.0)
        else:
            pieces[d - 1][...] = piece.astype(BF16)


def split(group, leaves, narrow, own, other):
    rows = own.shape[0]
    if narrow % 128:
        leaf = lax.axis_index("leaf")
        q = own + other.astype(F32)
        blocks = [column_block(q, place_of(group, leaf ^ d), narrow) for d in range(leaves)]
        total = jnp.where(member(group, leaf) > 0, blocks[0], 0.0)
        return total, *[block.astype(BF16) for block in blocks[1:]]
    return pl.pallas_call(
        functools.partial(split_kernel, group, narrow),
        out_shape=[jax.ShapeDtypeStruct((rows, narrow), F32)]
        + [jax.ShapeDtypeStruct((rows, narrow), BF16)] * (leaves - 1),
        in_specs=[VMEM, VMEM],
        out_specs=[VMEM] * leaves,
        compiler_params=pltpu.CompilerParams(vmem_limit_bytes=6 << 20),
        name="split",
    )(own, other)


def on_device(sep_inverse, rhs_block, coupling, ancestor_rows, ancestor_rhs):
    inverse, rhs, couple = sep_inverse[0], rhs_block[0], coupling[0]
    leaves, n_row = lax.axis_size("leaf"), lax.axis_size("row")
    rows = inverse.shape[0]
    width = rhs.shape[1]
    narrow = width // leaves
    dims = [1 << b for b in range(1, n_row.bit_length() - 1)]
    routes = (dims, dims[::-1])
    masks = ([0], [0])
    for step in range(len(dims)):
        for k in (0, 1):
            masks[k].extend([m ^ routes[k][step] for m in masks[k]])
    edge = leaves // 4
    cut = edge * narrow
    is_inner = lambda j: edge <= j < leaves - edge
    dests = [[j for j in range(leaves) if is_inner(j) == bool(c)] for c in (0, 1)]

    def partner(x):
        return lax.ppermute(x, "row", [(i, i ^ 1) for i in range(n_row)])

    def gather(x):
        pieces = [x]
        for step in range(len(dims)):
            pairs = [(i, i ^ routes[i & 1][step]) for i in range(n_row)]
            for p in range(len(pieces)):
                pieces.append(lax.ppermute(pieces[p], "row", pairs))
        return pieces

    chunks = (
        jnp.concatenate([rhs[:, :cut], rhs[:, width - cut :]], axis=1),
        rhs[:, cut : width - cut],
    )
    gathered = [gather(x) for x in chunks]

    def inv_block(other):
        return pick(masks, other, inverse, rows)

    def cpl_block(other):
        return select_rows(masks, other, couple, ancestor_rows, rows)

    def both(block):
        sent = block(True)
        kept = block(False)
        return kept, partner(sent)

    inv = both(inv_block)
    cpl = both(cpl_block)

    solved = []
    for pieces in gathered:
        own, other = partials(*inv, pieces)
        other = partner(other)
        solved.append((own + other.astype(F32)).astype(BF16))

    out = ancestor_rhs
    for c, y in enumerate(solved):
        pieces = gather(y)
        sums = ()
        if c:
            sums = partials(*cpl, pieces[:-1], other_type=F32)
        first = len(pieces) - 1 if c else 0
        own, other = partials(*cpl, pieces[first:], first, sums)
        other = partner(other)
        total, *sent = split(dests[c], leaves, narrow, own, other)
        for d in range(1, leaves):
            got = lax.ppermute(sent[d - 1], "leaf", [(j ^ d, j) for j in dests[c]])
            total = total + got.astype(F32)
        out = out - total

    y_outer, y_inner = solved
    solution = jnp.concatenate([y_outer[:, :cut], y_inner, y_outer[:, cut:]], axis=1)
    return (solution[None], out)


def solution(mesh):
    return jax.shard_map(
        on_device,
        mesh=mesh,
        in_specs=(
            P("leaf", "row", None),
            P("leaf", "row", None),
            P("leaf", "row", None),
            P("leaf", "row"),
            P("row", "leaf"),
        ),
        out_specs=(P("leaf", "row", None), P("row", "leaf")),
        check_vma=False,
    )
```

time: 93.6 us -> 101 us (1.079); the launches traced: 92.1 us -> 101 us
  waiting for transfers between devices: 29.5 us -> 37.1 us
  Pallas kernels: 26.8 us -> 19.4 us
  starting transfers between devices: 32.8 us -> 38.9 us
  local copies, waits for them, and re-layouts: 0.79 us -> 2.6 us
    pallas_call x11, Pallas kernels: 26.8 us -> 19.4 us  [the longest x5 8.93 us: partials(): pl.pallas_call(functools.partial(partial_kernel, n, first, bool(sums)), o...]
    ppermute x6, waiting for transfers between devices: 3.1 us -> 7.57 us  [on_device(): got = lax.ppermute(sent[d - 1], 'leaf', [(j ^ d, j) for j in dests[c]])]
    ppermute x12, starting transfers between devices: 18.3 us -> 21.9 us  [gather(): pieces.append(lax.ppermute(pieces[p], 'row', pairs))]
    ppermute x12, waiting for transfers between devices: 26.4 us -> 29.5 us  [gather(): pieces.append(lax.ppermute(pieces[p], 'row', pairs))]
    ppermute x6, starting transfers between devices: 12.5 us -> 15.5 us  [on_device(): got = lax.ppermute(sent[d - 1], 'leaf', [(j ^ d, j) for j in dests[c]])]
    unnamed x6 -> x16, local copies, waits for them, and re-layouts: 0.01 us -> 2.52 us
  transfers between devices with their start and end apart: 24 -> 24, of which waited for: 9 -> 10; matrix products, arithmetic and copies ran while one was open for 1% -> 1% of each run, Pallas kernels for 24% -> 17%
where the time goes in v3:
time: 101 us
  starting transfers between devices  38.9 us (39%)
  waiting for transfers between devices  37.1 us (37%)
  Pallas kernels  19.4 us (19%)
  local copies, waits for them, and re-layouts  2.6 us (3%)
  other arithmetic  2.04 us (2%)
    ppermute x12, waiting for transfers between devices, gather(): pieces.append(lax.ppermute(pieces[p], 'row', pairs))  29.5 us
    ppermute x12, starting transfers between devices, gather(): pieces.append(lax.ppermute(pieces[p], 'row', pairs))  21.9 us
    ppermute x6, starting transfers between devices, on_device(): got = lax.ppermute(sent[d - 1], 'leaf', [(j ^ d, j) for j in dests[c]])  15.5 us
    pallas_call x5, Pallas kernels, partials(): pl.pallas_call(functools.partial(partial_kernel, n, first, bool(sums)), o...  8.93 us
    ppermute x6, waiting for transfers between devices, on_device(): got = lax.ppermute(sent[d - 1], 'leaf', [(j ^ d, j) for j in dests[c]])  7.57 us
    pallas_call x2, Pallas kernels, select_rows(): pl.pallas_call(functools.partial(select_kernel, masks, other), out_shape=...  7.09 us
    pallas_call x2, Pallas kernels, pick(): pl.pallas_call(functools.partial(pick_kernel, masks, other), out_shape=ja...  3.13 us
    unnamed x16, local copies, waits for them, and re-layouts  2.52 us
  transfers between devices with their start and end apart: 24, of which 10 were waited for; matrix products, arithmetic and copies ran while one was open for 1% of the time, Pallas kernels for 17%

profile of v3, /device:TPU:0, one launch (start us, length us, event | category | flops | bytes accessed | tf_op | source)
XLA Modules:
  0.0 101.0 jit_solution(8666023440836699288)
XLA Ops:
  0.6 0.0 slice-start
  0.7 0.0 slice-start.1
  0.7 2.6 %pick.3 = bf16[768,3072]{1,0:T(8,128)(2,1)S(1)} custom-call(bf16[768,6144]{1,0:T(8,128)(2,1)} %bitcast.5), custom_call_target="tpu_custom_call" | custom-call | tf_op jit(solution)/shard_map/pick/pallas_call | solution.py:65
  3.3 0.6 collective-permute-start
  3.8 1.0 %copy-done = bf16[1,512,6144]{2,1,0:T(8,128)(2,1)S(1)} copy-done((bf16[1,512,6144]{2,1,0:T(8,128)(2,1)S(1)}, bf16[1,512,6144]{2,1,0:T(8,128)(2,1)}, u32[]{:S(2)}) %copy-start) | copy-done | bytes 6291480
  4.9 1.5 %copy-done.1 = s32[1,512]{1,0:T(1,128)S(1)} copy-done((s32[1,512]{1,0:T(1,128)S(1)}, s32[1,512]{1,0:T(1,128)}, u32[]{:S(2)}) %copy-start.1) | copy-done | bytes 2072
  6.3 3.5 %select_rows.3 = bf16[512,3072]{1,0:T(8,128)(2,1)S(1)} custom-call(s32[1,512]{1,0:T(1,128)S(1)} %copy-done.1, bf16[512,6144]{1,0:T(8,128)(2,1)S(1)} %bitcast.9), custom_call_target="tpu_custom_call" | custom-call | tf_op jit(solution)/shard_map/select_rows/pallas_call | solution.py:100
  9.8 0.6 collective-permute-start.9
  10.4 2.5 %collective-permute-start.5 = (bf16[768,256]{1,0:T(8,128)(2,1)S(1)}, bf16[768,256]{1,0:T(8,128)(2,1)S(1)}, u32[]{:S(2)}, u32[]{:S(2)}) collective-permute-start(bf16[768,256]{1,0:T(8,128)(2,1)S(1)} %slice.23.refs_0_), channel_id=1, source_target_pairs={{0,2},{1,5},{2,0},{3,7},{4,6},{5,1},{6,4},{7,3},{8,10},{9,13},{10,... | collective-permute-start | bytes 1179656 | tf_op jit(solution)/shard_map/ppermute | solution.py:208
  13.0 0.1 collective-permute-start.1
  13.1 2.1 %collective-permute-start.6 = (bf16[768,256]{1,0:T(8,128)(2,1)S(1)}, bf16[768,256]{1,0:T(8,128)(2,1)S(1)}, u32[]{:S(2)}, u32[]{:S(2)}) collective-permute-start(bf16[768,256]{1,0:T(8,128)(2,1)S(1)} %slice.23.refs_0_), channel_id=1, source_target_pairs={{0,4},{1,3},{2,6},{3,1},{4,0},{5,7},{6,2},{7,5},{8,12},{9,11},{10,... | collective-permute-start | bytes 1179656 | tf_op jit(solution)/shard_map/ppermute | solution.py:208
  15.2 6.2 %collective-permute-done.5.refs_1_ = bf16[768,256]{1,0:T(8,128)(2,1)S(1)} collective-permute-done((bf16[768,256]{1,0:T(8,128)(2,1)S(1)}, bf16[768,256]{1,0:T(8,128)(2,1)S(1)}, u32[]{:S(2)}, u32[]{:S(2)}) %collective-permute-start.5) | collective-permute-done | bytes 393248 | tf_op jit(solution)/shard_map/ppermute | solution.py:208
  21.3 2.5 %collective-permute-start.7 = (bf16[768,256]{1,0:T(8,128)(2,1)S(1)}, bf16[768,256]{1,0:T(8,128)(2,1)S(1)}, u32[]{:S(2)}, u32[]{:S(2)}) collective-permute-start(bf16[768,256]{1,0:T(8,128)(2,1)S(1)} %collective-permute-done.5.refs_1_), channel_id=1, source_target_pairs={{0,4},{1,3},{2,6},{3,1},{4,0},{5,7},{6,2},{7,5},{8,12},{9,11},{10,... | collective-permute-start | bytes 1179656 | tf_op jit(solution)/shard_map/ppermute | solution.py:208
  23.9 5.9 %collective-permute-done.1.refs_1_ = bf16[768,256]{1,0:T(8,128)(2,1)S(1)} collective-permute-done((bf16[768,256]{1,0:T(8,128)(2,1)S(1)}, bf16[768,256]{1,0:T(8,128)(2,1)S(1)}, u32[]{:S(2)}, u32[]{:S(2)}) %collective-permute-start.1) | collective-permute-done | bytes 393248 | tf_op jit(solution)/shard_map/ppermute | solution.py:208
  29.8 2.5 %collective-permute-start.2 = (bf16[768,256]{1,0:T(8,128)(2,1)S(1)}, bf16[768,256]{1,0:T(8,128)(2,1)S(1)}, u32[]{:S(2)}, u32[]{:S(2)}) collective-permute-start(bf16[768,256]{1,0:T(8,128)(2,1)S(1)} %pad_maximum_fusion.refs_0_), channel_id=1, source_target_pairs={{0,4},{1,3},{2,6},{3,1},{4,0},{5,7},{6,2},{7,5},{8,12},{9,11},{10,... | collective-permute-start | bytes 1179656 | tf_op jit(solution)/shard_map/ppermute | solution.py:208
  32.3 0.0 collective-permute-done.6.refs_2_
  32.3 0.0 collective-permute-start.3
  32.3 0.5 pick.2.keep
  32.8 0.0 collective-permute-done.7.refs_3_
  32.9 0.0 collective-permute-done.swap
  32.9 2.6 %partials.6 = (f32[768,256]{1,0:T(8,128)S(1)}, bf16[768,256]{1,0:T(8,128)(2,1)S(1)}) custom-call(bf16[768,3072]{1,0:T(8,128)(2,1)S(1)} %pick.2.keep, bf16[768,3072]{1,0:T(8,128)(2,1)S(1)} %collective-permute-done.swap, bf16[768,256]{1,0:T(8,128)(2,1)S(1)} %slice.23.refs_0_, bf16[768,256]{1,0:T(8,128)(2,1)S(1)} %collective-permute-done.5.refs_1_, ...), custom_call_target="tpu_custom_call" | custom-call | tf_op jit(solution)/shard_map/partials/pallas_call | solution.py:131
  35.5 0.1 collective-permute-start.8
  35.6 2.5 %collective-permute-done.2.refs_2_ = bf16[768,256]{1,0:T(8,128)(2,1)S(1)} collective-permute-done((bf16[768,256]{1,0:T(8,128)(2,1)S(1)}, bf16[768,256]{1,0:T(8,128)(2,1)S(1)}, u32[]{:S(2)}, u32[]{:S(2)}) %collective-permute-start.2) | collective-permute-done | bytes 393248 | tf_op jit(solution)/shard_map/ppermute | solution.py:208
  38.0 4.2 %collective-permute-done.3.refs_3_ = bf16[768,256]{1,0:T(8,128)(2,1)S(1)} collective-permute-done((bf16[768,256]{1,0:T(8,128)(2,1)S(1)}, bf16[768,256]{1,0:T(8,128)(2,1)S(1)}, u32[]{:S(2)}, u32[]{:S(2)}) %collective-permute-start.3) | collective-permute-done | bytes 393248 | tf_op jit(solution)/shard_map/ppermute | solution.py:208
  42.3 2.6 %partials.5 = (f32[768,256]{1,0:T(8,128)S(1)}, bf16[768,256]{1,0:T(8,128)(2,1)S(1)}) custom-call(bf16[768,3072]{1,0:T(8,128)(2,1)S(1)} %pick.2.keep, bf16[768,3072]{1,0:T(8,128)(2,1)S(1)} %collective-permute-done.swap, bf16[768,256]{1,0:T(8,128)(2,1)S(1)} %pad_maximum_fusion.refs_0_, bf16[768,256]{1,0:T(8,128)(2,1)S(1)} %collective-permute-done.1.refs_1_, ...), custom_call_target="tpu_custom_call" | custom-call | tf_op jit(solution)/shard_map/partials/pallas_call | solution.py:131
  44.9 0.0 copy-start.2
  44.9 0.1 collective-permute-start.4
  44.9 0.0 collective-permute-done.8
  45.0 0.1 add_convert_fusion.refs_0_
  45.1 2.0 %collective-permute-start.17 = (bf16[768,256]{1,0:T(8,128)(2,1)S(1)}, bf16[768,256]{1,0:T(8,128)(2,1)S(1)}, u32[]{:S(2)}, u32[]{:S(2)}) collective-permute-start(bf16[768,256]{1,0:T(8,128)(2,1)S(1)} %add_convert_fusion.refs_0_), channel_id=1, source_target_pairs={{0,2},{1,5},{2,0},{3,7},{4,6},{5,1},{6,4},{7,3},{8,10},{9,13},{10,... | collective-permute-start | bytes 1179656 | tf_op jit(solution)/shard_map/ppermute | solution.py:208
  47.1 0.0 collective-permute-done.4
  47.1 0.1 add_convert_fusion.1.refs_0_
  47.2 1.6 %collective-permute-start.10 = (bf16[768,256]{1,0:T(8,128)(2,1)S(1)}, bf16[768,256]{1,0:T(8,128)(2,1)S(1)}, u32[]{:S(2)}, u32[]{:S(2)}) collective-permute-start(bf16[768,256]{1,0:T(8,128)(2,1)S(1)} %add_convert_fusion.1.refs_0_), channel_id=1, source_target_pairs={{0,2},{1,5},{2,0},{3,7},{4,6},{5,1},{6,4},{7,3},{8,10},{9,13},{10,... | collective-permute-start | bytes 1179656 | tf_op jit(solution)/shard_map/ppermute | solution.py:208
  48.8 1.5 %collective-permute-start.19 = (bf16[768,256]{1,0:T(8,128)(2,1)S(1)}, bf16[768,256]{1,0:T(8,128)(2,1)S(1)}, u32[]{:S(2)}, u32[]{:S(2)}) collective-permute-start(bf16[768,256]{1,0:T(8,128)(2,1)S(1)} %add_convert_fusion.refs_0_), channel_id=1, source_target_pairs={{0,4},{1,3},{2,6},{3,1},{4,0},{5,7},{6,2},{7,5},{8,12},{9,11},{10,... | collective-permute-start | bytes 1179656 | tf_op jit(solution)/shard_map/ppermute | solution.py:208
  50.3 4.2 %collective-permute-done.17.refs_1_ = bf16[768,256]{1,0:T(8,128)(2,1)S(1)} collective-permute-done((bf16[768,256]{1,0:T(8,128)(2,1)S(1)}, bf16[768,256]{1,0:T(8,128)(2,1)S(1)}, u32[]{:S(2)}, u32[]{:S(2)}) %collective-permute-start.17) | collective-permute-done | bytes 393248 | tf_op jit(solution)/shard_map/ppermute | solution.py:208
  54.5 3.5 %collective-permute-start.18 = (bf16[768,256]{1,0:T(8,128)(2,1)S(1)}, bf16[768,256]{1,0:T(8,128)(2,1)S(1)}, u32[]{:S(2)}, u32[]{:S(2)}) collective-permute-start(bf16[768,256]{1,0:T(8,128)(2,1)S(1)} %collective-permute-done.17.refs_1_), channel_id=1, source_target_pairs={{0,4},{1,3},{2,6},{3,1},{4,0},{5,7},{6,2},{7,5},{8,12},{9,11},{10,... | collective-permute-start | bytes 1179656 | tf_op jit(solution)/shard_map/ppermute | solution.py:208
  58.0 0.0 collective-permute-start.11
  58.0 4.9 %collective-permute-done.10.refs_1_ = bf16[768,256]{1,0:T(8,128)(2,1)S(1)} collective-permute-done((bf16[768,256]{1,0:T(8,128)(2,1)S(1)}, bf16[768,256]{1,0:T(8,128)(2,1)S(1)}, u32[]{:S(2)}, u32[]{:S(2)}) %collective-permute-start.10) | collective-permute-done | bytes 393248 | tf_op jit(solution)/shard_map/ppermute | solution.py:208
  62.9 3.5 %collective-permute-start.12 = (bf16[768,256]{1,0:T(8,128)(2,1)S(1)}, bf16[768,256]{1,0:T(8,128)(2,1)S(1)}, u32[]{:S(2)}, u32[]{:S(2)}) collective-permute-start(bf16[768,256]{1,0:T(8,128)(2,1)S(1)} %collective-permute-done.10.refs_1_), channel_id=1, source_target_pairs={{0,4},{1,3},{2,6},{3,1},{4,0},{5,7},{6,2},{7,5},{8,12},{9,11},{10,... | collective-permute-start | bytes 1179656 | tf_op jit(solution)/shard_map/ppermute | solution.py:208
  66.4 3.6 %select_rows.2.keep = bf16[512,3072]{1,0:T(8,128)(2,1)S(1)} custom-call(s32[1,512]{1,0:T(1,128)S(1)} %copy-done.2, bf16[512,6144]{1,0:T(8,128)(2,1)S(1)} %bitcast.10), custom_call_target="tpu_custom_call" | custom-call | tf_op jit(solution)/shard_map/select_rows/pallas_call | solution.py:100
  70.0 0.0 collective-permute-done.9.swap
  70.0 0.0 collective-permute-done.19.refs_2_
  70.1 1.4 %partials.8 = (f32[512,256]{1,0:T(8,128)S(1)}, f32[512,256]{1,0:T(8,128)S(1)}) custom-call(bf16[512,3072]{1,0:T(8,128)(2,1)S(1)} %select_rows.2.keep, bf16[512,3072]{1,0:T(8,128)(2,1)S(1)} %collective-permute-done.9.swap, bf16[768,256]{1,0:T(8,128)(2,1)S(1)} %add_convert_fusion.refs_0_, bf16[768,256]{1,0:T(8,128)(2,1)S(1)} %collective-permute-done.17.refs_1_, ...), custom_call_target="tpu_custom_call" | custom-call | tf_op jit(solution)/shard_map/partials/pallas_call | solution.py:131
  71.4 0.0 collective-permute-done.18.refs_0_
  71.4 0.6 partials.9
  72.0 0.1 collective-permute-start.20
  72.1 0.0 collective-permute-done.11.refs_2_
  72.1 1.6 %collective-permute-done.12.refs_3_ = bf16[768,256]{1,0:T(8,128)(2,1)S(1)} collective-permute-done((bf16[768,256]{1,0:T(8,128)(2,1)S(1)}, bf16[768,256]{1,0:T(8,128)(2,1)S(1)}, u32[]{:S(2)}, u32[]{:S(2)}) %collective-permute-start.12) | collective-permute-done | bytes 393248 | tf_op jit(solution)/shard_map/ppermute | solution.py:208
  73.8 1.8 %partials.7 = (f32[512,256]{1,0:T(8,128)S(1)}, bf16[512,256]{1,0:T(8,128)(2,1)S(1)}) custom-call(bf16[512,3072]{1,0:T(8,128)(2,1)S(1)} %select_rows.2.keep, bf16[512,3072]{1,0:T(8,128)(2,1)S(1)} %collective-permute-done.9.swap, bf16[768,256]{1,0:T(8,128)(2,1)S(1)} %add_convert_fusion.1.refs_0_, bf16[768,256]{1,0:T(8,128)(2,1)S(1)} %collective-permute-done.10.refs_1_, ...), custom_call_target="tpu_custom_call" | custom-call | tf_op jit(solution)/shard_map/partials/pallas_call | solution.py:131
  75.6 0.0 copy-start.4
  75.6 0.2 collective-permute-start.13
  75.7 0.1 split.3
  75.9 0.7 collective-permute-start.23
  76.6 6.6 %collective-permute-start.22 = (bf16[512,128]{1,0:T(8,128)(2,1)S(1)}, bf16[512,128]{1,0:T(8,128)(2,1)S(1)}, u32[]{:S(2)}, u32[]{:S(2)}) collective-permute-start(bf16[512,128]{1,0:T(8,128)(2,1)S(1)} %get-tuple-element.36), channel_id=1, source_target_pairs={{24,8},{0,16},{25,9},{1,17},{26,10},{2,18},{27,11},{3,19},{28,12},... | collective-permute-start | bytes 393224 | tf_op jit(solution)/shard_map/ppermute | solution.py:248
  83.2 1.4 %collective-permute-start.21 = (bf16[512,128]{1,0:T(8,128)(2,1)S(1)}, bf16[512,128]{1,0:T(8,128)(2,1)S(1)}, u32[]{:S(2)}, u32[]{:S(2)}) collective-permute-start(bf16[512,128]{1,0:T(8,128)(2,1)S(1)} %get-tuple-element.35), channel_id=1, source_target_pairs={{0,8},{24,16},{1,9},{25,17},{2,10},{26,18},{3,11},{27,19},{4,12},{... | collective-permute-start | bytes 393224 | tf_op jit(solution)/shard_map/ppermute | solution.py:248
  84.6 0.1 split.2
  84.7 4.3 %collective-permute-start.16 = (bf16[512,128]{1,0:T(8,128)(2,1)S(1)}, bf16[512,128]{1,0:T(8,128)(2,1)S(1)}, u32[]{:S(2)}, u32[]{:S(2)}) collective-permute-start(bf16[512,128]{1,0:T(8,128)(2,1)S(1)} %get-tuple-element.29), channel_id=1, source_target_pairs={{24,0},{0,24},{25,1},{1,25},{26,2},{2,26},{27,3},{3,27},{28,4},{4,... | collective-permute-start | bytes 393224 | tf_op jit(solution)/shard_map/ppermute | solution.py:248
  89.0 1.3 %collective-permute-start.15 = (bf16[512,128]{1,0:T(8,128)(2,1)S(1)}, bf16[512,128]{1,0:T(8,128)(2,1)S(1)}, u32[]{:S(2)}, u32[]{:S(2)}) collective-permute-start(bf16[512,128]{1,0:T(8,128)(2,1)S(1)} %get-tuple-element.28), channel_id=1, source_target_pairs={{16,0},{8,24},{17,1},{9,25},{18,2},{10,26},{19,3},{11,27},{20,4},{... | collective-permute-start | bytes 393224 | tf_op jit(solution)/shard_map/ppermute | solution.py:248
  90.3 1.3 %collective-permute-start.14 = (bf16[512,128]{1,0:T(8,128)(2,1)S(1)}, bf16[512,128]{1,0:T(8,128)(2,1)S(1)}, u32[]{:S(2)}, u32[]{:S(2)}) collective-permute-start(bf16[512,128]{1,0:T(8,128)(2,1)S(1)} %get-tuple-element.27), channel_id=1, source_target_pairs={{8,0},{16,24},{9,1},{17,25},{10,2},{18,26},{11,3},{19,27},{12,4},{... | collective-permute-start | bytes 393224 | tf_op jit(solution)/shard_map/ppermute | solution.py:248
  91.6 1.0 maximum_bitcast_fusion
  92.6 2.1 %collective-permute-done.16 = bf16[512,128]{1,0:T(8,128)(2,1)S(1)} collective-permute-done((bf16[512,128]{1,0:T(8,128)(2,1)S(1)}, bf16[512,128]{1,0:T(8,128)(2,1)S(1)}, u32[]{:S(2)}, u32[]{:S(2)}) %collective-permute-start.16) | collective-permute-done | bytes 131104 | tf_op jit(solution)/shard_map/ppermute | solution.py:248
  94.7 2.8 %collective-permute-done.15 = bf16[512,128]{1,0:T(8,128)(2,1)S(1)} collective-permute-done((bf16[512,128]{1,0:T(8,128)(2,1)S(1)}, bf16[512,128]{1,0:T(8,128)(2,1)S(1)}, u32[]{:S(2)}, u32[]{:S(2)}) %collective-permute-start.15) | collective-permute-done | bytes 131104 | tf_op jit(solution)/shard_map/ppermute | solution.py:248
  97.4 2.7 %collective-permute-done.14 = bf16[512,128]{1,0:T(8,128)(2,1)S(1)} collective-permute-done((bf16[512,128]{1,0:T(8,128)(2,1)S(1)}, bf16[512,128]{1,0:T(8,128)(2,1)S(1)}, u32[]{:S(2)}, u32[]{:S(2)}) %collective-permute-start.14) | collective-permute-done | bytes 131104 | tf_op jit(solution)/shard_map/ppermute | solution.py:248
  100.2 0.8 add_subtract_fusion
  (20 shorter events, 0.2 us)
Async XLA Ops:
  0.6 4.2 %copy-start = (bf16[1,512,6144]{2,1,0:T(8,128)(2,1)S(1)}, bf16[1,512,6144]{2,1,0:T(8,128)(2,1)}, u32[]{:S(2)}) copy-start(bf16[1,512,6144]{2,1,0:T(8,128)(2,1)} %param.7) | copy-start | bytes 18874372
  0.6 31.7 %slice-start = ((s8[9437184]{0:T(1024)(128)(4,1)}), s8[4194304]{0:T(1024)(128)(4,1)S(1)}, s32[]{:S(2)}) async-start(s8[9437184]{0:T(1024)(128)(4,1)} %bitcast.6), calls=%async_computation | async-start | bytes 8388608
  0.7 31.7 %slice-start.1 = ((s8[9437184]{0:T(1024)(128)(4,1)}), s8[4194304]{0:T(1024)(128)(4,1)S(1)}, s32[]{:S(2)}) async-start(s8[9437184]{0:T(1024)(128)(4,1)} %bitcast.6), calls=%async_computation.1 | async-start | bytes 8388608
  3.3 29.6 %collective-permute-start = (bf16[768,3072]{1,0:T(8,128)(2,1)S(1)}, bf16[768,3072]{1,0:T(8,128)(2,1)S(1)}, u32[]{:S(2)}, u32[]{:S(2)}) collective-permute-start(bf16[768,3072]{1,0:T(8,128)(2,1)S(1)} %pick.3), channel_id=1, source_target_pairs={{0,1},{1,0},{2,3},{3,2},{4,5},{5,4},{6,7},{7,6},{8,9},{9,8},{10,11... | collective-permute-start | bytes 14155784 | tf_op jit(solution)/shard_map/ppermute | solution.py:201
  4.9 1.5 %copy-start.1 = (s32[1,512]{1,0:T(1,128)S(1)}, s32[1,512]{1,0:T(1,128)}, u32[]{:S(2)}) copy-start(s32[1,512]{1,0:T(1,128)} %places.3) | copy-start | bytes 6148
  6.3 4.0 %copy-start.3 = (bf16[1,768,512]{2,1,0:T(8,128)(2,1)S(1)}, bf16[1,768,512]{2,1,0:T(8,128)(2,1)}, u32[]{:S(2)}) copy-start(bf16[1,768,512]{2,1,0:T(8,128)(2,1)} %param.6) | copy-start | bytes 2359300
  6.3 26.0 %slice-start.2 = ((s8[9437184]{0:T(1024)(128)(4,1)}), s8[1048576]{0:T(1024)(128)(4,1)S(1)}, s32[]{:S(2)}) async-start(s8[9437184]{0:T(1024)(128)(4,1)} %bitcast.6), calls=%async_computation.2 | async-start | bytes 2097152
  9.8 60.2 %collective-permute-start.9 = (bf16[512,3072]{1,0:T(8,128)(2,1)S(1)}, bf16[512,3072]{1,0:T(8,128)(2,1)S(1)}, u32[]{:S(2)}, u32[]{:S(2)}) collective-permute-start(bf16[512,3072]{1,0:T(8,128)(2,1)S(1)} %select_rows.3), channel_id=1, source_target_pairs={{0,1},{1,0},{2,3},{3,2},{4,5},{5,4},{6,7},{7,6},{8,9},{9,8},{10,11... | collective-permute-start | bytes 9437192 | tf_op jit(solution)/shard_map/ppermute | solution.py:201
  10.4 11.0 %collective-permute-start.5 = (bf16[768,256]{1,0:T(8,128)(2,1)S(1)}, bf16[768,256]{1,0:T(8,128)(2,1)S(1)}, u32[]{:S(2)}, u32[]{:S(2)}) collective-permute-start(bf16[768,256]{1,0:T(8,128)(2,1)S(1)} %slice.23.refs_0_), channel_id=1, source_target_pairs={{0,2},{1,5},{2,0},{3,7},{4,6},{5,1},{6,4},{7,3},{8,10},{9,13},{10,... | collective-permute-start | bytes 1179656 | tf_op jit(solution)/shard_map/ppermute | solution.py:208
  13.0 16.8 %collective-permute-start.1 = (bf16[768,256]{1,0:T(8,128)(2,1)S(1)}, bf16[768,256]{1,0:T(8,128)(2,1)S(1)}, u32[]{:S(2)}, u32[]{:S(2)}) collective-permute-start(bf16[768,256]{1,0:T(8,128)(2,1)S(1)} %pad_maximum_fusion.refs_0_), channel_id=1, source_target_pairs={{0,2},{1,5},{2,0},{3,7},{4,6},{5,1},{6,4},{7,3},{8,10},{9,13},{10,... | collective-permute-start | bytes 1179656 | tf_op jit(solution)/shard_map/ppermute | solution.py:208
  13.1 19.2 %collective-permute-start.6 = (bf16[768,256]{1,0:T(8,128)(2,1)S(1)}, bf16[768,256]{1,0:T(8,128)(2,1)S(1)}, u32[]{:S(2)}, u32[]{:S(2)}) collective-permute-start(bf16[768,256]{1,0:T(8,128)(2,1)S(1)} %slice.23.refs_0_), channel_id=1, source_target_pairs={{0,4},{1,3},{2,6},{3,1},{4,0},{5,7},{6,2},{7,5},{8,12},{9,11},{10,... | collective-permute-start | bytes 1179656 | tf_op jit(solution)/shard_map/ppermute | solution.py:208
  21.3 11.5 %collective-permute-start.7 = (bf16[768,256]{1,0:T(8,128)(2,1)S(1)}, bf16[768,256]{1,0:T(8,128)(2,1)S(1)}, u32[]{:S(2)}, u32[]{:S(2)}) collective-permute-start(bf16[768,256]{1,0:T(8,128)(2,1)S(1)} %collective-permute-done.5.refs_1_), channel_id=1, source_target_pairs={{0,4},{1,3},{2,6},{3,1},{4,0},{5,7},{6,2},{7,5},{8,12},{9,11},{10,... | collective-permute-start | bytes 1179656 | tf_op jit(solution)/shard_map/ppermute | solution.py:208
  29.8 8.3 %collective-permute-start.2 = (bf16[768,256]{1,0:T(8,128)(2,1)S(1)}, bf16[768,256]{1,0:T(8,128)(2,1)S(1)}, u32[]{:S(2)}, u32[]{:S(2)}) collective-permute-start(bf16[768,256]{1,0:T(8,128)(2,1)S(1)} %pad_maximum_fusion.refs_0_), channel_id=1, source_target_pairs={{0,4},{1,3},{2,6},{3,1},{4,0},{5,7},{6,2},{7,5},{8,12},{9,11},{10,... | collective-permute-start | bytes 1179656 | tf_op jit(solution)/shard_map/ppermute | solution.py:208
  32.3 10.0 %collective-permute-start.3 = (bf16[768,256]{1,0:T(8,128)(2,1)S(1)}, bf16[768,256]{1,0:T(8,128)(2,1)S(1)}, u32[]{:S(2)}, u32[]{:S(2)}) collective-permute-start(bf16[768,256]{1,0:T(8,128)(2,1)S(1)} %collective-permute-done.1.refs_1_), channel_id=1, source_target_pairs={{0,4},{1,3},{2,6},{3,1},{4,0},{5,7},{6,2},{7,5},{8,12},{9,11},{10,... | collective-permute-start | bytes 1179656 | tf_op jit(solution)/shard_map/ppermute | solution.py:208
  35.5 9.5 %collective-permute-start.8 = (bf16[768,256]{1,0:T(8,128)(2,1)S(1)}, bf16[768,256]{1,0:T(8,128)(2,1)S(1)}, u32[]{:S(2)}, u32[]{:S(2)}) collective-permute-start(bf16[768,256]{1,0:T(8,128)(2,1)S(1)} %get-tuple-element.23), channel_id=1, source_target_pairs={{0,1},{1,0},{2,3},{3,2},{4,5},{5,4},{6,7},{7,6},{8,9},{9,8},{10,11... | collective-permute-start | bytes 1179656 | tf_op jit(solution)/shard_map/ppermute | solution.py:201
  44.9 21.5 %copy-start.2 = (s32[1,512]{1,0:T(1,128)S(1)}, s32[1,512]{1,0:T(1,128)}, u32[]{:S(2)}) copy-start(s32[1,512]{1,0:T(1,128)} %places.3) | copy-start | bytes 6148
  44.9 2.2 %collective-permute-start.4 = (bf16[768,256]{1,0:T(8,128)(2,1)S(1)}, bf16[768,256]{1,0:T(8,128)(2,1)S(1)}, u32[]{:S(2)}, u32[]{:S(2)}) collective-permute-start(bf16[768,256]{1,0:T(8,128)(2,1)S(1)} %get-tuple-element.21), channel_id=1, source_target_pairs={{0,1},{1,0},{2,3},{3,2},{4,5},{5,4},{6,7},{7,6},{8,9},{9,8},{10,11... | collective-permute-start | bytes 1179656 | tf_op jit(solution)/shard_map/ppermute | solution.py:201
  45.1 9.4 %collective-permute-start.17 = (bf16[768,256]{1,0:T(8,128)(2,1)S(1)}, bf16[768,256]{1,0:T(8,128)(2,1)S(1)}, u32[]{:S(2)}, u32[]{:S(2)}) collective-permute-start(bf16[768,256]{1,0:T(8,128)(2,1)S(1)} %add_convert_fusion.refs_0_), channel_id=1, source_target_pairs={{0,2},{1,5},{2,0},{3,7},{4,6},{5,1},{6,4},{7,3},{8,10},{9,13},{10,... | collective-permute-start | bytes 1179656 | tf_op jit(solution)/shard_map/ppermute | solution.py:208
  47.2 15.7 %collective-permute-start.10 = (bf16[768,256]{1,0:T(8,128)(2,1)S(1)}, bf16[768,256]{1,0:T(8,128)(2,1)S(1)}, u32[]{:S(2)}, u32[]{:S(2)}) collective-permute-start(bf16[768,256]{1,0:T(8,128)(2,1)S(1)} %add_convert_fusion.1.refs_0_), channel_id=1, source_target_pairs={{0,2},{1,5},{2,0},{3,7},{4,6},{5,1},{6,4},{7,3},{8,10},{9,13},{10,... | collective-permute-start | bytes 1179656 | tf_op jit(solution)/shard_map/ppermute | solution.py:208
  48.8 21.3 %collective-permute-start.19 = (bf16[768,256]{1,0:T(8,128)(2,1)S(1)}, bf16[768,256]{1,0:T(8,128)(2,1)S(1)}, u32[]{:S(2)}, u32[]{:S(2)}) collective-permute-start(bf16[768,256]{1,0:T(8,128)(2,1)S(1)} %add_convert_fusion.refs_0_), channel_id=1, source_target_pairs={{0,4},{1,3},{2,6},{3,1},{4,0},{5,7},{6,2},{7,5},{8,12},{9,11},{10,... | collective-permute-start | bytes 1179656 | tf_op jit(solution)/shard_map/ppermute | solution.py:208
  54.5 17.0 %collective-permute-start.18 = (bf16[768,256]{1,0:T(8,128)(2,1)S(1)}, bf16[768,256]{1,0:T(8,128)(2,1)S(1)}, u32[]{:S(2)}, u32[]{:S(2)}) collective-permute-start(bf16[768,256]{1,0:T(8,128)(2,1)S(1)} %collective-permute-done.17.refs_1_), channel_id=1, source_target_pairs={{0,4},{1,3},{2,6},{3,1},{4,0},{5,7},{6,2},{7,5},{8,12},{9,11},{10,... | collective-permute-start | bytes 1179656 | tf_op jit(solution)/shard_map/ppermute | solution.py:208
  58.0 14.1 %collective-permute-start.11 = (bf16[768,256]{1,0:T(8,128)(2,1)S(1)}, bf16[768,256]{1,0:T(8,128)(2,1)S(1)}, u32[]{:S(2)}, u32[]{:S(2)}) collective-permute-start(bf16[768,256]{1,0:T(8,128)(2,1)S(1)} %add_convert_fusion.1.refs_0_), channel_id=1, source_target_pairs={{0,4},{1,3},{2,6},{3,1},{4,0},{5,7},{6,2},{7,5},{8,12},{9,11},{10,... | collective-permute-start | bytes 1179656 | tf_op jit(solution)/shard_map/ppermute | solution.py:208
  62.9 10.9 %collective-permute-start.12 = (bf16[768,256]{1,0:T(8,128)(2,1)S(1)}, bf16[768,256]{1,0:T(8,128)(2,1)S(1)}, u32[]{:S(2)}, u32[]{:S(2)}) collective-permute-start(bf16[768,256]{1,0:T(8,128)(2,1)S(1)} %collective-permute-done.10.refs_1_), channel_id=1, source_target_pairs={{0,4},{1,3},{2,6},{3,1},{4,0},{5,7},{6,2},{7,5},{8,12},{9,11},{10,... | collective-permute-start | bytes 1179656 | tf_op jit(solution)/shard_map/ppermute | solution.py:208
  72.0 3.7 %collective-permute-start.20 = (bf16[512,256]{1,0:T(8,128)(2,1)S(1)}, bf16[512,256]{1,0:T(8,128)(2,1)S(1)}, u32[]{:S(2)}, u32[]{:S(2)}) collective-permute-start(bf16[512,256]{1,0:T(8,128)(2,1)S(1)} %get-tuple-element.33), channel_id=1, source_target_pairs={{0,1},{1,0},{2,3},{3,2},{4,5},{5,4},{6,7},{7,6},{8,9},{9,8},{10,11... | collective-permute-start | bytes 786440 | tf_op jit(solution)/shard_map/ppermute | solution.py:201
  75.6 24.6 %copy-start.4 = (f32[512,128]{1,0:T(8,128)S(1)}, f32[512,128]{1,0:T(8,128)}, u32[]{:S(2)}) copy-start(f32[512,128]{1,0:T(8,128)} %param.9) | copy-start | bytes 786436
  75.6 9.0 %collective-permute-start.13 = (bf16[512,256]{1,0:T(8,128)(2,1)S(1)}, bf16[512,256]{1,0:T(8,128)(2,1)S(1)}, u32[]{:S(2)}, u32[]{:S(2)}) collective-permute-start(bf16[512,256]{1,0:T(8,128)(2,1)S(1)} %get-tuple-element.25), channel_id=1, source_target_pairs={{0,1},{1,0},{2,3},{3,2},{4,5},{5,4},{6,7},{7,6},{8,9},{9,8},{10,11... | collective-permute-start | bytes 786440 | tf_op jit(solution)/shard_map/ppermute | solution.py:201
  75.9 14.4 %collective-permute-start.23 = (bf16[512,128]{1,0:T(8,128)(2,1)S(1)}, bf16[512,128]{1,0:T(8,128)(2,1)S(1)}, u32[]{:S(2)}, u32[]{:S(2)}) collective-permute-start(bf16[512,128]{1,0:T(8,128)(2,1)S(1)} %get-tuple-element.37), channel_id=1, source_target_pairs={{16,8},{8,16},{17,9},{9,17},{18,10},{10,18},{19,11},{11,19},{20,12... | collective-permute-start | bytes 393224 | tf_op jit(solution)/shard_map/ppermute | solution.py:248
  76.6 16.0 %collective-permute-start.22 = (bf16[512,128]{1,0:T(8,128)(2,1)S(1)}, bf16[512,128]{1,0:T(8,128)(2,1)S(1)}, u32[]{:S(2)}, u32[]{:S(2)}) collective-permute-start(bf16[512,128]{1,0:T(8,128)(2,1)S(1)} %get-tuple-element.36), channel_id=1, source_target_pairs={{24,8},{0,16},{25,9},{1,17},{26,10},{2,18},{27,11},{3,19},{28,12},... | collective-permute-start | bytes 393224 | tf_op jit(solution)/shard_map/ppermute | solution.py:248
  83.2 9.4 %collective-permute-start.21 = (bf16[512,128]{1,0:T(8,128)(2,1)S(1)}, bf16[512,128]{1,0:T(8,128)(2,1)S(1)}, u32[]{:S(2)}, u32[]{:S(2)}) collective-permute-start(bf16[512,128]{1,0:T(8,128)(2,1)S(1)} %get-tuple-element.35), channel_id=1, source_target_pairs={{0,8},{24,16},{1,9},{25,17},{2,10},{26,18},{3,11},{27,19},{4,12},{... | collective-permute-start | bytes 393224 | tf_op jit(solution)/shard_map/ppermute | solution.py:248
  84.7 9.9 %collective-permute-start.16 = (bf16[512,128]{1,0:T(8,128)(2,1)S(1)}, bf16[512,128]{1,0:T(8,128)(2,1)S(1)}, u32[]{:S(2)}, u32[]{:S(2)}) collective-permute-start(bf16[512,128]{1,0:T(8,128)(2,1)S(1)} %get-tuple-element.29), channel_id=1, source_target_pairs={{24,0},{0,24},{25,1},{1,25},{26,2},{2,26},{27,3},{3,27},{28,4},{4,... | collective-permute-start | bytes 393224 | tf_op jit(solution)/shard_map/ppermute | solution.py:248
  89.0 8.4 %collective-permute-start.15 = (bf16[512,128]{1,0:T(8,128)(2,1)S(1)}, bf16[512,128]{1,0:T(8,128)(2,1)S(1)}, u32[]{:S(2)}, u32[]{:S(2)}) collective-permute-start(bf16[512,128]{1,0:T(8,128)(2,1)S(1)} %get-tuple-element.28), channel_id=1, source_target_pairs={{16,0},{8,24},{17,1},{9,25},{18,2},{10,26},{19,3},{11,27},{20,4},{... | collective-permute-start | bytes 393224 | tf_op jit(solution)/shard_map/ppermute | solution.py:248
  90.3 9.8 %collective-permute-start.14 = (bf16[512,128]{1,0:T(8,128)(2,1)S(1)}, bf16[512,128]{1,0:T(8,128)(2,1)S(1)}, u32[]{:S(2)}, u32[]{:S(2)}) collective-permute-start(bf16[512,128]{1,0:T(8,128)(2,1)S(1)} %get-tuple-element.27), channel_id=1, source_target_pairs={{8,0},{16,24},{9,1},{17,25},{10,2},{18,26},{11,3},{19,27},{12,4},{... | collective-permute-start | bytes 393224 | tf_op jit(solution)/shard_map/ppermute | solution.py:248

commit v4 on v3

--- a/solution.py
+++ b/solution.py
@@ -142,37 +142,92 @@
     )(keep, swap, *pieces, *sums)
 
 
-def place_of(group, leaf):
-    return sum(jnp.where(leaf == j, i, 0) for i, j in enumerate(group))
-
-
-def member(group, leaf):
-    return sum(jnp.where(leaf == j, 1.0, 0.0) for j in group)
-
-
-def split_kernel(group, narrow, own, other, total, *pieces):
+def swap_halves(x):
+    return pltpu.roll(x, x.shape[1] // 2, 1)
+
+
+def low_lanes(shape):
+    return lax.broadcasted_iota(jnp.int32, shape, 1) < shape[1] // 2
+
+
+def tile(t):
+    return slice(t * 128, (t + 1) * 128)
+
+
+def chunk_kernel(c, x, out):
+    for t in range(out.shape[1] // 128):
+        a, b = x[:, tile(2 * t)].astype(F32), x[:, tile(2 * t + 1)].astype(F32)
+        low = low_lanes(a.shape)
+        both = jnp.where(low, swap_halves(a), b) if c else jnp.where(low, a, swap_halves(b))
+        out[:, tile(t)] = both.astype(out.dtype)
+
+
+def chunk(x, c, leaves):
+    rows, width = x.shape
+    half = width // leaves // 2
+    if half != 64:
+        return x.reshape(rows, leaves, 2, half)[:, :, c].reshape(rows, width // 2)
+    return pl.pallas_call(
+        functools.partial(chunk_kernel, c),
+        out_shape=jax.ShapeDtypeStruct((rows, width // 2), x.dtype),
+        in_specs=[VMEM],
+        out_specs=VMEM,
+        compiler_params=pltpu.CompilerParams(vmem_limit_bytes=4 << 20),
+        name="chunk",
+    )(x)
+
+
+def join_kernel(x, y, out):
+    for t in range(x.shape[1] // 128):
+        a, b = x[:, tile(t)].astype(F32), y[:, tile(t)].astype(F32)
+        low = low_lanes(a.shape)
+        out[:, tile(2 * t)] = jnp.where(low, a, swap_halves(b)).astype(out.dtype)
+        out[:, tile(2 * t + 1)] = jnp.where(low, swap_halves(a), b).astype(out.dtype)
+
+
+def join(x, y, leaves):
+    rows, width = x.shape
+    half = width // leaves
+    if half != 64:
+        parts = [p.reshape(rows, leaves, 1, half) for p in (x, y)]
+        return jnp.concatenate(parts, axis=2).reshape(rows, 2 * width)
+    return pl.pallas_call(
+        join_kernel,
+        out_shape=jax.ShapeDtypeStruct((rows, 2 * width), x.dtype),
+        in_specs=[VMEM, VMEM],
+        out_specs=VMEM,
+        compiler_params=pltpu.CompilerParams(vmem_limit_bytes=6 << 20),
+        name="join",
+    )(x, y)
+
+
+def split_kernel(own, other, *pieces):
+    rows = own.shape[0] // 2
     leaf = lax.axis_index("leaf")
-    for d in range(len(pieces) + 1):
-        start = pl.multiple_of(place_of(group, leaf ^ d) * narrow, 128)
-        piece = own[:, pl.ds(start, narrow)] + other[:, pl.ds(start, narrow)].astype(F32)
-        if d == 0:
-            total[...] = jnp.where(member(group, leaf) > 0, piece, 0.0)
-        else:
-            pieces[d - 1][...] = piece.astype(BF16)
-
-
-def split(group, leaves, narrow, own, other):
-    rows = own.shape[0]
-    if narrow % 128:
+    for d, out in enumerate(pieces):
+        target = leaf ^ d
+        columns = pl.ds(pl.multiple_of((target >> 1) * 128, 128), 128)
+        both = own[:, columns] + other[:, columns].astype(F32)
+        top, bottom = both[:rows], both[rows:]
+        low = low_lanes(top.shape)
+        even = jnp.where(low, top, swap_halves(bottom))
+        odd = jnp.where(low, swap_halves(top), bottom)
+        out[...] = jnp.where((target & 1) == 1, odd, even).astype(out.dtype)
+
+
+def split(own, other, leaves):
+    rows, width = own.shape
+    half = width // leaves
+    if half != 64:
         leaf = lax.axis_index("leaf")
         q = own + other.astype(F32)
-        blocks = [column_block(q, place_of(group, leaf ^ d), narrow) for d in range(leaves)]
-        total = jnp.where(member(group, leaf) > 0, blocks[0], 0.0)
-        return total, *[block.astype(BF16) for block in blocks[1:]]
-    return pl.pallas_call(
-        functools.partial(split_kernel, group, narrow),
-        out_shape=[jax.ShapeDtypeStruct((rows, narrow), F32)]
-        + [jax.ShapeDtypeStruct((rows, narrow), BF16)] * (leaves - 1),
+        blocks = [column_block(q, leaf ^ d, half) for d in range(leaves)]
+        return blocks[0], *[block.astype(BF16) for block in blocks[1:]]
+    return pl.pallas_call(
+        split_kernel,
+        out_shape=[
+            jax.ShapeDtypeStruct((rows // 2, 128), BF16 if d else F32) for d in range(leaves)
+        ],
         in_specs=[VMEM, VMEM],
         out_specs=[VMEM] * leaves,
         compiler_params=pltpu.CompilerParams(vmem_limit_bytes=6 << 20),
@@ -180,22 +235,40 @@
     )(own, other)
 
 
+def finish_kernel(n, rhs, *refs):
+    groups, out = (refs[:n], refs[n : 2 * n]), refs[2 * n]
+    first, second = (sum((g[...].astype(F32) for g in group[1:]), group[0][...]) for group in groups)
+    rows = first.shape[0]
+    low = low_lanes(first.shape)
+    out[:rows] = rhs[:rows] - jnp.where(low, first, swap_halves(second))
+    out[rows:] = rhs[rows:] - jnp.where(low, swap_halves(first), second)
+
+
+def finish(rhs, groups):
+    if rhs.shape[1] != 128:
+        sums = [sum((g.astype(F32) for g in group[1:]), group[0]) for group in groups]
+        return rhs - jnp.concatenate(sums, axis=1)
+    n = len(groups[0])
+    return pl.pallas_call(
+        functools.partial(finish_kernel, n),
+        out_shape=jax.ShapeDtypeStruct(rhs.shape, F32),
+        in_specs=[VMEM] * (1 + 2 * n),
+        out_specs=VMEM,
+        compiler_params=pltpu.CompilerParams(vmem_limit_bytes=4 << 20),
+        name="finish",
+    )(rhs, *groups[0], *groups[1])
+
+
 def on_device(sep_inverse, rhs_block, coupling, ancestor_rows, ancestor_rhs):
     inverse, rhs, couple = sep_inverse[0], rhs_block[0], coupling[0]
     leaves, n_row = lax.axis_size("leaf"), lax.axis_size("row")
     rows = inverse.shape[0]
-    width = rhs.shape[1]
-    narrow = width // leaves
     dims = [1 << b for b in range(1, n_row.bit_length() - 1)]
     routes = (dims, dims[::-1])
     masks = ([0], [0])
     for step in range(len(dims)):
         for k in (0, 1):
             masks[k].extend([m ^ routes[k][step] for m in masks[k]])
-    edge = leaves // 4
-    cut = edge * narrow
-    is_inner = lambda j: edge <= j < leaves - edge
-    dests = [[j for j in range(leaves) if is_inner(j) == bool(c)] for c in (0, 1)]
 
     def partner(x):
         return lax.ppermute(x, "row", [(i, i ^ 1) for i in range(n_row)])
@@ -208,11 +281,10 @@
                 pieces.append(lax.ppermute(pieces[p], "row", pairs))
         return pieces
 
-    chunks = (
-        jnp.concatenate([rhs[:, :cut], rhs[:, width - cut :]], axis=1),
-        rhs[:, cut : width - cut],
-    )
-    gathered = [gather(x) for x in chunks]
+    gathered = []
+    for c in (0, 1):
+        x = chunk(rhs, c, leaves)
+        gathered.append(gather(x))
 
     def inv_block(other):
         return pick(masks, other, inverse, rows)
@@ -234,7 +306,7 @@
         other = partner(other)
         solved.append((own + other.astype(F32)).astype(BF16))
 
-    out = ancestor_rhs
+    groups = []
     for c, y in enumerate(solved):
         pieces = gather(y)
         sums = ()
@@ -243,14 +315,13 @@
         first = len(pieces) - 1 if c else 0
         own, other = partials(*cpl, pieces[first:], first, sums)
         other = partner(other)
-        total, *sent = split(dests[c], leaves, narrow, own, other)
+        group = list(split(own, other, leaves))
         for d in range(1, leaves):
-            got = lax.ppermute(sent[d - 1], "leaf", [(j ^ d, j) for j in dests[c]])
-            total = total + got.astype(F32)
-        out = out - total
-
-    y_outer, y_inner = solved
-    solution = jnp.concatenate([y_outer[:, :cut], y_inner, y_outer[:, cut:]], axis=1)
+            group[d] = lax.ppermute(group[d], "leaf", [(j, j ^ d) for j in range(leaves)])
+        groups.append(group)
+
+    solution = join(*solved, leaves)
+    out = finish(ancestor_rhs, groups)
     return (solution[None], out)
 
 

time: 101 us -> 89.9 us (0.89)
  starting transfers between devices: 38.9 us -> 31.4 us
  waiting for transfers between devices: 37.1 us -> 31.7 us
  Pallas kernels: 19.4 us -> 22.1 us
  other arithmetic: 2.04 us -> 0.17 us
    ppermute x6, starting transfers between devices: 15.5 us -> 9.2 us  [on_device(): lax.ppermute(group[d], 'leaf', [(j, j ^ d) for j in range(leaves)])]
    ppermute x12, waiting for transfers between devices: 29.5 us -> 26.5 us  [gather(): pieces.append(lax.ppermute(pieces[p], 'row', pairs))]
    pallas_call x2 -> x6, Pallas kernels: 0.23 us -> 2.92 us  [the longest x1 1.21 us: join(): pl.pallas_call(join_kernel, out_shape=jax.ShapeDtypeStruct((rows, 2 * wid...]
    ppermute x6, waiting for transfers between devices: 7.57 us -> 5.27 us  [on_device(): lax.ppermute(group[d], 'leaf', [(j, j ^ d) for j in range(leaves)])]
    ppermute x12, starting transfers between devices: 21.9 us -> 20.6 us  [gather(): pieces.append(lax.ppermute(pieces[p], 'row', pairs))]
    unnamed x16 -> x18, local copies, waits for them, and re-layouts: 2.52 us -> 3.52 us
  transfers between devices with their start and end apart: 24 -> 24, of which waited for: 10 -> 10; matrix products, arithmetic and copies ran while one was open for 1% -> 0% of each run, Pallas kernels for 17% -> 21%
where the time goes in v4:
time: 89.9 us; the launch traced here: 89.7 us
  waiting for transfers between devices  31.7 us (35%)
  starting transfers between devices  31.4 us (35%)
  Pallas kernels  22.1 us (25%)
  local copies, waits for them, and re-layouts  3.52 us (4%)
    ppermute x12, waiting for transfers between devices, gather(): pieces.append(lax.ppermute(pieces[p], 'row', pairs))  26.5 us
    ppermute x12, starting transfers between devices, gather(): pieces.append(lax.ppermute(pieces[p], 'row', pairs))  20.6 us
    ppermute x6, starting transfers between devices, on_device(): lax.ppermute(group[d], 'leaf', [(j, j ^ d) for j in range(leaves)])  9.2 us
    pallas_call x5, Pallas kernels, partials(): pl.pallas_call(functools.partial(partial_kernel, n, first, bool(sums)), o...  8.92 us
    pallas_call x2, Pallas kernels, select_rows(): pl.pallas_call(functools.partial(select_kernel, masks, other), out_shape=...  7.09 us
    ppermute x6, waiting for transfers between devices, on_device(): lax.ppermute(group[d], 'leaf', [(j, j ^ d) for j in range(leaves)])  5.27 us
    unnamed x18, local copies, waits for them, and re-layouts  3.52 us
    pallas_call x2, Pallas kernels, pick(): pl.pallas_call(functools.partial(pick_kernel, masks, other), out_shape=ja...  3.13 us
  transfers between devices with their start and end apart: 24, of which 10 were waited for; matrix products, arithmetic and copies ran while one was open for 0% of the time, Pallas kernels for 21%

profile of v4, /device:TPU:0, one launch (start us, length us, event | category | flops | bytes accessed | tf_op | source)
XLA Modules:
  0.0 89.7 jit_solution(17207623925002345733)
XLA Ops:
  0.6 0.0 slice-start
  0.7 0.0 slice-start.1
  0.7 2.6 %pick.3 = bf16[768,3072]{1,0:T(8,128)(2,1)S(1)} custom-call(bf16[768,6144]{1,0:T(8,128)(2,1)} %bitcast.4), custom_call_target="tpu_custom_call" | custom-call | tf_op jit(solution)/shard_map/pick/pallas_call | solution.py:65
  3.3 0.6 collective-permute-start
  3.8 3.5 %copy-done = bf16[1,512,6144]{2,1,0:T(8,128)(2,1)S(1)} copy-done((bf16[1,512,6144]{2,1,0:T(8,128)(2,1)S(1)}, bf16[1,512,6144]{2,1,0:T(8,128)(2,1)}, u32[]{:S(2)}) %copy-start) | copy-done | bytes 6291480
  7.3 3.5 %select_rows.3 = bf16[512,3072]{1,0:T(8,128)(2,1)S(1)} custom-call(s32[1,512]{1,0:T(1,128)S(1)} %copy-done.3, bf16[512,6144]{1,0:T(8,128)(2,1)S(1)} %bitcast.8), custom_call_target="tpu_custom_call" | custom-call | tf_op jit(solution)/shard_map/select_rows/pallas_call | solution.py:100
  10.8 0.1 collective-permute-start.9
  10.9 0.2 chunk.2.refs_0_
  11.1 2.8 %collective-permute-start.1 = (bf16[768,256]{1,0:T(8,128)(2,1)S(1)}, bf16[768,256]{1,0:T(8,128)(2,1)S(1)}, u32[]{:S(2)}, u32[]{:S(2)}) collective-permute-start(bf16[768,256]{1,0:T(8,128)(2,1)S(1)} %chunk.2.refs_0_), channel_id=1, source_target_pairs={{0,2},{1,5},{2,0},{3,7},{4,6},{5,1},{6,4},{7,3},{8,10},{9,13},{10,... | collective-permute-start | bytes 1179656 | tf_op jit(solution)/shard_map/ppermute | solution.py:281
  13.9 1.5 %collective-permute-start.2 = (bf16[768,256]{1,0:T(8,128)(2,1)S(1)}, bf16[768,256]{1,0:T(8,128)(2,1)S(1)}, u32[]{:S(2)}, u32[]{:S(2)}) collective-permute-start(bf16[768,256]{1,0:T(8,128)(2,1)S(1)} %chunk.2.refs_0_), channel_id=1, source_target_pairs={{0,4},{1,3},{2,6},{3,1},{4,0},{5,7},{6,2},{7,5},{8,12},{9,11},{10,... | collective-permute-start | bytes 1179656 | tf_op jit(solution)/shard_map/ppermute | solution.py:281
  15.4 0.2 chunk.3.refs_0_
  15.6 0.6 collective-permute-start.5
  16.2 6.7 %collective-permute-done.1.refs_1_ = bf16[768,256]{1,0:T(8,128)(2,1)S(1)} collective-permute-done((bf16[768,256]{1,0:T(8,128)(2,1)S(1)}, bf16[768,256]{1,0:T(8,128)(2,1)S(1)}, u32[]{:S(2)}, u32[]{:S(2)}) %collective-permute-start.1) | collective-permute-done | bytes 393248 | tf_op jit(solution)/shard_map/ppermute | solution.py:281
  22.9 2.4 %collective-permute-start.3 = (bf16[768,256]{1,0:T(8,128)(2,1)S(1)}, bf16[768,256]{1,0:T(8,128)(2,1)S(1)}, u32[]{:S(2)}, u32[]{:S(2)}) collective-permute-start(bf16[768,256]{1,0:T(8,128)(2,1)S(1)} %collective-permute-done.1.refs_1_), channel_id=1, source_target_pairs={{0,4},{1,3},{2,6},{3,1},{4,0},{5,7},{6,2},{7,5},{8,12},{9,11},{10,... | collective-permute-start | bytes 1179656 | tf_op jit(solution)/shard_map/ppermute | solution.py:281
  25.3 0.6 collective-permute-done.2.refs_2_
  25.9 1.5 %collective-permute-start.6 = (bf16[768,256]{1,0:T(8,128)(2,1)S(1)}, bf16[768,256]{1,0:T(8,128)(2,1)S(1)}, u32[]{:S(2)}, u32[]{:S(2)}) collective-permute-start(bf16[768,256]{1,0:T(8,128)(2,1)S(1)} %chunk.3.refs_0_), channel_id=1, source_target_pairs={{0,4},{1,3},{2,6},{3,1},{4,0},{5,7},{6,2},{7,5},{8,12},{9,11},{10,... | collective-permute-start | bytes 1179656 | tf_op jit(solution)/shard_map/ppermute | solution.py:281
  27.4 3.4 %collective-permute-done.5.refs_1_ = bf16[768,256]{1,0:T(8,128)(2,1)S(1)} collective-permute-done((bf16[768,256]{1,0:T(8,128)(2,1)S(1)}, bf16[768,256]{1,0:T(8,128)(2,1)S(1)}, u32[]{:S(2)}, u32[]{:S(2)}) %collective-permute-start.5) | collective-permute-done | bytes 393248 | tf_op jit(solution)/shard_map/ppermute | solution.py:281
  30.8 1.8 %collective-permute-start.7 = (bf16[768,256]{1,0:T(8,128)(2,1)S(1)}, bf16[768,256]{1,0:T(8,128)(2,1)S(1)}, u32[]{:S(2)}, u32[]{:S(2)}) collective-permute-start(bf16[768,256]{1,0:T(8,128)(2,1)S(1)} %collective-permute-done.5.refs_1_), channel_id=1, source_target_pairs={{0,4},{1,3},{2,6},{3,1},{4,0},{5,7},{6,2},{7,5},{8,12},{9,11},{10,... | collective-permute-start | bytes 1179656 | tf_op jit(solution)/shard_map/ppermute | solution.py:281
  32.7 0.5 pick.2.keep
  33.2 0.0 collective-permute-done.3.refs_3_
  33.2 0.0 collective-permute-done.swap
  33.2 2.6 %partials.5 = (f32[768,256]{1,0:T(8,128)S(1)}, bf16[768,256]{1,0:T(8,128)(2,1)S(1)}) custom-call(bf16[768,3072]{1,0:T(8,128)(2,1)S(1)} %pick.2.keep, bf16[768,3072]{1,0:T(8,128)(2,1)S(1)} %collective-permute-done.swap, bf16[768,256]{1,0:T(8,128)(2,1)S(1)} %chunk.2.refs_0_, bf16[768,256]{1,0:T(8,128)(2,1)S(1)} %collective-permute-done.1.refs_1_, ...), custom_call_target="tpu_custom_call" | custom-call | tf_op jit(solution)/shard_map/partials/pallas_call | solution.py:131
  35.8 0.0 slice-start.3
  35.8 0.0 slice-start.4
  35.8 0.1 collective-permute-start.4
  35.9 0.2 collective-permute-done.6.refs_2_
  36.1 4.2 %collective-permute-done.7.refs_3_ = bf16[768,256]{1,0:T(8,128)(2,1)S(1)} collective-permute-done((bf16[768,256]{1,0:T(8,128)(2,1)S(1)}, bf16[768,256]{1,0:T(8,128)(2,1)S(1)}, u32[]{:S(2)}, u32[]{:S(2)}) %collective-permute-start.7) | collective-permute-done | bytes 393248 | tf_op jit(solution)/shard_map/ppermute | solution.py:281
  40.3 2.6 %partials.6 = (f32[768,256]{1,0:T(8,128)S(1)}, bf16[768,256]{1,0:T(8,128)(2,1)S(1)}) custom-call(bf16[768,3072]{1,0:T(8,128)(2,1)S(1)} %pick.2.keep, bf16[768,3072]{1,0:T(8,128)(2,1)S(1)} %collective-permute-done.swap, bf16[768,256]{1,0:T(8,128)(2,1)S(1)} %chunk.3.refs_0_, bf16[768,256]{1,0:T(8,128)(2,1)S(1)} %collective-permute-done.5.refs_1_, ...), custom_call_target="tpu_custom_call" | custom-call | tf_op jit(solution)/shard_map/partials/pallas_call | solution.py:131
  42.9 0.3 collective-permute-start.8
  43.2 0.0 collective-permute-done.4
  43.2 0.1 add_convert_fusion.1.x.refs_0_
  43.3 2.1 %collective-permute-start.10 = (bf16[768,256]{1,0:T(8,128)(2,1)S(1)}, bf16[768,256]{1,0:T(8,128)(2,1)S(1)}, u32[]{:S(2)}, u32[]{:S(2)}) collective-permute-start(bf16[768,256]{1,0:T(8,128)(2,1)S(1)} %add_convert_fusion.1.x.refs_0_), channel_id=1, source_target_pairs={{0,2},{1,5},{2,0},{3,7},{4,6},{5,1},{6,4},{7,3},{8,10},{9,13},{10,... | collective-permute-start | bytes 1179656 | tf_op jit(solution)/shard_map/ppermute | solution.py:281
  45.4 0.0 collective-permute-done.8
  45.4 0.1 add_convert_fusion.y.refs_0_
  45.5 1.3 %collective-permute-start.17 = (bf16[768,256]{1,0:T(8,128)(2,1)S(1)}, bf16[768,256]{1,0:T(8,128)(2,1)S(1)}, u32[]{:S(2)}, u32[]{:S(2)}) collective-permute-start(bf16[768,256]{1,0:T(8,128)(2,1)S(1)} %add_convert_fusion.y.refs_0_), channel_id=1, source_target_pairs={{0,2},{1,5},{2,0},{3,7},{4,6},{5,1},{6,4},{7,3},{8,10},{9,13},{10,... | collective-permute-start | bytes 1179656 | tf_op jit(solution)/shard_map/ppermute | solution.py:281
  46.7 1.3 %collective-permute-start.11 = (bf16[768,256]{1,0:T(8,128)(2,1)S(1)}, bf16[768,256]{1,0:T(8,128)(2,1)S(1)}, u32[]{:S(2)}, u32[]{:S(2)}) collective-permute-start(bf16[768,256]{1,0:T(8,128)(2,1)S(1)} %add_convert_fusion.1.x.refs_0_), channel_id=1, source_target_pairs={{0,4},{1,3},{2,6},{3,1},{4,0},{5,7},{6,2},{7,5},{8,12},{9,11},{10,... | collective-permute-start | bytes 1179656 | tf_op jit(solution)/shard_map/ppermute | solution.py:281
  48.1 5.2 %collective-permute-done.10.refs_1_ = bf16[768,256]{1,0:T(8,128)(2,1)S(1)} collective-permute-done((bf16[768,256]{1,0:T(8,128)(2,1)S(1)}, bf16[768,256]{1,0:T(8,128)(2,1)S(1)}, u32[]{:S(2)}, u32[]{:S(2)}) %collective-permute-start.10) | collective-permute-done | bytes 393248 | tf_op jit(solution)/shard_map/ppermute | solution.py:281
  53.3 2.6 %collective-permute-start.12 = (bf16[768,256]{1,0:T(8,128)(2,1)S(1)}, bf16[768,256]{1,0:T(8,128)(2,1)S(1)}, u32[]{:S(2)}, u32[]{:S(2)}) collective-permute-start(bf16[768,256]{1,0:T(8,128)(2,1)S(1)} %collective-permute-done.10.refs_1_), channel_id=1, source_target_pairs={{0,4},{1,3},{2,6},{3,1},{4,0},{5,7},{6,2},{7,5},{8,12},{9,11},{10,... | collective-permute-start | bytes 1179656 | tf_op jit(solution)/shard_map/ppermute | solution.py:281
  55.9 0.0 collective-permute-start.19
  55.9 5.8 %collective-permute-done.17.refs_1_ = bf16[768,256]{1,0:T(8,128)(2,1)S(1)} collective-permute-done((bf16[768,256]{1,0:T(8,128)(2,1)S(1)}, bf16[768,256]{1,0:T(8,128)(2,1)S(1)}, u32[]{:S(2)}, u32[]{:S(2)}) %collective-permute-start.17) | collective-permute-done | bytes 393248 | tf_op jit(solution)/shard_map/ppermute | solution.py:281
  61.7 2.6 %collective-permute-start.18 = (bf16[768,256]{1,0:T(8,128)(2,1)S(1)}, bf16[768,256]{1,0:T(8,128)(2,1)S(1)}, u32[]{:S(2)}, u32[]{:S(2)}) collective-permute-start(bf16[768,256]{1,0:T(8,128)(2,1)S(1)} %collective-permute-done.17.refs_1_), channel_id=1, source_target_pairs={{0,4},{1,3},{2,6},{3,1},{4,0},{5,7},{6,2},{7,5},{8,12},{9,11},{10,... | collective-permute-start | bytes 1179656 | tf_op jit(solution)/shard_map/ppermute | solution.py:281
  64.3 3.6 %select_rows.2.keep = bf16[512,3072]{1,0:T(8,128)(2,1)S(1)} custom-call(s32[1,512]{1,0:T(1,128)S(1)} %copy-done.3, bf16[512,6144]{1,0:T(8,128)(2,1)S(1)} %bitcast.11), custom_call_target="tpu_custom_call" | custom-call | tf_op jit(solution)/shard_map/select_rows/pallas_call | solution.py:100
  68.0 0.0 collective-permute-done.9.swap
  68.0 0.0 collective-permute-done.11.refs_2_
  68.0 1.8 %partials.7 = (f32[512,256]{1,0:T(8,128)S(1)}, bf16[512,256]{1,0:T(8,128)(2,1)S(1)}) custom-call(bf16[512,3072]{1,0:T(8,128)(2,1)S(1)} %select_rows.2.keep, bf16[512,3072]{1,0:T(8,128)(2,1)S(1)} %collective-permute-done.9.swap, bf16[768,256]{1,0:T(8,128)(2,1)S(1)} %add_convert_fusion.1.x.refs_0_, bf16[768,256]{1,0:T(8,128)(2,1)S(1)} %collective-permute-done.10.refs_1_, ...), custom_call_target="tpu_custom_call" | custom-call | tf_op jit(solution)/shard_map/partials/pallas_call | solution.py:131
  69.8 0.1 collective-permute-start.13
  69.9 0.0 collective-permute-done.19.refs_2_
  69.9 1.4 %partials.8 = (f32[512,256]{1,0:T(8,128)S(1)}, f32[512,256]{1,0:T(8,128)S(1)}) custom-call(bf16[512,3072]{1,0:T(8,128)(2,1)S(1)} %select_rows.2.keep, bf16[512,3072]{1,0:T(8,128)(2,1)S(1)} %collective-permute-done.9.swap, bf16[768,256]{1,0:T(8,128)(2,1)S(1)} %add_convert_fusion.y.refs_0_, bf16[768,256]{1,0:T(8,128)(2,1)S(1)} %collective-permute-done.17.refs_1_, ...), custom_call_target="tpu_custom_call" | custom-call | tf_op jit(solution)/shard_map/partials/pallas_call | solution.py:131
  71.3 0.3 collective-permute-done.18.refs_0_
  71.6 0.6 partials.9
  72.1 0.5 collective-permute-start.20
  72.7 0.3 split.2
  72.9 2.2 %collective-permute-start.14 = (bf16[256,128]{1,0:T(8,128)(2,1)S(1)}, bf16[256,128]{1,0:T(8,128)(2,1)S(1)}, u32[]{:S(2)}, u32[]{:S(2)}) collective-permute-start(bf16[256,128]{1,0:T(8,128)(2,1)S(1)} %get-tuple-element.27), channel_id=1, source_target_pairs={{0,8},{8,0},{16,24},{24,16},{1,9},{9,1},{17,25},{25,17},{2,10},{10... | collective-permute-start | bytes 196616 | tf_op jit(solution)/shard_map/ppermute | solution.py:320
  75.1 2.6 %collective-permute-start.15 = (bf16[256,128]{1,0:T(8,128)(2,1)S(1)}, bf16[256,128]{1,0:T(8,128)(2,1)S(1)}, u32[]{:S(2)}, u32[]{:S(2)}) collective-permute-start(bf16[256,128]{1,0:T(8,128)(2,1)S(1)} %get-tuple-element.28), channel_id=1, source_target_pairs={{0,16},{8,24},{16,0},{24,8},{1,17},{9,25},{17,1},{25,9},{2,18},{10... | collective-permute-start | bytes 196616 | tf_op jit(solution)/shard_map/ppermute | solution.py:320
  77.7 0.3 split.3
  78.0 1.0 %collective-permute-start.21 = (bf16[256,128]{1,0:T(8,128)(2,1)S(1)}, bf16[256,128]{1,0:T(8,128)(2,1)S(1)}, u32[]{:S(2)}, u32[]{:S(2)}) collective-permute-start(bf16[256,128]{1,0:T(8,128)(2,1)S(1)} %get-tuple-element.35), channel_id=1, source_target_pairs={{0,8},{8,0},{16,24},{24,16},{1,9},{9,1},{17,25},{25,17},{2,10},{10... | collective-permute-start | bytes 196616 | tf_op jit(solution)/shard_map/ppermute | solution.py:320
  78.9 3.5 %collective-permute-start.22 = (bf16[256,128]{1,0:T(8,128)(2,1)S(1)}, bf16[256,128]{1,0:T(8,128)(2,1)S(1)}, u32[]{:S(2)}, u32[]{:S(2)}) collective-permute-start(bf16[256,128]{1,0:T(8,128)(2,1)S(1)} %get-tuple-element.36), channel_id=1, source_target_pairs={{0,16},{8,24},{16,0},{24,8},{1,17},{9,25},{17,1},{25,9},{2,18},{10... | collective-permute-start | bytes 196616 | tf_op jit(solution)/shard_map/ppermute | solution.py:320
  82.4 0.0 collective-permute-start.23
  82.4 1.2 %join.1 = bf16[768,512]{1,0:T(8,128)(2,1)} custom-call(bf16[768,256]{1,0:T(8,128)(2,1)S(1)} %add_convert_fusion.1.x.refs_0_, bf16[768,256]{1,0:T(8,128)(2,1)S(1)} %add_convert_fusion.y.refs_0_), custom_call_target="tpu_custom_call" | custom-call | tf_op jit(solution)/shard_map/join/pallas_call | solution.py:194
  83.6 0.8 collective-permute-done.16.refs_3_
  84.5 0.0 collective-permute-done.21.refs_5_
  84.5 4.4 %collective-permute-done.22.refs_6_ = bf16[256,128]{1,0:T(8,128)(2,1)S(1)} collective-permute-done((bf16[256,128]{1,0:T(8,128)(2,1)S(1)}, bf16[256,128]{1,0:T(8,128)(2,1)S(1)}, u32[]{:S(2)}, u32[]{:S(2)}) %collective-permute-start.22) | collective-permute-done | bytes 65568 | tf_op jit(solution)/shard_map/ppermute | solution.py:320
  88.9 0.0 collective-permute-done.23.refs_7_
  88.9 0.8 finish.1
  (21 shorter events, 0.0 us)
Async XLA Ops:
  0.6 3.2 %copy-start.3 = (s32[1,512]{1,0:T(1,128)S(1)}, s32[1,512]{1,0:T(1,128)}, u32[]{:S(2)}) copy-start(s32[1,512]{1,0:T(1,128)} %places.3) | copy-start | bytes 6148
  0.6 32.0 %slice-start = ((s8[9437184]{0:T(1024)(128)(4,1)}), s8[4194304]{0:T(1024)(128)(4,1)S(1)}, s32[]{:S(2)}) async-start(s8[9437184]{0:T(1024)(128)(4,1)} %bitcast.5), calls=%async_computation | async-start | bytes 8388608
  0.7 32.0 %slice-start.1 = ((s8[9437184]{0:T(1024)(128)(4,1)}), s8[4194304]{0:T(1024)(128)(4,1)S(1)}, s32[]{:S(2)}) async-start(s8[9437184]{0:T(1024)(128)(4,1)} %bitcast.5), calls=%async_computation.1 | async-start | bytes 8388608
  3.3 29.9 %collective-permute-start = (bf16[768,3072]{1,0:T(8,128)(2,1)S(1)}, bf16[768,3072]{1,0:T(8,128)(2,1)S(1)}, u32[]{:S(2)}, u32[]{:S(2)}) collective-permute-start(bf16[768,3072]{1,0:T(8,128)(2,1)S(1)} %pick.3), channel_id=1, source_target_pairs={{0,1},{1,0},{2,3},{3,2},{4,5},{5,4},{6,7},{7,6},{8,9},{9,8},{10,11... | collective-permute-start | bytes 14155784 | tf_op jit(solution)/shard_map/ppermute | solution.py:274
  3.8 3.5 %copy-start = (bf16[1,512,6144]{2,1,0:T(8,128)(2,1)S(1)}, bf16[1,512,6144]{2,1,0:T(8,128)(2,1)}, u32[]{:S(2)}) copy-start(bf16[1,512,6144]{2,1,0:T(8,128)(2,1)} %param.7) | copy-start | bytes 18874372
  7.3 3.6 %copy-start.1 = (bf16[1,768,512]{2,1,0:T(8,128)(2,1)S(1)}, bf16[1,768,512]{2,1,0:T(8,128)(2,1)}, u32[]{:S(2)}) copy-start(bf16[1,768,512]{2,1,0:T(8,128)(2,1)} %param.6) | copy-start | bytes 2359300
  7.3 25.4 %slice-start.2 = ((s8[9437184]{0:T(1024)(128)(4,1)}), s8[1048576]{0:T(1024)(128)(4,1)S(1)}, s32[]{:S(2)}) async-start(s8[9437184]{0:T(1024)(128)(4,1)} %bitcast.5), calls=%async_computation.2 | async-start | bytes 2097152
  10.8 57.2 %collective-permute-start.9 = (bf16[512,3072]{1,0:T(8,128)(2,1)S(1)}, bf16[512,3072]{1,0:T(8,128)(2,1)S(1)}, u32[]{:S(2)}, u32[]{:S(2)}) collective-permute-start(bf16[512,3072]{1,0:T(8,128)(2,1)S(1)} %select_rows.3), channel_id=1, source_target_pairs={{0,1},{1,0},{2,3},{3,2},{4,5},{5,4},{6,7},{7,6},{8,9},{9,8},{10,11... | collective-permute-start | bytes 9437192 | tf_op jit(solution)/shard_map/ppermute | solution.py:274
  11.1 11.8 %collective-permute-start.1 = (bf16[768,256]{1,0:T(8,128)(2,1)S(1)}, bf16[768,256]{1,0:T(8,128)(2,1)S(1)}, u32[]{:S(2)}, u32[]{:S(2)}) collective-permute-start(bf16[768,256]{1,0:T(8,128)(2,1)S(1)} %chunk.2.refs_0_), channel_id=1, source_target_pairs={{0,2},{1,5},{2,0},{3,7},{4,6},{5,1},{6,4},{7,3},{8,10},{9,13},{10,... | collective-permute-start | bytes 1179656 | tf_op jit(solution)/shard_map/ppermute | solution.py:281
  13.9 12.0 %collective-permute-start.2 = (bf16[768,256]{1,0:T(8,128)(2,1)S(1)}, bf16[768,256]{1,0:T(8,128)(2,1)S(1)}, u32[]{:S(2)}, u32[]{:S(2)}) collective-permute-start(bf16[768,256]{1,0:T(8,128)(2,1)S(1)} %chunk.2.refs_0_), channel_id=1, source_target_pairs={{0,4},{1,3},{2,6},{3,1},{4,0},{5,7},{6,2},{7,5},{8,12},{9,11},{10,... | collective-permute-start | bytes 1179656 | tf_op jit(solution)/shard_map/ppermute | solution.py:281
  15.6 15.2 %collective-permute-start.5 = (bf16[768,256]{1,0:T(8,128)(2,1)S(1)}, bf16[768,256]{1,0:T(8,128)(2,1)S(1)}, u32[]{:S(2)}, u32[]{:S(2)}) collective-permute-start(bf16[768,256]{1,0:T(8,128)(2,1)S(1)} %chunk.3.refs_0_), channel_id=1, source_target_pairs={{0,2},{1,5},{2,0},{3,7},{4,6},{5,1},{6,4},{7,3},{8,10},{9,13},{10,... | collective-permute-start | bytes 1179656 | tf_op jit(solution)/shard_map/ppermute | solution.py:281
  22.9 10.3 %collective-permute-start.3 = (bf16[768,256]{1,0:T(8,128)(2,1)S(1)}, bf16[768,256]{1,0:T(8,128)(2,1)S(1)}, u32[]{:S(2)}, u32[]{:S(2)}) collective-permute-start(bf16[768,256]{1,0:T(8,128)(2,1)S(1)} %collective-permute-done.1.refs_1_), channel_id=1, source_target_pairs={{0,4},{1,3},{2,6},{3,1},{4,0},{5,7},{6,2},{7,5},{8,12},{9,11},{10,... | collective-permute-start | bytes 1179656 | tf_op jit(solution)/shard_map/ppermute | solution.py:281
  25.9 10.2 %collective-permute-start.6 = (bf16[768,256]{1,0:T(8,128)(2,1)S(1)}, bf16[768,256]{1,0:T(8,128)(2,1)S(1)}, u32[]{:S(2)}, u32[]{:S(2)}) collective-permute-start(bf16[768,256]{1,0:T(8,128)(2,1)S(1)} %chunk.3.refs_0_), channel_id=1, source_target_pairs={{0,4},{1,3},{2,6},{3,1},{4,0},{5,7},{6,2},{7,5},{8,12},{9,11},{10,... | collective-permute-start | bytes 1179656 | tf_op jit(solution)/shard_map/ppermute | solution.py:281
  30.8 9.5 %collective-permute-start.7 = (bf16[768,256]{1,0:T(8,128)(2,1)S(1)}, bf16[768,256]{1,0:T(8,128)(2,1)S(1)}, u32[]{:S(2)}, u32[]{:S(2)}) collective-permute-start(bf16[768,256]{1,0:T(8,128)(2,1)S(1)} %collective-permute-done.5.refs_1_), channel_id=1, source_target_pairs={{0,4},{1,3},{2,6},{3,1},{4,0},{5,7},{6,2},{7,5},{8,12},{9,11},{10,... | collective-permute-start | bytes 1179656 | tf_op jit(solution)/shard_map/ppermute | solution.py:281
  35.8 28.5 %slice-start.3 = ((s8[6291456]{0:T(1024)(128)(4,1)}), s8[4194304]{0:T(1024)(128)(4,1)S(1)}, s32[]{:S(2)}) async-start(s8[6291456]{0:T(1024)(128)(4,1)} %bitcast.9), calls=%async_computation.3 | async-start | bytes 8388608
  35.8 28.5 %slice-start.4 = ((s8[6291456]{0:T(1024)(128)(4,1)}), s8[2097152]{0:T(1024)(128)(4,1)S(1)}, s32[]{:S(2)}) async-start(s8[6291456]{0:T(1024)(128)(4,1)} %bitcast.9), calls=%async_computation.4 | async-start | bytes 4194304
  35.8 7.4 %collective-permute-start.4 = (bf16[768,256]{1,0:T(8,128)(2,1)S(1)}, bf16[768,256]{1,0:T(8,128)(2,1)S(1)}, u32[]{:S(2)}, u32[]{:S(2)}) collective-permute-start(bf16[768,256]{1,0:T(8,128)(2,1)S(1)} %get-tuple-element.21), channel_id=1, source_target_pairs={{0,1},{1,0},{2,3},{3,2},{4,5},{5,4},{6,7},{7,6},{8,9},{9,8},{10,11... | collective-permute-start | bytes 1179656 | tf_op jit(solution)/shard_map/ppermute | solution.py:274
  42.9 2.4 %collective-permute-start.8 = (bf16[768,256]{1,0:T(8,128)(2,1)S(1)}, bf16[768,256]{1,0:T(8,128)(2,1)S(1)}, u32[]{:S(2)}, u32[]{:S(2)}) collective-permute-start(bf16[768,256]{1,0:T(8,128)(2,1)S(1)} %get-tuple-element.23), channel_id=1, source_target_pairs={{0,1},{1,0},{2,3},{3,2},{4,5},{5,4},{6,7},{7,6},{8,9},{9,8},{10,11... | collective-permute-start | bytes 1179656 | tf_op jit(solution)/shard_map/ppermute | solution.py:274
  43.3 10.0 %collective-permute-start.10 = (bf16[768,256]{1,0:T(8,128)(2,1)S(1)}, bf16[768,256]{1,0:T(8,128)(2,1)S(1)}, u32[]{:S(2)}, u32[]{:S(2)}) collective-permute-start(bf16[768,256]{1,0:T(8,128)(2,1)S(1)} %add_convert_fusion.1.x.refs_0_), channel_id=1, source_target_pairs={{0,2},{1,5},{2,0},{3,7},{4,6},{5,1},{6,4},{7,3},{8,10},{9,13},{10,... | collective-permute-start | bytes 1179656 | tf_op jit(solution)/shard_map/ppermute | solution.py:281
  45.5 16.3 %collective-permute-start.17 = (bf16[768,256]{1,0:T(8,128)(2,1)S(1)}, bf16[768,256]{1,0:T(8,128)(2,1)S(1)}, u32[]{:S(2)}, u32[]{:S(2)}) collective-permute-start(bf16[768,256]{1,0:T(8,128)(2,1)S(1)} %add_convert_fusion.y.refs_0_), channel_id=1, source_target_pairs={{0,2},{1,5},{2,0},{3,7},{4,6},{5,1},{6,4},{7,3},{8,10},{9,13},{10,... | collective-permute-start | bytes 1179656 | tf_op jit(solution)/shard_map/ppermute | solution.py:281
  46.7 21.3 %collective-permute-start.11 = (bf16[768,256]{1,0:T(8,128)(2,1)S(1)}, bf16[768,256]{1,0:T(8,128)(2,1)S(1)}, u32[]{:S(2)}, u32[]{:S(2)}) collective-permute-start(bf16[768,256]{1,0:T(8,128)(2,1)S(1)} %add_convert_fusion.1.x.refs_0_), channel_id=1, source_target_pairs={{0,4},{1,3},{2,6},{3,1},{4,0},{5,7},{6,2},{7,5},{8,12},{9,11},{10,... | collective-permute-start | bytes 1179656 | tf_op jit(solution)/shard_map/ppermute | solution.py:281
  53.3 14.7 %collective-permute-start.12 = (bf16[768,256]{1,0:T(8,128)(2,1)S(1)}, bf16[768,256]{1,0:T(8,128)(2,1)S(1)}, u32[]{:S(2)}, u32[]{:S(2)}) collective-permute-start(bf16[768,256]{1,0:T(8,128)(2,1)S(1)} %collective-permute-done.10.refs_1_), channel_id=1, source_target_pairs={{0,4},{1,3},{2,6},{3,1},{4,0},{5,7},{6,2},{7,5},{8,12},{9,11},{10,... | collective-permute-start | bytes 1179656 | tf_op jit(solution)/shard_map/ppermute | solution.py:281
  55.9 14.0 %collective-permute-start.19 = (bf16[768,256]{1,0:T(8,128)(2,1)S(1)}, bf16[768,256]{1,0:T(8,128)(2,1)S(1)}, u32[]{:S(2)}, u32[]{:S(2)}) collective-permute-start(bf16[768,256]{1,0:T(8,128)(2,1)S(1)} %add_convert_fusion.y.refs_0_), channel_id=1, source_target_pairs={{0,4},{1,3},{2,6},{3,1},{4,0},{5,7},{6,2},{7,5},{8,12},{9,11},{10,... | collective-permute-start | bytes 1179656 | tf_op jit(solution)/shard_map/ppermute | solution.py:281
  61.7 9.8 %collective-permute-start.18 = (bf16[768,256]{1,0:T(8,128)(2,1)S(1)}, bf16[768,256]{1,0:T(8,128)(2,1)S(1)}, u32[]{:S(2)}, u32[]{:S(2)}) collective-permute-start(bf16[768,256]{1,0:T(8,128)(2,1)S(1)} %collective-permute-done.17.refs_1_), channel_id=1, source_target_pairs={{0,4},{1,3},{2,6},{3,1},{4,0},{5,7},{6,2},{7,5},{8,12},{9,11},{10,... | collective-permute-start | bytes 1179656 | tf_op jit(solution)/shard_map/ppermute | solution.py:281
  69.8 2.9 %collective-permute-start.13 = (bf16[512,256]{1,0:T(8,128)(2,1)S(1)}, bf16[512,256]{1,0:T(8,128)(2,1)S(1)}, u32[]{:S(2)}, u32[]{:S(2)}) collective-permute-start(bf16[512,256]{1,0:T(8,128)(2,1)S(1)} %get-tuple-element.25), channel_id=1, source_target_pairs={{0,1},{1,0},{2,3},{3,2},{4,5},{5,4},{6,7},{7,6},{8,9},{9,8},{10,11... | collective-permute-start | bytes 786440 | tf_op jit(solution)/shard_map/ppermute | solution.py:274
  71.5 17.4 %copy-start.2 = (f32[512,128]{1,0:T(8,128)S(1)}, f32[512,128]{1,0:T(8,128)}, u32[]{:S(2)}) copy-start(f32[512,128]{1,0:T(8,128)} %rhs.1) | copy-start | bytes 786436
  72.1 5.6 %collective-permute-start.20 = (bf16[512,256]{1,0:T(8,128)(2,1)S(1)}, bf16[512,256]{1,0:T(8,128)(2,1)S(1)}, u32[]{:S(2)}, u32[]{:S(2)}) collective-permute-start(bf16[512,256]{1,0:T(8,128)(2,1)S(1)} %get-tuple-element.33), channel_id=1, source_target_pairs={{0,1},{1,0},{2,3},{3,2},{4,5},{5,4},{6,7},{7,6},{8,9},{9,8},{10,11... | collective-permute-start | bytes 786440 | tf_op jit(solution)/shard_map/ppermute | solution.py:274
  72.9 9.5 %collective-permute-start.14 = (bf16[256,128]{1,0:T(8,128)(2,1)S(1)}, bf16[256,128]{1,0:T(8,128)(2,1)S(1)}, u32[]{:S(2)}, u32[]{:S(2)}) collective-permute-start(bf16[256,128]{1,0:T(8,128)(2,1)S(1)} %get-tuple-element.27), channel_id=1, source_target_pairs={{0,8},{8,0},{16,24},{24,16},{1,9},{9,1},{17,25},{25,17},{2,10},{10... | collective-permute-start | bytes 196616 | tf_op jit(solution)/shard_map/ppermute | solution.py:320
  75.1 8.5 %collective-permute-start.15 = (bf16[256,128]{1,0:T(8,128)(2,1)S(1)}, bf16[256,128]{1,0:T(8,128)(2,1)S(1)}, u32[]{:S(2)}, u32[]{:S(2)}) collective-permute-start(bf16[256,128]{1,0:T(8,128)(2,1)S(1)} %get-tuple-element.28), channel_id=1, source_target_pairs={{0,16},{8,24},{16,0},{24,8},{1,17},{9,25},{17,1},{25,9},{2,18},{10... | collective-permute-start | bytes 196616 | tf_op jit(solution)/shard_map/ppermute | solution.py:320
  77.7 6.8 %collective-permute-start.16 = (bf16[256,128]{1,0:T(8,128)(2,1)S(1)}, bf16[256,128]{1,0:T(8,128)(2,1)S(1)}, u32[]{:S(2)}, u32[]{:S(2)}) collective-permute-start(bf16[256,128]{1,0:T(8,128)(2,1)S(1)} %get-tuple-element.29), channel_id=1, source_target_pairs={{0,24},{8,16},{16,8},{24,0},{1,25},{9,17},{17,9},{25,1},{2,26},{10... | collective-permute-start | bytes 196616 | tf_op jit(solution)/shard_map/ppermute | solution.py:320
  78.0 6.5 %collective-permute-start.21 = (bf16[256,128]{1,0:T(8,128)(2,1)S(1)}, bf16[256,128]{1,0:T(8,128)(2,1)S(1)}, u32[]{:S(2)}, u32[]{:S(2)}) collective-permute-start(bf16[256,128]{1,0:T(8,128)(2,1)S(1)} %get-tuple-element.35), channel_id=1, source_target_pairs={{0,8},{8,0},{16,24},{24,16},{1,9},{9,1},{17,25},{25,17},{2,10},{10... | collective-permute-start | bytes 196616 | tf_op jit(solution)/shard_map/ppermute | solution.py:320
  78.9 10.0 %collective-permute-start.22 = (bf16[256,128]{1,0:T(8,128)(2,1)S(1)}, bf16[256,128]{1,0:T(8,128)(2,1)S(1)}, u32[]{:S(2)}, u32[]{:S(2)}) collective-permute-start(bf16[256,128]{1,0:T(8,128)(2,1)S(1)} %get-tuple-element.36), channel_id=1, source_target_pairs={{0,16},{8,24},{16,0},{24,8},{1,17},{9,25},{17,1},{25,9},{2,18},{10... | collective-permute-start | bytes 196616 | tf_op jit(solution)/shard_map/ppermute | solution.py:320
  82.4 6.5 %collective-permute-start.23 = (bf16[256,128]{1,0:T(8,128)(2,1)S(1)}, bf16[256,128]{1,0:T(8,128)(2,1)S(1)}, u32[]{:S(2)}, u32[]{:S(2)}) collective-permute-start(bf16[256,128]{1,0:T(8,128)(2,1)S(1)} %get-tuple-element.37), channel_id=1, source_target_pairs={{0,24},{8,16},{16,8},{24,0},{1,25},{9,17},{17,9},{25,1},{2,26},{10... | collective-permute-start | bytes 196616 | tf_op jit(solution)/shard_map/ppermute | solution.py:320

commit v5 on v4

--- a/solution.py
+++ b/solution.py
@@ -8,7 +8,7 @@
 from jax.sharding import PartitionSpec as P
 
 VMEM = pl.BlockSpec(memory_space=pltpu.VMEM)
-SPLIT = 4
+SPLIT = 2
 F32 = jnp.float32
 BF16 = jnp.bfloat16
 
@@ -154,7 +154,7 @@
     return slice(t * 128, (t + 1) * 128)
 
 
-def chunk_kernel(c, x, out):
+def halves(c, x, out):
     for t in range(out.shape[1] // 128):
         a, b = x[:, tile(2 * t)].astype(F32), x[:, tile(2 * t + 1)].astype(F32)
         low = low_lanes(a.shape)
@@ -162,19 +162,46 @@
         out[:, tile(t)] = both.astype(out.dtype)
 
 
+def chunk_kernel(c, x, out, buf, sem):
+    rows = x.shape[0] // SPLIT
+    copies = [
+        pltpu.make_async_copy(
+            x.at[pl.ds(r * rows, rows)], buf.at[pl.ds(r * rows, rows)], sem.at[r]
+        )
+        for r in range(SPLIT)
+    ]
+    for copy in copies:
+        copy.start()
+    for r, copy in enumerate(copies):
+        copy.wait()
+        block = pl.ds(r * rows, rows)
+        halves(c, buf.at[block], out.at[block])
+
+
 def chunk(x, c, leaves):
     rows, width = x.shape
     half = width // leaves // 2
     if half != 64:
         return x.reshape(rows, leaves, 2, half)[:, :, c].reshape(rows, width // 2)
+    out = jax.ShapeDtypeStruct((rows, width // 2), x.dtype)
+    if c:
+        return pl.pallas_call(
+            functools.partial(halves, c),
+            out_shape=out,
+            in_specs=[VMEM],
+            out_specs=VMEM,
+            compiler_params=pltpu.CompilerParams(vmem_limit_bytes=4 << 20),
+            name="chunk",
+        )(x)
     return pl.pallas_call(
         functools.partial(chunk_kernel, c),
-        out_shape=jax.ShapeDtypeStruct((rows, width // 2), x.dtype),
-        in_specs=[VMEM],
-        out_specs=VMEM,
+        out_shape=out,
+        in_specs=[pl.BlockSpec(memory_space=pl.ANY)],
+        out_specs=VMEM,
+        scratch_shapes=[pltpu.VMEM((rows, width), x.dtype), pltpu.SemaphoreType.DMA((SPLIT,))],
         compiler_params=pltpu.CompilerParams(vmem_limit_bytes=4 << 20),
         name="chunk",
-    )(x)
+    )(pltpu.with_memory_space_constraint(x, pltpu.HBM))
 
 
 def join_kernel(x, y, out):

time: 89.9 us -> 90.8 us (1.010)
    pallas_call x2, Pallas kernels: 0.35 us -> 1.43 us  [the longest x1 1.26 us: chunk(): pl.pallas_call(functools.partial(chunk_kernel, c), out_shape=out, in_spec...]
where the time goes in v5:
time: 90.8 us; the launch traced here: 90.6 us
  waiting for transfers between devices  32.2 us (35%)
  starting transfers between devices  31.1 us (34%)
  Pallas kernels  22.7 us (25%)
  local copies, waits for them, and re-layouts  3.58 us (4%)
    ppermute x12, waiting for transfers between devices, gather(): pieces.append(lax.ppermute(pieces[p], 'row', pairs))  26.9 us
    ppermute x12, starting transfers between devices, gather(): pieces.append(lax.ppermute(pieces[p], 'row', pairs))  20.2 us
    ppermute x6, starting transfers between devices, on_device(): lax.ppermute(group[d], 'leaf', [(j, j ^ d) for j in range(leaves)])  9.21 us
    pallas_call x5, Pallas kernels, partials(): pl.pallas_call(functools.partial(partial_kernel, n, first, bool(sums)), o...  8.92 us
    pallas_call x2, Pallas kernels, select_rows(): pl.pallas_call(functools.partial(select_kernel, masks, other), out_shape=...  6.65 us
    ppermute x6, waiting for transfers between devices, on_device(): lax.ppermute(group[d], 'leaf', [(j, j ^ d) for j in range(leaves)])  5.27 us
    unnamed x18, local copies, waits for them, and re-layouts  3.58 us
    pallas_call x2, Pallas kernels, pick(): pl.pallas_call(functools.partial(pick_kernel, masks, other), out_shape=ja...  3.15 us
  transfers between devices with their start and end apart: 24, of which 10 were waited for; matrix products, arithmetic and copies ran while one was open for 0% of the time, Pallas kernels for 21%

profile of v5, /device:TPU:0, one launch (start us, length us, event | category | flops | bytes accessed | tf_op | source)
XLA Modules:
  0.0 90.6 jit_solution(5961777427172591794)
XLA Ops:
  0.6 0.0 slice-start
  0.7 0.0 slice-start.1
  0.7 2.6 %pick.3 = bf16[768,3072]{1,0:T(8,128)(2,1)S(1)} custom-call(bf16[768,6144]{1,0:T(8,128)(2,1)} %bitcast.4), custom_call_target="tpu_custom_call" | custom-call | tf_op jit(solution)/shard_map/pick/pallas_call | solution.py:65
  3.2 0.6 collective-permute-start
  3.8 3.5 %copy-done = bf16[1,512,6144]{2,1,0:T(8,128)(2,1)S(1)} copy-done((bf16[1,512,6144]{2,1,0:T(8,128)(2,1)S(1)}, bf16[1,512,6144]{2,1,0:T(8,128)(2,1)}, u32[]{:S(2)}) %copy-start) | copy-done | bytes 6291480
  7.3 3.2 %select_rows.3 = bf16[512,3072]{1,0:T(8,128)(2,1)S(1)} custom-call(s32[1,512]{1,0:T(1,128)S(1)} %copy-done.3, bf16[512,6144]{1,0:T(8,128)(2,1)S(1)} %bitcast.8), custom_call_target="tpu_custom_call" | custom-call | tf_op jit(solution)/shard_map/select_rows/pallas_call | solution.py:100
  10.6 0.1 collective-permute-start.9
  10.7 1.3 %chunk.2.refs_0_ = bf16[768,256]{1,0:T(8,128)(2,1)S(1)} custom-call(bf16[768,512]{1,0:T(8,128)(2,1)} %bitcast.12), custom_call_target="tpu_custom_call" | custom-call | tf_op jit(solution)/shard_map/chunk/pallas_call | solution.py:196
  11.9 2.8 %collective-permute-start.1 = (bf16[768,256]{1,0:T(8,128)(2,1)S(1)}, bf16[768,256]{1,0:T(8,128)(2,1)S(1)}, u32[]{:S(2)}, u32[]{:S(2)}) collective-permute-start(bf16[768,256]{1,0:T(8,128)(2,1)S(1)} %chunk.2.refs_0_), channel_id=1, source_target_pairs={{0,2},{1,5},{2,0},{3,7},{4,6},{5,1},{6,4},{7,3},{8,10},{9,13},{10,... | collective-permute-start | bytes 1179656 | tf_op jit(solution)/shard_map/ppermute | solution.py:308
  14.8 1.5 %collective-permute-start.2 = (bf16[768,256]{1,0:T(8,128)(2,1)S(1)}, bf16[768,256]{1,0:T(8,128)(2,1)S(1)}, u32[]{:S(2)}, u32[]{:S(2)}) collective-permute-start(bf16[768,256]{1,0:T(8,128)(2,1)S(1)} %chunk.2.refs_0_), channel_id=1, source_target_pairs={{0,4},{1,3},{2,6},{3,1},{4,0},{5,7},{6,2},{7,5},{8,12},{9,11},{10,... | collective-permute-start | bytes 1179656 | tf_op jit(solution)/shard_map/ppermute | solution.py:308
  16.3 0.2 chunk.3.refs_0_
  16.5 0.6 collective-permute-start.5
  17.1 6.7 %collective-permute-done.1.refs_1_ = bf16[768,256]{1,0:T(8,128)(2,1)S(1)} collective-permute-done((bf16[768,256]{1,0:T(8,128)(2,1)S(1)}, bf16[768,256]{1,0:T(8,128)(2,1)S(1)}, u32[]{:S(2)}, u32[]{:S(2)}) %collective-permute-start.1) | collective-permute-done | bytes 393248 | tf_op jit(solution)/shard_map/ppermute | solution.py:308
  23.8 2.4 %collective-permute-start.3 = (bf16[768,256]{1,0:T(8,128)(2,1)S(1)}, bf16[768,256]{1,0:T(8,128)(2,1)S(1)}, u32[]{:S(2)}, u32[]{:S(2)}) collective-permute-start(bf16[768,256]{1,0:T(8,128)(2,1)S(1)} %collective-permute-done.1.refs_1_), channel_id=1, source_target_pairs={{0,4},{1,3},{2,6},{3,1},{4,0},{5,7},{6,2},{7,5},{8,12},{9,11},{10,... | collective-permute-start | bytes 1179656 | tf_op jit(solution)/shard_map/ppermute | solution.py:308
  26.1 0.6 collective-permute-done.2.refs_2_
  26.7 1.5 %collective-permute-start.6 = (bf16[768,256]{1,0:T(8,128)(2,1)S(1)}, bf16[768,256]{1,0:T(8,128)(2,1)S(1)}, u32[]{:S(2)}, u32[]{:S(2)}) collective-permute-start(bf16[768,256]{1,0:T(8,128)(2,1)S(1)} %chunk.3.refs_0_), channel_id=1, source_target_pairs={{0,4},{1,3},{2,6},{3,1},{4,0},{5,7},{6,2},{7,5},{8,12},{9,11},{10,... | collective-permute-start | bytes 1179656 | tf_op jit(solution)/shard_map/ppermute | solution.py:308
  28.3 3.5 %collective-permute-done.5.refs_1_ = bf16[768,256]{1,0:T(8,128)(2,1)S(1)} collective-permute-done((bf16[768,256]{1,0:T(8,128)(2,1)S(1)}, bf16[768,256]{1,0:T(8,128)(2,1)S(1)}, u32[]{:S(2)}, u32[]{:S(2)}) %collective-permute-start.5) | collective-permute-done | bytes 393248 | tf_op jit(solution)/shard_map/ppermute | solution.py:308
  31.8 1.8 %collective-permute-start.7 = (bf16[768,256]{1,0:T(8,128)(2,1)S(1)}, bf16[768,256]{1,0:T(8,128)(2,1)S(1)}, u32[]{:S(2)}, u32[]{:S(2)}) collective-permute-start(bf16[768,256]{1,0:T(8,128)(2,1)S(1)} %collective-permute-done.5.refs_1_), channel_id=1, source_target_pairs={{0,4},{1,3},{2,6},{3,1},{4,0},{5,7},{6,2},{7,5},{8,12},{9,11},{10,... | collective-permute-start | bytes 1179656 | tf_op jit(solution)/shard_map/ppermute | solution.py:308
  33.5 0.6 pick.2.keep
  34.1 0.0 collective-permute-done.3.refs_3_
  34.2 2.6 %partials.5 = (f32[768,256]{1,0:T(8,128)S(1)}, bf16[768,256]{1,0:T(8,128)(2,1)S(1)}) custom-call(bf16[768,3072]{1,0:T(8,128)(2,1)S(1)} %pick.2.keep, bf16[768,3072]{1,0:T(8,128)(2,1)S(1)} %collective-permute-done.swap, bf16[768,256]{1,0:T(8,128)(2,1)S(1)} %chunk.2.refs_0_, bf16[768,256]{1,0:T(8,128)(2,1)S(1)} %collective-permute-done.1.refs_1_, ...), custom_call_target="tpu_custom_call" | custom-call | tf_op jit(solution)/shard_map/partials/pallas_call | solution.py:131
  36.8 0.0 slice-start.3
  36.8 0.0 slice-start.4
  36.8 0.1 collective-permute-start.4
  36.9 0.1 collective-permute-done.6.refs_2_
  37.0 4.2 %collective-permute-done.7.refs_3_ = bf16[768,256]{1,0:T(8,128)(2,1)S(1)} collective-permute-done((bf16[768,256]{1,0:T(8,128)(2,1)S(1)}, bf16[768,256]{1,0:T(8,128)(2,1)S(1)}, u32[]{:S(2)}, u32[]{:S(2)}) %collective-permute-start.7) | collective-permute-done | bytes 393248 | tf_op jit(solution)/shard_map/ppermute | solution.py:308
  41.2 2.6 %partials.6 = (f32[768,256]{1,0:T(8,128)S(1)}, bf16[768,256]{1,0:T(8,128)(2,1)S(1)}) custom-call(bf16[768,3072]{1,0:T(8,128)(2,1)S(1)} %pick.2.keep, bf16[768,3072]{1,0:T(8,128)(2,1)S(1)} %collective-permute-done.swap, bf16[768,256]{1,0:T(8,128)(2,1)S(1)} %chunk.3.refs_0_, bf16[768,256]{1,0:T(8,128)(2,1)S(1)} %collective-permute-done.5.refs_1_, ...), custom_call_target="tpu_custom_call" | custom-call | tf_op jit(solution)/shard_map/partials/pallas_call | solution.py:131
  43.8 0.3 collective-permute-start.8
  44.1 0.0 collective-permute-done.4
  44.1 0.1 add_convert_fusion.1.x.refs_0_
  44.2 2.1 %collective-permute-start.10 = (bf16[768,256]{1,0:T(8,128)(2,1)S(1)}, bf16[768,256]{1,0:T(8,128)(2,1)S(1)}, u32[]{:S(2)}, u32[]{:S(2)}) collective-permute-start(bf16[768,256]{1,0:T(8,128)(2,1)S(1)} %add_convert_fusion.1.x.refs_0_), channel_id=1, source_target_pairs={{0,2},{1,5},{2,0},{3,7},{4,6},{5,1},{6,4},{7,3},{8,10},{9,13},{10,... | collective-permute-start | bytes 1179656 | tf_op jit(solution)/shard_map/ppermute | solution.py:308
  46.2 0.1 add_convert_fusion.y.refs_0_
  46.3 1.3 %collective-permute-start.17 = (bf16[768,256]{1,0:T(8,128)(2,1)S(1)}, bf16[768,256]{1,0:T(8,128)(2,1)S(1)}, u32[]{:S(2)}, u32[]{:S(2)}) collective-permute-start(bf16[768,256]{1,0:T(8,128)(2,1)S(1)} %add_convert_fusion.y.refs_0_), channel_id=1, source_target_pairs={{0,2},{1,5},{2,0},{3,7},{4,6},{5,1},{6,4},{7,3},{8,10},{9,13},{10,... | collective-permute-start | bytes 1179656 | tf_op jit(solution)/shard_map/ppermute | solution.py:308
  47.6 1.3 %collective-permute-start.11 = (bf16[768,256]{1,0:T(8,128)(2,1)S(1)}, bf16[768,256]{1,0:T(8,128)(2,1)S(1)}, u32[]{:S(2)}, u32[]{:S(2)}) collective-permute-start(bf16[768,256]{1,0:T(8,128)(2,1)S(1)} %add_convert_fusion.1.x.refs_0_), channel_id=1, source_target_pairs={{0,4},{1,3},{2,6},{3,1},{4,0},{5,7},{6,2},{7,5},{8,12},{9,11},{10,... | collective-permute-start | bytes 1179656 | tf_op jit(solution)/shard_map/ppermute | solution.py:308
  48.9 5.3 %collective-permute-done.10.refs_1_ = bf16[768,256]{1,0:T(8,128)(2,1)S(1)} collective-permute-done((bf16[768,256]{1,0:T(8,128)(2,1)S(1)}, bf16[768,256]{1,0:T(8,128)(2,1)S(1)}, u32[]{:S(2)}, u32[]{:S(2)}) %collective-permute-start.10) | collective-permute-done | bytes 393248 | tf_op jit(solution)/shard_map/ppermute | solution.py:308
  54.2 2.5 %collective-permute-start.12 = (bf16[768,256]{1,0:T(8,128)(2,1)S(1)}, bf16[768,256]{1,0:T(8,128)(2,1)S(1)}, u32[]{:S(2)}, u32[]{:S(2)}) collective-permute-start(bf16[768,256]{1,0:T(8,128)(2,1)S(1)} %collective-permute-done.10.refs_1_), channel_id=1, source_target_pairs={{0,4},{1,3},{2,6},{3,1},{4,0},{5,7},{6,2},{7,5},{8,12},{9,11},{10,... | collective-permute-start | bytes 1179656 | tf_op jit(solution)/shard_map/ppermute | solution.py:308
  56.7 0.0 collective-permute-start.19
  56.7 5.9 %collective-permute-done.17.refs_1_ = bf16[768,256]{1,0:T(8,128)(2,1)S(1)} collective-permute-done((bf16[768,256]{1,0:T(8,128)(2,1)S(1)}, bf16[768,256]{1,0:T(8,128)(2,1)S(1)}, u32[]{:S(2)}, u32[]{:S(2)}) %collective-permute-start.17) | collective-permute-done | bytes 393248 | tf_op jit(solution)/shard_map/ppermute | solution.py:308
  62.6 2.5 %collective-permute-start.18 = (bf16[768,256]{1,0:T(8,128)(2,1)S(1)}, bf16[768,256]{1,0:T(8,128)(2,1)S(1)}, u32[]{:S(2)}, u32[]{:S(2)}) collective-permute-start(bf16[768,256]{1,0:T(8,128)(2,1)S(1)} %collective-permute-done.17.refs_1_), channel_id=1, source_target_pairs={{0,4},{1,3},{2,6},{3,1},{4,0},{5,7},{6,2},{7,5},{8,12},{9,11},{10,... | collective-permute-start | bytes 1179656 | tf_op jit(solution)/shard_map/ppermute | solution.py:308
  65.1 3.4 %select_rows.2.keep = bf16[512,3072]{1,0:T(8,128)(2,1)S(1)} custom-call(s32[1,512]{1,0:T(1,128)S(1)} %copy-done.3, bf16[512,6144]{1,0:T(8,128)(2,1)S(1)} %bitcast.11), custom_call_target="tpu_custom_call" | custom-call | tf_op jit(solution)/shard_map/select_rows/pallas_call | solution.py:100
  68.5 0.0 collective-permute-done.11.refs_2_
  68.6 0.0 collective-permute-done.12.refs_3_
  68.6 1.8 %partials.7 = (f32[512,256]{1,0:T(8,128)S(1)}, bf16[512,256]{1,0:T(8,128)(2,1)S(1)}) custom-call(bf16[512,3072]{1,0:T(8,128)(2,1)S(1)} %select_rows.2.keep, bf16[512,3072]{1,0:T(8,128)(2,1)S(1)} %collective-permute-done.9.swap, bf16[768,256]{1,0:T(8,128)(2,1)S(1)} %add_convert_fusion.1.x.refs_0_, bf16[768,256]{1,0:T(8,128)(2,1)S(1)} %collective-permute-done.10.refs_1_, ...), custom_call_target="tpu_custom_call" | custom-call | tf_op jit(solution)/shard_map/partials/pallas_call | solution.py:131
  70.4 0.1 collective-permute-start.13
  70.4 0.0 collective-permute-done.19.refs_2_
  70.5 1.4 %partials.8 = (f32[512,256]{1,0:T(8,128)S(1)}, f32[512,256]{1,0:T(8,128)S(1)}) custom-call(bf16[512,3072]{1,0:T(8,128)(2,1)S(1)} %select_rows.2.keep, bf16[512,3072]{1,0:T(8,128)(2,1)S(1)} %collective-permute-done.9.swap, bf16[768,256]{1,0:T(8,128)(2,1)S(1)} %add_convert_fusion.y.refs_0_, bf16[768,256]{1,0:T(8,128)(2,1)S(1)} %collective-permute-done.17.refs_1_, ...), custom_call_target="tpu_custom_call" | custom-call | tf_op jit(solution)/shard_map/partials/pallas_call | solution.py:131
  71.8 0.5 collective-permute-done.18.refs_0_
  72.4 0.6 partials.9
  73.0 0.6 collective-permute-start.20
  73.5 0.3 split.2
  73.8 2.2 %collective-permute-start.14 = (bf16[256,128]{1,0:T(8,128)(2,1)S(1)}, bf16[256,128]{1,0:T(8,128)(2,1)S(1)}, u32[]{:S(2)}, u32[]{:S(2)}) collective-permute-start(bf16[256,128]{1,0:T(8,128)(2,1)S(1)} %get-tuple-element.27), channel_id=1, source_target_pairs={{0,8},{8,0},{16,24},{24,16},{1,9},{9,1},{17,25},{25,17},{2,10},{10... | collective-permute-start | bytes 196616 | tf_op jit(solution)/shard_map/ppermute | solution.py:347
  76.0 2.6 %collective-permute-start.15 = (bf16[256,128]{1,0:T(8,128)(2,1)S(1)}, bf16[256,128]{1,0:T(8,128)(2,1)S(1)}, u32[]{:S(2)}, u32[]{:S(2)}) collective-permute-start(bf16[256,128]{1,0:T(8,128)(2,1)S(1)} %get-tuple-element.28), channel_id=1, source_target_pairs={{0,16},{8,24},{16,0},{24,8},{1,17},{9,25},{17,1},{25,9},{2,18},{10... | collective-permute-start | bytes 196616 | tf_op jit(solution)/shard_map/ppermute | solution.py:347
  78.6 0.0 collective-permute-start.16
  78.6 0.0 collective-permute-done.20.other
  78.6 0.3 split.3
  78.8 1.0 %collective-permute-start.21 = (bf16[256,128]{1,0:T(8,128)(2,1)S(1)}, bf16[256,128]{1,0:T(8,128)(2,1)S(1)}, u32[]{:S(2)}, u32[]{:S(2)}) collective-permute-start(bf16[256,128]{1,0:T(8,128)(2,1)S(1)} %get-tuple-element.35), channel_id=1, source_target_pairs={{0,8},{8,0},{16,24},{24,16},{1,9},{9,1},{17,25},{25,17},{2,10},{10... | collective-permute-start | bytes 196616 | tf_op jit(solution)/shard_map/ppermute | solution.py:347
  79.8 3.5 %collective-permute-start.22 = (bf16[256,128]{1,0:T(8,128)(2,1)S(1)}, bf16[256,128]{1,0:T(8,128)(2,1)S(1)}, u32[]{:S(2)}, u32[]{:S(2)}) collective-permute-start(bf16[256,128]{1,0:T(8,128)(2,1)S(1)} %get-tuple-element.36), channel_id=1, source_target_pairs={{0,16},{8,24},{16,0},{24,8},{1,17},{9,25},{17,1},{25,9},{2,18},{10... | collective-permute-start | bytes 196616 | tf_op jit(solution)/shard_map/ppermute | solution.py:347
  83.3 0.0 collective-permute-done.14.refs_1_
  83.3 0.0 collective-permute-start.23
  83.3 1.2 %join.1 = bf16[768,512]{1,0:T(8,128)(2,1)} custom-call(bf16[768,256]{1,0:T(8,128)(2,1)S(1)} %add_convert_fusion.1.x.refs_0_, bf16[768,256]{1,0:T(8,128)(2,1)S(1)} %add_convert_fusion.y.refs_0_), custom_call_target="tpu_custom_call" | custom-call | tf_op jit(solution)/shard_map/join/pallas_call | solution.py:221
  84.5 0.0 collective-permute-done.15.refs_2_
  84.5 0.8 collective-permute-done.16.refs_3_
  85.3 4.4 %collective-permute-done.22.refs_6_ = bf16[256,128]{1,0:T(8,128)(2,1)S(1)} collective-permute-done((bf16[256,128]{1,0:T(8,128)(2,1)S(1)}, bf16[256,128]{1,0:T(8,128)(2,1)S(1)}, u32[]{:S(2)}, u32[]{:S(2)}) %collective-permute-start.22) | collective-permute-done | bytes 65568 | tf_op jit(solution)/shard_map/ppermute | solution.py:347
  89.8 0.8 finish.1
  (21 shorter events, 0.0 us)
Async XLA Ops:
  0.6 3.2 %copy-start.3 = (s32[1,512]{1,0:T(1,128)S(1)}, s32[1,512]{1,0:T(1,128)}, u32[]{:S(2)}) copy-start(s32[1,512]{1,0:T(1,128)} %places.3) | copy-start | bytes 6148
  0.6 32.9 %slice-start = ((s8[9437184]{0:T(1024)(128)(4,1)}), s8[4194304]{0:T(1024)(128)(4,1)S(1)}, s32[]{:S(2)}) async-start(s8[9437184]{0:T(1024)(128)(4,1)} %bitcast.5), calls=%async_computation | async-start | bytes 8388608
  0.7 32.9 %slice-start.1 = ((s8[9437184]{0:T(1024)(128)(4,1)}), s8[4194304]{0:T(1024)(128)(4,1)S(1)}, s32[]{:S(2)}) async-start(s8[9437184]{0:T(1024)(128)(4,1)} %bitcast.5), calls=%async_computation.1 | async-start | bytes 8388608
  3.2 30.9 %collective-permute-start = (bf16[768,3072]{1,0:T(8,128)(2,1)S(1)}, bf16[768,3072]{1,0:T(8,128)(2,1)S(1)}, u32[]{:S(2)}, u32[]{:S(2)}) collective-permute-start(bf16[768,3072]{1,0:T(8,128)(2,1)S(1)} %pick.3), channel_id=1, source_target_pairs={{0,1},{1,0},{2,3},{3,2},{4,5},{5,4},{6,7},{7,6},{8,9},{9,8},{10,11... | collective-permute-start | bytes 14155784 | tf_op jit(solution)/shard_map/ppermute | solution.py:301
  3.8 3.5 %copy-start = (bf16[1,512,6144]{2,1,0:T(8,128)(2,1)S(1)}, bf16[1,512,6144]{2,1,0:T(8,128)(2,1)}, u32[]{:S(2)}) copy-start(bf16[1,512,6144]{2,1,0:T(8,128)(2,1)} %param.7) | copy-start | bytes 18874372
  7.3 9.0 %copy-start.1 = (bf16[1,768,512]{2,1,0:T(8,128)(2,1)S(1)}, bf16[1,768,512]{2,1,0:T(8,128)(2,1)}, u32[]{:S(2)}) copy-start(bf16[1,768,512]{2,1,0:T(8,128)(2,1)} %param.6) | copy-start | bytes 2359300
  7.3 26.2 %slice-start.2 = ((s8[9437184]{0:T(1024)(128)(4,1)}), s8[1048576]{0:T(1024)(128)(4,1)S(1)}, s32[]{:S(2)}) async-start(s8[9437184]{0:T(1024)(128)(4,1)} %bitcast.5), calls=%async_computation.2 | async-start | bytes 2097152
  10.6 58.0 %collective-permute-start.9 = (bf16[512,3072]{1,0:T(8,128)(2,1)S(1)}, bf16[512,3072]{1,0:T(8,128)(2,1)S(1)}, u32[]{:S(2)}, u32[]{:S(2)}) collective-permute-start(bf16[512,3072]{1,0:T(8,128)(2,1)S(1)} %select_rows.3), channel_id=1, source_target_pairs={{0,1},{1,0},{2,3},{3,2},{4,5},{5,4},{6,7},{7,6},{8,9},{9,8},{10,11... | collective-permute-start | bytes 9437192 | tf_op jit(solution)/shard_map/ppermute | solution.py:301
  11.9 11.8 %collective-permute-start.1 = (bf16[768,256]{1,0:T(8,128)(2,1)S(1)}, bf16[768,256]{1,0:T(8,128)(2,1)S(1)}, u32[]{:S(2)}, u32[]{:S(2)}) collective-permute-start(bf16[768,256]{1,0:T(8,128)(2,1)S(1)} %chunk.2.refs_0_), channel_id=1, source_target_pairs={{0,2},{1,5},{2,0},{3,7},{4,6},{5,1},{6,4},{7,3},{8,10},{9,13},{10,... | collective-permute-start | bytes 1179656 | tf_op jit(solution)/shard_map/ppermute | solution.py:308
  14.8 12.0 %collective-permute-start.2 = (bf16[768,256]{1,0:T(8,128)(2,1)S(1)}, bf16[768,256]{1,0:T(8,128)(2,1)S(1)}, u32[]{:S(2)}, u32[]{:S(2)}) collective-permute-start(bf16[768,256]{1,0:T(8,128)(2,1)S(1)} %chunk.2.refs_0_), channel_id=1, source_target_pairs={{0,4},{1,3},{2,6},{3,1},{4,0},{5,7},{6,2},{7,5},{8,12},{9,11},{10,... | collective-permute-start | bytes 1179656 | tf_op jit(solution)/shard_map/ppermute | solution.py:308
  16.5 15.3 %collective-permute-start.5 = (bf16[768,256]{1,0:T(8,128)(2,1)S(1)}, bf16[768,256]{1,0:T(8,128)(2,1)S(1)}, u32[]{:S(2)}, u32[]{:S(2)}) collective-permute-start(bf16[768,256]{1,0:T(8,128)(2,1)S(1)} %chunk.3.refs_0_), channel_id=1, source_target_pairs={{0,2},{1,5},{2,0},{3,7},{4,6},{5,1},{6,4},{7,3},{8,10},{9,13},{10,... | collective-permute-start | bytes 1179656 | tf_op jit(solution)/shard_map/ppermute | solution.py:308
  23.8 10.4 %collective-permute-start.3 = (bf16[768,256]{1,0:T(8,128)(2,1)S(1)}, bf16[768,256]{1,0:T(8,128)(2,1)S(1)}, u32[]{:S(2)}, u32[]{:S(2)}) collective-permute-start(bf16[768,256]{1,0:T(8,128)(2,1)S(1)} %collective-permute-done.1.refs_1_), channel_id=1, source_target_pairs={{0,4},{1,3},{2,6},{3,1},{4,0},{5,7},{6,2},{7,5},{8,12},{9,11},{10,... | collective-permute-start | bytes 1179656 | tf_op jit(solution)/shard_map/ppermute | solution.py:308
  26.7 10.2 %collective-permute-start.6 = (bf16[768,256]{1,0:T(8,128)(2,1)S(1)}, bf16[768,256]{1,0:T(8,128)(2,1)S(1)}, u32[]{:S(2)}, u32[]{:S(2)}) collective-permute-start(bf16[768,256]{1,0:T(8,128)(2,1)S(1)} %chunk.3.refs_0_), channel_id=1, source_target_pairs={{0,4},{1,3},{2,6},{3,1},{4,0},{5,7},{6,2},{7,5},{8,12},{9,11},{10,... | collective-permute-start | bytes 1179656 | tf_op jit(solution)/shard_map/ppermute | solution.py:308
  31.8 9.4 %collective-permute-start.7 = (bf16[768,256]{1,0:T(8,128)(2,1)S(1)}, bf16[768,256]{1,0:T(8,128)(2,1)S(1)}, u32[]{:S(2)}, u32[]{:S(2)}) collective-permute-start(bf16[768,256]{1,0:T(8,128)(2,1)S(1)} %collective-permute-done.5.refs_1_), channel_id=1, source_target_pairs={{0,4},{1,3},{2,6},{3,1},{4,0},{5,7},{6,2},{7,5},{8,12},{9,11},{10,... | collective-permute-start | bytes 1179656 | tf_op jit(solution)/shard_map/ppermute | solution.py:308
  36.8 28.4 %slice-start.3 = ((s8[6291456]{0:T(1024)(128)(4,1)}), s8[4194304]{0:T(1024)(128)(4,1)S(1)}, s32[]{:S(2)}) async-start(s8[6291456]{0:T(1024)(128)(4,1)} %bitcast.9), calls=%async_computation.3 | async-start | bytes 8388608
  36.8 28.3 %slice-start.4 = ((s8[6291456]{0:T(1024)(128)(4,1)}), s8[2097152]{0:T(1024)(128)(4,1)S(1)}, s32[]{:S(2)}) async-start(s8[6291456]{0:T(1024)(128)(4,1)} %bitcast.9), calls=%async_computation.4 | async-start | bytes 4194304
  36.8 7.3 %collective-permute-start.4 = (bf16[768,256]{1,0:T(8,128)(2,1)S(1)}, bf16[768,256]{1,0:T(8,128)(2,1)S(1)}, u32[]{:S(2)}, u32[]{:S(2)}) collective-permute-start(bf16[768,256]{1,0:T(8,128)(2,1)S(1)} %get-tuple-element.21), channel_id=1, source_target_pairs={{0,1},{1,0},{2,3},{3,2},{4,5},{5,4},{6,7},{7,6},{8,9},{9,8},{10,11... | collective-permute-start | bytes 1179656 | tf_op jit(solution)/shard_map/ppermute | solution.py:301
  43.8 2.5 %collective-permute-start.8 = (bf16[768,256]{1,0:T(8,128)(2,1)S(1)}, bf16[768,256]{1,0:T(8,128)(2,1)S(1)}, u32[]{:S(2)}, u32[]{:S(2)}) collective-permute-start(bf16[768,256]{1,0:T(8,128)(2,1)S(1)} %get-tuple-element.23), channel_id=1, source_target_pairs={{0,1},{1,0},{2,3},{3,2},{4,5},{5,4},{6,7},{7,6},{8,9},{9,8},{10,11... | collective-permute-start | bytes 1179656 | tf_op jit(solution)/shard_map/ppermute | solution.py:301
  44.2 10.0 %collective-permute-start.10 = (bf16[768,256]{1,0:T(8,128)(2,1)S(1)}, bf16[768,256]{1,0:T(8,128)(2,1)S(1)}, u32[]{:S(2)}, u32[]{:S(2)}) collective-permute-start(bf16[768,256]{1,0:T(8,128)(2,1)S(1)} %add_convert_fusion.1.x.refs_0_), channel_id=1, source_target_pairs={{0,2},{1,5},{2,0},{3,7},{4,6},{5,1},{6,4},{7,3},{8,10},{9,13},{10,... | collective-permute-start | bytes 1179656 | tf_op jit(solution)/shard_map/ppermute | solution.py:308
  46.3 16.3 %collective-permute-start.17 = (bf16[768,256]{1,0:T(8,128)(2,1)S(1)}, bf16[768,256]{1,0:T(8,128)(2,1)S(1)}, u32[]{:S(2)}, u32[]{:S(2)}) collective-permute-start(bf16[768,256]{1,0:T(8,128)(2,1)S(1)} %add_convert_fusion.y.refs_0_), channel_id=1, source_target_pairs={{0,2},{1,5},{2,0},{3,7},{4,6},{5,1},{6,4},{7,3},{8,10},{9,13},{10,... | collective-permute-start | bytes 1179656 | tf_op jit(solution)/shard_map/ppermute | solution.py:308
  47.6 21.0 %collective-permute-start.11 = (bf16[768,256]{1,0:T(8,128)(2,1)S(1)}, bf16[768,256]{1,0:T(8,128)(2,1)S(1)}, u32[]{:S(2)}, u32[]{:S(2)}) collective-permute-start(bf16[768,256]{1,0:T(8,128)(2,1)S(1)} %add_convert_fusion.1.x.refs_0_), channel_id=1, source_target_pairs={{0,4},{1,3},{2,6},{3,1},{4,0},{5,7},{6,2},{7,5},{8,12},{9,11},{10,... | collective-permute-start | bytes 1179656 | tf_op jit(solution)/shard_map/ppermute | solution.py:308
  54.2 14.4 %collective-permute-start.12 = (bf16[768,256]{1,0:T(8,128)(2,1)S(1)}, bf16[768,256]{1,0:T(8,128)(2,1)S(1)}, u32[]{:S(2)}, u32[]{:S(2)}) collective-permute-start(bf16[768,256]{1,0:T(8,128)(2,1)S(1)} %collective-permute-done.10.refs_1_), channel_id=1, source_target_pairs={{0,4},{1,3},{2,6},{3,1},{4,0},{5,7},{6,2},{7,5},{8,12},{9,11},{10,... | collective-permute-start | bytes 1179656 | tf_op jit(solution)/shard_map/ppermute | solution.py:308
  56.7 13.8 %collective-permute-start.19 = (bf16[768,256]{1,0:T(8,128)(2,1)S(1)}, bf16[768,256]{1,0:T(8,128)(2,1)S(1)}, u32[]{:S(2)}, u32[]{:S(2)}) collective-permute-start(bf16[768,256]{1,0:T(8,128)(2,1)S(1)} %add_convert_fusion.y.refs_0_), channel_id=1, source_target_pairs={{0,4},{1,3},{2,6},{3,1},{4,0},{5,7},{6,2},{7,5},{8,12},{9,11},{10,... | collective-permute-start | bytes 1179656 | tf_op jit(solution)/shard_map/ppermute | solution.py:308
  62.6 9.8 %collective-permute-start.18 = (bf16[768,256]{1,0:T(8,128)(2,1)S(1)}, bf16[768,256]{1,0:T(8,128)(2,1)S(1)}, u32[]{:S(2)}, u32[]{:S(2)}) collective-permute-start(bf16[768,256]{1,0:T(8,128)(2,1)S(1)} %collective-permute-done.17.refs_1_), channel_id=1, source_target_pairs={{0,4},{1,3},{2,6},{3,1},{4,0},{5,7},{6,2},{7,5},{8,12},{9,11},{10,... | collective-permute-start | bytes 1179656 | tf_op jit(solution)/shard_map/ppermute | solution.py:308
  70.4 3.2 %collective-permute-start.13 = (bf16[512,256]{1,0:T(8,128)(2,1)S(1)}, bf16[512,256]{1,0:T(8,128)(2,1)S(1)}, u32[]{:S(2)}, u32[]{:S(2)}) collective-permute-start(bf16[512,256]{1,0:T(8,128)(2,1)S(1)} %get-tuple-element.25), channel_id=1, source_target_pairs={{0,1},{1,0},{2,3},{3,2},{4,5},{5,4},{6,7},{7,6},{8,9},{9,8},{10,11... | collective-permute-start | bytes 786440 | tf_op jit(solution)/shard_map/ppermute | solution.py:301
  72.4 17.4 %copy-start.2 = (f32[512,128]{1,0:T(8,128)S(1)}, f32[512,128]{1,0:T(8,128)}, u32[]{:S(2)}) copy-start(f32[512,128]{1,0:T(8,128)} %rhs.1) | copy-start | bytes 786436
  73.0 5.6 %collective-permute-start.20 = (bf16[512,256]{1,0:T(8,128)(2,1)S(1)}, bf16[512,256]{1,0:T(8,128)(2,1)S(1)}, u32[]{:S(2)}, u32[]{:S(2)}) collective-permute-start(bf16[512,256]{1,0:T(8,128)(2,1)S(1)} %get-tuple-element.33), channel_id=1, source_target_pairs={{0,1},{1,0},{2,3},{3,2},{4,5},{5,4},{6,7},{7,6},{8,9},{9,8},{10,11... | collective-permute-start | bytes 786440 | tf_op jit(solution)/shard_map/ppermute | solution.py:301
  73.8 9.5 %collective-permute-start.14 = (bf16[256,128]{1,0:T(8,128)(2,1)S(1)}, bf16[256,128]{1,0:T(8,128)(2,1)S(1)}, u32[]{:S(2)}, u32[]{:S(2)}) collective-permute-start(bf16[256,128]{1,0:T(8,128)(2,1)S(1)} %get-tuple-element.27), channel_id=1, source_target_pairs={{0,8},{8,0},{16,24},{24,16},{1,9},{9,1},{17,25},{25,17},{2,10},{10... | collective-permute-start | bytes 196616 | tf_op jit(solution)/shard_map/ppermute | solution.py:347
  76.0 8.5 %collective-permute-start.15 = (bf16[256,128]{1,0:T(8,128)(2,1)S(1)}, bf16[256,128]{1,0:T(8,128)(2,1)S(1)}, u32[]{:S(2)}, u32[]{:S(2)}) collective-permute-start(bf16[256,128]{1,0:T(8,128)(2,1)S(1)} %get-tuple-element.28), channel_id=1, source_target_pairs={{0,16},{8,24},{16,0},{24,8},{1,17},{9,25},{17,1},{25,9},{2,18},{10... | collective-permute-start | bytes 196616 | tf_op jit(solution)/shard_map/ppermute | solution.py:347
  78.6 6.8 %collective-permute-start.16 = (bf16[256,128]{1,0:T(8,128)(2,1)S(1)}, bf16[256,128]{1,0:T(8,128)(2,1)S(1)}, u32[]{:S(2)}, u32[]{:S(2)}) collective-permute-start(bf16[256,128]{1,0:T(8,128)(2,1)S(1)} %get-tuple-element.29), channel_id=1, source_target_pairs={{0,24},{8,16},{16,8},{24,0},{1,25},{9,17},{17,9},{25,1},{2,26},{10... | collective-permute-start | bytes 196616 | tf_op jit(solution)/shard_map/ppermute | solution.py:347
  78.8 6.5 %collective-permute-start.21 = (bf16[256,128]{1,0:T(8,128)(2,1)S(1)}, bf16[256,128]{1,0:T(8,128)(2,1)S(1)}, u32[]{:S(2)}, u32[]{:S(2)}) collective-permute-start(bf16[256,128]{1,0:T(8,128)(2,1)S(1)} %get-tuple-element.35), channel_id=1, source_target_pairs={{0,8},{8,0},{16,24},{24,16},{1,9},{9,1},{17,25},{25,17},{2,10},{10... | collective-permute-start | bytes 196616 | tf_op jit(solution)/shard_map/ppermute | solution.py:347
  79.8 10.0 %collective-permute-start.22 = (bf16[256,128]{1,0:T(8,128)(2,1)S(1)}, bf16[256,128]{1,0:T(8,128)(2,1)S(1)}, u32[]{:S(2)}, u32[]{:S(2)}) collective-permute-start(bf16[256,128]{1,0:T(8,128)(2,1)S(1)} %get-tuple-element.36), channel_id=1, source_target_pairs={{0,16},{8,24},{16,0},{24,8},{1,17},{9,25},{17,1},{25,9},{2,18},{10... | collective-permute-start | bytes 196616 | tf_op jit(solution)/shard_map/ppermute | solution.py:347
  83.3 6.5 %collective-permute-start.23 = (bf16[256,128]{1,0:T(8,128)(2,1)S(1)}, bf16[256,128]{1,0:T(8,128)(2,1)S(1)}, u32[]{:S(2)}, u32[]{:S(2)}) collective-permute-start(bf16[256,128]{1,0:T(8,128)(2,1)S(1)} %get-tuple-element.37), channel_id=1, source_target_pairs={{0,24},{8,16},{16,8},{24,0},{1,25},{9,17},{17,9},{25,1},{2,26},{10... | collective-permute-start | bytes 196616 | tf_op jit(solution)/shard_map/ppermute | solution.py:347

commit v6 on v5

--- a/solution.py
+++ b/solution.py
@@ -146,6 +146,23 @@
     return pltpu.roll(x, x.shape[1] // 2, 1)
 
 
+def last_kernel(column, block, piece, early, out):
+    depth = piece.shape[0]
+    value = jnp.dot(block[:, column : column + depth], piece[...], preferred_element_type=F32)
+    out[...] = (early[...] + value).astype(out.dtype)
+
+
+def last_part(block, piece, early, place, kind):
+    return pl.pallas_call(
+        functools.partial(last_kernel, place * piece.shape[0]),
+        out_shape=jax.ShapeDtypeStruct(early.shape, kind),
+        in_specs=[VMEM] * 3,
+        out_specs=VMEM,
+        compiler_params=pltpu.CompilerParams(vmem_limit_bytes=8 << 20),
+        name="last_part",
+    )(block, piece, early)
+
+
 def low_lanes(shape):
     return lax.broadcasted_iota(jnp.int32, shape, 1) < shape[1] // 2
 
@@ -336,11 +353,13 @@
     groups = []
     for c, y in enumerate(solved):
         pieces = gather(y)
-        sums = ()
         if c:
-            sums = partials(*cpl, pieces[:-1], other_type=F32)
-        first = len(pieces) - 1 if c else 0
-        own, other = partials(*cpl, pieces[first:], first, sums)
+            own, other = partials(*cpl, pieces[:-1], other_type=F32)
+            place = len(pieces) - 1
+            other = last_part(cpl[1], pieces[-1], other, place, BF16)
+            own = last_part(cpl[0], pieces[-1], own, place, F32)
+        else:
+            own, other = partials(*cpl, pieces)
         other = partner(other)
         group = list(split(own, other, leaves))
         for d in range(1, leaves):

time: 90.8 us -> 90.8 us (level)
    pallas_call x5 -> x4, Pallas kernels: 8.92 us -> 8.35 us  [partials(): pl.pallas_call(functools.partial(partial_kernel, n, first, bool(sums)), o...]
where the time goes in v6:
time: 90.8 us; the launch traced here: 90.7 us
  waiting for transfers between devices  32 us (35%)
  starting transfers between devices  31.2 us (34%)
  Pallas kernels  22.9 us (25%)
  local copies, waits for them, and re-layouts  3.58 us (4%)
    ppermute x12, waiting for transfers between devices, gather(): pieces.append(lax.ppermute(pieces[p], 'row', pairs))  26.9 us
    ppermute x12, starting transfers between devices, gather(): pieces.append(lax.ppermute(pieces[p], 'row', pairs))  20.2 us
    ppermute x6, starting transfers between devices, on_device(): lax.ppermute(group[d], 'leaf', [(j, j ^ d) for j in range(leaves)])  9.28 us
    pallas_call x4, Pallas kernels, partials(): pl.pallas_call(functools.partial(partial_kernel, n, first, bool(sums)), o...  8.35 us
    pallas_call x2, Pallas kernels, select_rows(): pl.pallas_call(functools.partial(select_kernel, masks, other), out_shape=...  6.65 us
    ppermute x6, waiting for transfers between devices, on_device(): lax.ppermute(group[d], 'leaf', [(j, j ^ d) for j in range(leaves)])  5.08 us
    unnamed x18, local copies, waits for them, and re-layouts  3.58 us
    pallas_call x2, Pallas kernels, pick(): pl.pallas_call(functools.partial(pick_kernel, masks, other), out_shape=ja...  3.15 us
  transfers between devices with their start and end apart: 24, of which 10 were waited for; matrix products, arithmetic and copies ran while one was open for 0% of the time, Pallas kernels for 21%

profile of v6, /device:TPU:0, one launch (start us, length us, event | category | flops | bytes accessed | tf_op | source)
XLA Modules:
  0.0 90.7 jit_solution(9914983431177499149)
XLA Ops:
  0.6 0.0 slice-start
  0.7 0.0 slice-start.1
  0.7 2.6 %pick.3 = bf16[768,3072]{1,0:T(8,128)(2,1)S(1)} custom-call(bf16[768,6144]{1,0:T(8,128)(2,1)} %bitcast.4), custom_call_target="tpu_custom_call" | custom-call | tf_op jit(solution)/shard_map/pick/pallas_call | solution.py:65
  3.2 0.6 collective-permute-start
  3.8 3.5 %copy-done = bf16[1,512,6144]{2,1,0:T(8,128)(2,1)S(1)} copy-done((bf16[1,512,6144]{2,1,0:T(8,128)(2,1)S(1)}, bf16[1,512,6144]{2,1,0:T(8,128)(2,1)}, u32[]{:S(2)}) %copy-start) | copy-done | bytes 6291480
  7.3 3.2 %select_rows.3 = bf16[512,3072]{1,0:T(8,128)(2,1)S(1)} custom-call(s32[1,512]{1,0:T(1,128)S(1)} %copy-done.3, bf16[512,6144]{1,0:T(8,128)(2,1)S(1)} %bitcast.8), custom_call_target="tpu_custom_call" | custom-call | tf_op jit(solution)/shard_map/select_rows/pallas_call | solution.py:100
  10.6 0.1 collective-permute-start.9
  10.7 1.3 %chunk.2.refs_0_ = bf16[768,256]{1,0:T(8,128)(2,1)S(1)} custom-call(bf16[768,512]{1,0:T(8,128)(2,1)} %bitcast.12), custom_call_target="tpu_custom_call" | custom-call | tf_op jit(solution)/shard_map/chunk/pallas_call | solution.py:213
  11.9 2.8 %collective-permute-start.1 = (bf16[768,256]{1,0:T(8,128)(2,1)S(1)}, bf16[768,256]{1,0:T(8,128)(2,1)S(1)}, u32[]{:S(2)}, u32[]{:S(2)}) collective-permute-start(bf16[768,256]{1,0:T(8,128)(2,1)S(1)} %chunk.2.refs_0_), channel_id=1, source_target_pairs={{0,2},{1,5},{2,0},{3,7},{4,6},{5,1},{6,4},{7,3},{8,10},{9,13},{10,... | collective-permute-start | bytes 1179656 | tf_op jit(solution)/shard_map/ppermute | solution.py:325
  14.8 1.5 %collective-permute-start.2 = (bf16[768,256]{1,0:T(8,128)(2,1)S(1)}, bf16[768,256]{1,0:T(8,128)(2,1)S(1)}, u32[]{:S(2)}, u32[]{:S(2)}) collective-permute-start(bf16[768,256]{1,0:T(8,128)(2,1)S(1)} %chunk.2.refs_0_), channel_id=1, source_target_pairs={{0,4},{1,3},{2,6},{3,1},{4,0},{5,7},{6,2},{7,5},{8,12},{9,11},{10,... | collective-permute-start | bytes 1179656 | tf_op jit(solution)/shard_map/ppermute | solution.py:325
  16.3 0.2 chunk.3.refs_0_
  16.5 0.6 collective-permute-start.5
  17.1 6.7 %collective-permute-done.1.refs_1_ = bf16[768,256]{1,0:T(8,128)(2,1)S(1)} collective-permute-done((bf16[768,256]{1,0:T(8,128)(2,1)S(1)}, bf16[768,256]{1,0:T(8,128)(2,1)S(1)}, u32[]{:S(2)}, u32[]{:S(2)}) %collective-permute-start.1) | collective-permute-done | bytes 393248 | tf_op jit(solution)/shard_map/ppermute | solution.py:325
  23.8 2.4 %collective-permute-start.3 = (bf16[768,256]{1,0:T(8,128)(2,1)S(1)}, bf16[768,256]{1,0:T(8,128)(2,1)S(1)}, u32[]{:S(2)}, u32[]{:S(2)}) collective-permute-start(bf16[768,256]{1,0:T(8,128)(2,1)S(1)} %collective-permute-done.1.refs_1_), channel_id=1, source_target_pairs={{0,4},{1,3},{2,6},{3,1},{4,0},{5,7},{6,2},{7,5},{8,12},{9,11},{10,... | collective-permute-start | bytes 1179656 | tf_op jit(solution)/shard_map/ppermute | solution.py:325
  26.1 0.6 collective-permute-done.2.refs_2_
  26.7 1.5 %collective-permute-start.6 = (bf16[768,256]{1,0:T(8,128)(2,1)S(1)}, bf16[768,256]{1,0:T(8,128)(2,1)S(1)}, u32[]{:S(2)}, u32[]{:S(2)}) collective-permute-start(bf16[768,256]{1,0:T(8,128)(2,1)S(1)} %chunk.3.refs_0_), channel_id=1, source_target_pairs={{0,4},{1,3},{2,6},{3,1},{4,0},{5,7},{6,2},{7,5},{8,12},{9,11},{10,... | collective-permute-start | bytes 1179656 | tf_op jit(solution)/shard_map/ppermute | solution.py:325
  28.3 3.5 %collective-permute-done.5.refs_1_ = bf16[768,256]{1,0:T(8,128)(2,1)S(1)} collective-permute-done((bf16[768,256]{1,0:T(8,128)(2,1)S(1)}, bf16[768,256]{1,0:T(8,128)(2,1)S(1)}, u32[]{:S(2)}, u32[]{:S(2)}) %collective-permute-start.5) | collective-permute-done | bytes 393248 | tf_op jit(solution)/shard_map/ppermute | solution.py:325
  31.8 1.8 %collective-permute-start.7 = (bf16[768,256]{1,0:T(8,128)(2,1)S(1)}, bf16[768,256]{1,0:T(8,128)(2,1)S(1)}, u32[]{:S(2)}, u32[]{:S(2)}) collective-permute-start(bf16[768,256]{1,0:T(8,128)(2,1)S(1)} %collective-permute-done.5.refs_1_), channel_id=1, source_target_pairs={{0,4},{1,3},{2,6},{3,1},{4,0},{5,7},{6,2},{7,5},{8,12},{9,11},{10,... | collective-permute-start | bytes 1179656 | tf_op jit(solution)/shard_map/ppermute | solution.py:325
  33.5 0.6 pick.2.keep
  34.1 0.0 collective-permute-done.3.refs_3_
  34.2 2.6 %partials.4 = (f32[768,256]{1,0:T(8,128)S(1)}, bf16[768,256]{1,0:T(8,128)(2,1)S(1)}) custom-call(bf16[768,3072]{1,0:T(8,128)(2,1)S(1)} %pick.2.keep, bf16[768,3072]{1,0:T(8,128)(2,1)S(1)} %collective-permute-done.swap, bf16[768,256]{1,0:T(8,128)(2,1)S(1)} %chunk.2.refs_0_, bf16[768,256]{1,0:T(8,128)(2,1)S(1)} %collective-permute-done.1.refs_1_, ...), custom_call_target="tpu_custom_call" | custom-call | tf_op jit(solution)/shard_map/partials/pallas_call | solution.py:131
  36.8 0.0 slice-start.3
  36.8 0.0 slice-start.4
  36.8 0.1 collective-permute-start.4
  36.9 0.1 collective-permute-done.6.refs_2_
  37.0 4.2 %collective-permute-done.7.refs_3_ = bf16[768,256]{1,0:T(8,128)(2,1)S(1)} collective-permute-done((bf16[768,256]{1,0:T(8,128)(2,1)S(1)}, bf16[768,256]{1,0:T(8,128)(2,1)S(1)}, u32[]{:S(2)}, u32[]{:S(2)}) %collective-permute-start.7) | collective-permute-done | bytes 393248 | tf_op jit(solution)/shard_map/ppermute | solution.py:325
  41.2 2.6 %partials.5 = (f32[768,256]{1,0:T(8,128)S(1)}, bf16[768,256]{1,0:T(8,128)(2,1)S(1)}) custom-call(bf16[768,3072]{1,0:T(8,128)(2,1)S(1)} %pick.2.keep, bf16[768,3072]{1,0:T(8,128)(2,1)S(1)} %collective-permute-done.swap, bf16[768,256]{1,0:T(8,128)(2,1)S(1)} %chunk.3.refs_0_, bf16[768,256]{1,0:T(8,128)(2,1)S(1)} %collective-permute-done.5.refs_1_, ...), custom_call_target="tpu_custom_call" | custom-call | tf_op jit(solution)/shard_map/partials/pallas_call | solution.py:131
  43.8 0.3 collective-permute-start.8
  44.1 0.0 collective-permute-done.4
  44.1 0.1 add_convert_fusion.1.x.refs_0_
  44.2 2.1 %collective-permute-start.10 = (bf16[768,256]{1,0:T(8,128)(2,1)S(1)}, bf16[768,256]{1,0:T(8,128)(2,1)S(1)}, u32[]{:S(2)}, u32[]{:S(2)}) collective-permute-start(bf16[768,256]{1,0:T(8,128)(2,1)S(1)} %add_convert_fusion.1.x.refs_0_), channel_id=1, source_target_pairs={{0,2},{1,5},{2,0},{3,7},{4,6},{5,1},{6,4},{7,3},{8,10},{9,13},{10,... | collective-permute-start | bytes 1179656 | tf_op jit(solution)/shard_map/ppermute | solution.py:325
  46.2 0.1 add_convert_fusion.y.refs_0_
  46.3 1.3 %collective-permute-start.17 = (bf16[768,256]{1,0:T(8,128)(2,1)S(1)}, bf16[768,256]{1,0:T(8,128)(2,1)S(1)}, u32[]{:S(2)}, u32[]{:S(2)}) collective-permute-start(bf16[768,256]{1,0:T(8,128)(2,1)S(1)} %add_convert_fusion.y.refs_0_), channel_id=1, source_target_pairs={{0,2},{1,5},{2,0},{3,7},{4,6},{5,1},{6,4},{7,3},{8,10},{9,13},{10,... | collective-permute-start | bytes 1179656 | tf_op jit(solution)/shard_map/ppermute | solution.py:325
  47.6 1.3 %collective-permute-start.11 = (bf16[768,256]{1,0:T(8,128)(2,1)S(1)}, bf16[768,256]{1,0:T(8,128)(2,1)S(1)}, u32[]{:S(2)}, u32[]{:S(2)}) collective-permute-start(bf16[768,256]{1,0:T(8,128)(2,1)S(1)} %add_convert_fusion.1.x.refs_0_), channel_id=1, source_target_pairs={{0,4},{1,3},{2,6},{3,1},{4,0},{5,7},{6,2},{7,5},{8,12},{9,11},{10,... | collective-permute-start | bytes 1179656 | tf_op jit(solution)/shard_map/ppermute | solution.py:325
  48.9 5.3 %collective-permute-done.10.refs_1_ = bf16[768,256]{1,0:T(8,128)(2,1)S(1)} collective-permute-done((bf16[768,256]{1,0:T(8,128)(2,1)S(1)}, bf16[768,256]{1,0:T(8,128)(2,1)S(1)}, u32[]{:S(2)}, u32[]{:S(2)}) %collective-permute-start.10) | collective-permute-done | bytes 393248 | tf_op jit(solution)/shard_map/ppermute | solution.py:325
  54.2 2.5 %collective-permute-start.12 = (bf16[768,256]{1,0:T(8,128)(2,1)S(1)}, bf16[768,256]{1,0:T(8,128)(2,1)S(1)}, u32[]{:S(2)}, u32[]{:S(2)}) collective-permute-start(bf16[768,256]{1,0:T(8,128)(2,1)S(1)} %collective-permute-done.10.refs_1_), channel_id=1, source_target_pairs={{0,4},{1,3},{2,6},{3,1},{4,0},{5,7},{6,2},{7,5},{8,12},{9,11},{10,... | collective-permute-start | bytes 1179656 | tf_op jit(solution)/shard_map/ppermute | solution.py:325
  56.7 0.0 collective-permute-start.19
  56.7 5.9 %collective-permute-done.17.refs_1_ = bf16[768,256]{1,0:T(8,128)(2,1)S(1)} collective-permute-done((bf16[768,256]{1,0:T(8,128)(2,1)S(1)}, bf16[768,256]{1,0:T(8,128)(2,1)S(1)}, u32[]{:S(2)}, u32[]{:S(2)}) %collective-permute-start.17) | collective-permute-done | bytes 393248 | tf_op jit(solution)/shard_map/ppermute | solution.py:325
  62.6 2.5 %collective-permute-start.18 = (bf16[768,256]{1,0:T(8,128)(2,1)S(1)}, bf16[768,256]{1,0:T(8,128)(2,1)S(1)}, u32[]{:S(2)}, u32[]{:S(2)}) collective-permute-start(bf16[768,256]{1,0:T(8,128)(2,1)S(1)} %collective-permute-done.17.refs_1_), channel_id=1, source_target_pairs={{0,4},{1,3},{2,6},{3,1},{4,0},{5,7},{6,2},{7,5},{8,12},{9,11},{10,... | collective-permute-start | bytes 1179656 | tf_op jit(solution)/shard_map/ppermute | solution.py:325
  65.1 3.4 %select_rows.2.keep.block = bf16[512,3072]{1,0:T(8,128)(2,1)S(1)} custom-call(s32[1,512]{1,0:T(1,128)S(1)} %copy-done.3, bf16[512,6144]{1,0:T(8,128)(2,1)S(1)} %bitcast.11), custom_call_target="tpu_custom_call" | custom-call | tf_op jit(solution)/shard_map/select_rows/pallas_call | solution.py:100
  68.5 0.0 collective-permute-done.11.refs_2_
  68.6 0.0 collective-permute-done.12.refs_3_
  68.6 1.8 %partials.6 = (f32[512,256]{1,0:T(8,128)S(1)}, bf16[512,256]{1,0:T(8,128)(2,1)S(1)}) custom-call(bf16[512,3072]{1,0:T(8,128)(2,1)S(1)} %select_rows.2.keep.block, bf16[512,3072]{1,0:T(8,128)(2,1)S(1)} %collective-permute-done.9.swap.block, bf16[768,256]{1,0:T(8,128)(2,1)S(1)} %add_convert_fusion.1.x.refs_0_, ...), custom_call_target="tpu_custom_call" | custom-call | tf_op jit(solution)/shard_map/partials/pallas_call | solution.py:131
  70.4 0.1 collective-permute-start.13
  70.4 0.0 collective-permute-done.19.refs_2_
  70.5 1.4 %partials.7 = (f32[512,256]{1,0:T(8,128)S(1)}, f32[512,256]{1,0:T(8,128)S(1)}) custom-call(bf16[512,3072]{1,0:T(8,128)(2,1)S(1)} %select_rows.2.keep.block, bf16[512,3072]{1,0:T(8,128)(2,1)S(1)} %collective-permute-done.9.swap.block, bf16[768,256]{1,0:T(8,128)(2,1)S(1)} %add_convert_fusion.y.refs_0_, bf16[768,256]{1,0:T(8,128)(2,1)S(1)} %collective-permute-done.17.refs_1_, ...), custom_call_target="tpu_custom_call" | custom-call | tf_op jit(solution)/shard_map/partials/pallas_call | solution.py:131
  71.8 0.5 collective-permute-done.18.piece
  72.4 0.4 last_part.3
  72.8 0.0 copy-start.2
  72.8 0.6 collective-permute-start.20
  73.3 0.0 collective-permute-done.13.other
  73.3 0.3 split.2
  73.6 2.2 %collective-permute-start.14 = (bf16[256,128]{1,0:T(8,128)(2,1)S(1)}, bf16[256,128]{1,0:T(8,128)(2,1)S(1)}, u32[]{:S(2)}, u32[]{:S(2)}) collective-permute-start(bf16[256,128]{1,0:T(8,128)(2,1)S(1)} %get-tuple-element.25), channel_id=1, source_target_pairs={{0,8},{8,0},{16,24},{24,16},{1,9},{9,1},{17,25},{25,17},{2,10},{10... | collective-permute-start | bytes 196616 | tf_op jit(solution)/shard_map/ppermute | solution.py:366
  75.8 0.4 last_part.2.own
  76.2 2.6 %collective-permute-start.15 = (bf16[256,128]{1,0:T(8,128)(2,1)S(1)}, bf16[256,128]{1,0:T(8,128)(2,1)S(1)}, u32[]{:S(2)}, u32[]{:S(2)}) collective-permute-start(bf16[256,128]{1,0:T(8,128)(2,1)S(1)} %get-tuple-element.26), channel_id=1, source_target_pairs={{0,16},{8,24},{16,0},{24,8},{1,17},{9,25},{17,1},{25,9},{2,18},{10... | collective-permute-start | bytes 196616 | tf_op jit(solution)/shard_map/ppermute | solution.py:366
  78.8 0.0 collective-permute-start.16
  78.8 0.3 split.3
  79.1 1.0 %collective-permute-start.21 = (bf16[256,128]{1,0:T(8,128)(2,1)S(1)}, bf16[256,128]{1,0:T(8,128)(2,1)S(1)}, u32[]{:S(2)}, u32[]{:S(2)}) collective-permute-start(bf16[256,128]{1,0:T(8,128)(2,1)S(1)} %get-tuple-element.31), channel_id=1, source_target_pairs={{0,8},{8,0},{16,24},{24,16},{1,9},{9,1},{17,25},{25,17},{2,10},{10... | collective-permute-start | bytes 196616 | tf_op jit(solution)/shard_map/ppermute | solution.py:366
  80.0 3.5 %collective-permute-start.22 = (bf16[256,128]{1,0:T(8,128)(2,1)S(1)}, bf16[256,128]{1,0:T(8,128)(2,1)S(1)}, u32[]{:S(2)}, u32[]{:S(2)}) collective-permute-start(bf16[256,128]{1,0:T(8,128)(2,1)S(1)} %get-tuple-element.32), channel_id=1, source_target_pairs={{0,16},{8,24},{16,0},{24,8},{1,17},{9,25},{17,1},{25,9},{2,18},{10... | collective-permute-start | bytes 196616 | tf_op jit(solution)/shard_map/ppermute | solution.py:366
  83.5 0.0 collective-permute-start.23
  83.5 1.2 %join.1 = bf16[768,512]{1,0:T(8,128)(2,1)} custom-call(bf16[768,256]{1,0:T(8,128)(2,1)S(1)} %add_convert_fusion.1.x.refs_0_, bf16[768,256]{1,0:T(8,128)(2,1)S(1)} %add_convert_fusion.y.refs_0_), custom_call_target="tpu_custom_call" | custom-call | tf_op jit(solution)/shard_map/join/pallas_call | solution.py:238
  84.8 0.8 collective-permute-done.16.refs_3_
  85.6 4.2 %collective-permute-done.22.refs_6_ = bf16[256,128]{1,0:T(8,128)(2,1)S(1)} collective-permute-done((bf16[256,128]{1,0:T(8,128)(2,1)S(1)}, bf16[256,128]{1,0:T(8,128)(2,1)S(1)}, u32[]{:S(2)}, u32[]{:S(2)}) %collective-permute-start.22) | collective-permute-done | bytes 65568 | tf_op jit(solution)/shard_map/ppermute | solution.py:366
  89.8 0.8 finish.1
  (22 shorter events, 0.0 us)
Async XLA Ops:
  0.6 3.2 %copy-start.3 = (s32[1,512]{1,0:T(1,128)S(1)}, s32[1,512]{1,0:T(1,128)}, u32[]{:S(2)}) copy-start(s32[1,512]{1,0:T(1,128)} %places.3) | copy-start | bytes 6148
  0.6 32.9 %slice-start = ((s8[9437184]{0:T(1024)(128)(4,1)}), s8[4194304]{0:T(1024)(128)(4,1)S(1)}, s32[]{:S(2)}) async-start(s8[9437184]{0:T(1024)(128)(4,1)} %bitcast.5), calls=%async_computation | async-start | bytes 8388608
  0.7 32.9 %slice-start.1 = ((s8[9437184]{0:T(1024)(128)(4,1)}), s8[4194304]{0:T(1024)(128)(4,1)S(1)}, s32[]{:S(2)}) async-start(s8[9437184]{0:T(1024)(128)(4,1)} %bitcast.5), calls=%async_computation.1 | async-start | bytes 8388608
  3.2 30.9 %collective-permute-start = (bf16[768,3072]{1,0:T(8,128)(2,1)S(1)}, bf16[768,3072]{1,0:T(8,128)(2,1)S(1)}, u32[]{:S(2)}, u32[]{:S(2)}) collective-permute-start(bf16[768,3072]{1,0:T(8,128)(2,1)S(1)} %pick.3), channel_id=1, source_target_pairs={{0,1},{1,0},{2,3},{3,2},{4,5},{5,4},{6,7},{7,6},{8,9},{9,8},{10,11... | collective-permute-start | bytes 14155784 | tf_op jit(solution)/shard_map/ppermute | solution.py:318
  3.8 3.5 %copy-start = (bf16[1,512,6144]{2,1,0:T(8,128)(2,1)S(1)}, bf16[1,512,6144]{2,1,0:T(8,128)(2,1)}, u32[]{:S(2)}) copy-start(bf16[1,512,6144]{2,1,0:T(8,128)(2,1)} %param.7) | copy-start | bytes 18874372
  7.3 9.0 %copy-start.1 = (bf16[1,768,512]{2,1,0:T(8,128)(2,1)S(1)}, bf16[1,768,512]{2,1,0:T(8,128)(2,1)}, u32[]{:S(2)}) copy-start(bf16[1,768,512]{2,1,0:T(8,128)(2,1)} %param.6) | copy-start | bytes 2359300
  7.3 26.2 %slice-start.2 = ((s8[9437184]{0:T(1024)(128)(4,1)}), s8[1048576]{0:T(1024)(128)(4,1)S(1)}, s32[]{:S(2)}) async-start(s8[9437184]{0:T(1024)(128)(4,1)} %bitcast.5), calls=%async_computation.2 | async-start | bytes 2097152
  10.6 58.0 %collective-permute-start.9 = (bf16[512,3072]{1,0:T(8,128)(2,1)S(1)}, bf16[512,3072]{1,0:T(8,128)(2,1)S(1)}, u32[]{:S(2)}, u32[]{:S(2)}) collective-permute-start(bf16[512,3072]{1,0:T(8,128)(2,1)S(1)} %select_rows.3), channel_id=1, source_target_pairs={{0,1},{1,0},{2,3},{3,2},{4,5},{5,4},{6,7},{7,6},{8,9},{9,8},{10,11... | collective-permute-start | bytes 9437192 | tf_op jit(solution)/shard_map/ppermute | solution.py:318
  11.9 11.8 %collective-permute-start.1 = (bf16[768,256]{1,0:T(8,128)(2,1)S(1)}, bf16[768,256]{1,0:T(8,128)(2,1)S(1)}, u32[]{:S(2)}, u32[]{:S(2)}) collective-permute-start(bf16[768,256]{1,0:T(8,128)(2,1)S(1)} %chunk.2.refs_0_), channel_id=1, source_target_pairs={{0,2},{1,5},{2,0},{3,7},{4,6},{5,1},{6,4},{7,3},{8,10},{9,13},{10,... | collective-permute-start | bytes 1179656 | tf_op jit(solution)/shard_map/ppermute | solution.py:325
  14.8 12.0 %collective-permute-start.2 = (bf16[768,256]{1,0:T(8,128)(2,1)S(1)}, bf16[768,256]{1,0:T(8,128)(2,1)S(1)}, u32[]{:S(2)}, u32[]{:S(2)}) collective-permute-start(bf16[768,256]{1,0:T(8,128)(2,1)S(1)} %chunk.2.refs_0_), channel_id=1, source_target_pairs={{0,4},{1,3},{2,6},{3,1},{4,0},{5,7},{6,2},{7,5},{8,12},{9,11},{10,... | collective-permute-start | bytes 1179656 | tf_op jit(solution)/shard_map/ppermute | solution.py:325
  16.5 15.3 %collective-permute-start.5 = (bf16[768,256]{1,0:T(8,128)(2,1)S(1)}, bf16[768,256]{1,0:T(8,128)(2,1)S(1)}, u32[]{:S(2)}, u32[]{:S(2)}) collective-permute-start(bf16[768,256]{1,0:T(8,128)(2,1)S(1)} %chunk.3.refs_0_), channel_id=1, source_target_pairs={{0,2},{1,5},{2,0},{3,7},{4,6},{5,1},{6,4},{7,3},{8,10},{9,13},{10,... | collective-permute-start | bytes 1179656 | tf_op jit(solution)/shard_map/ppermute | solution.py:325
  23.8 10.4 %collective-permute-start.3 = (bf16[768,256]{1,0:T(8,128)(2,1)S(1)}, bf16[768,256]{1,0:T(8,128)(2,1)S(1)}, u32[]{:S(2)}, u32[]{:S(2)}) collective-permute-start(bf16[768,256]{1,0:T(8,128)(2,1)S(1)} %collective-permute-done.1.refs_1_), channel_id=1, source_target_pairs={{0,4},{1,3},{2,6},{3,1},{4,0},{5,7},{6,2},{7,5},{8,12},{9,11},{10,... | collective-permute-start | bytes 1179656 | tf_op jit(solution)/shard_map/ppermute | solution.py:325
  26.7 10.2 %collective-permute-start.6 = (bf16[768,256]{1,0:T(8,128)(2,1)S(1)}, bf16[768,256]{1,0:T(8,128)(2,1)S(1)}, u32[]{:S(2)}, u32[]{:S(2)}) collective-permute-start(bf16[768,256]{1,0:T(8,128)(2,1)S(1)} %chunk.3.refs_0_), channel_id=1, source_target_pairs={{0,4},{1,3},{2,6},{3,1},{4,0},{5,7},{6,2},{7,5},{8,12},{9,11},{10,... | collective-permute-start | bytes 1179656 | tf_op jit(solution)/shard_map/ppermute | solution.py:325
  31.8 9.4 %collective-permute-start.7 = (bf16[768,256]{1,0:T(8,128)(2,1)S(1)}, bf16[768,256]{1,0:T(8,128)(2,1)S(1)}, u32[]{:S(2)}, u32[]{:S(2)}) collective-permute-start(bf16[768,256]{1,0:T(8,128)(2,1)S(1)} %collective-permute-done.5.refs_1_), channel_id=1, source_target_pairs={{0,4},{1,3},{2,6},{3,1},{4,0},{5,7},{6,2},{7,5},{8,12},{9,11},{10,... | collective-permute-start | bytes 1179656 | tf_op jit(solution)/shard_map/ppermute | solution.py:325
  36.8 28.4 %slice-start.3 = ((s8[6291456]{0:T(1024)(128)(4,1)}), s8[4194304]{0:T(1024)(128)(4,1)S(1)}, s32[]{:S(2)}) async-start(s8[6291456]{0:T(1024)(128)(4,1)} %bitcast.9), calls=%async_computation.3 | async-start | bytes 8388608
  36.8 28.3 %slice-start.4 = ((s8[6291456]{0:T(1024)(128)(4,1)}), s8[2097152]{0:T(1024)(128)(4,1)S(1)}, s32[]{:S(2)}) async-start(s8[6291456]{0:T(1024)(128)(4,1)} %bitcast.9), calls=%async_computation.4 | async-start | bytes 4194304
  36.8 7.3 %collective-permute-start.4 = (bf16[768,256]{1,0:T(8,128)(2,1)S(1)}, bf16[768,256]{1,0:T(8,128)(2,1)S(1)}, u32[]{:S(2)}, u32[]{:S(2)}) collective-permute-start(bf16[768,256]{1,0:T(8,128)(2,1)S(1)} %get-tuple-element.19), channel_id=1, source_target_pairs={{0,1},{1,0},{2,3},{3,2},{4,5},{5,4},{6,7},{7,6},{8,9},{9,8},{10,11... | collective-permute-start | bytes 1179656 | tf_op jit(solution)/shard_map/ppermute | solution.py:318
  43.8 2.5 %collective-permute-start.8 = (bf16[768,256]{1,0:T(8,128)(2,1)S(1)}, bf16[768,256]{1,0:T(8,128)(2,1)S(1)}, u32[]{:S(2)}, u32[]{:S(2)}) collective-permute-start(bf16[768,256]{1,0:T(8,128)(2,1)S(1)} %get-tuple-element.21), channel_id=1, source_target_pairs={{0,1},{1,0},{2,3},{3,2},{4,5},{5,4},{6,7},{7,6},{8,9},{9,8},{10,11... | collective-permute-start | bytes 1179656 | tf_op jit(solution)/shard_map/ppermute | solution.py:318
  44.2 10.0 %collective-permute-start.10 = (bf16[768,256]{1,0:T(8,128)(2,1)S(1)}, bf16[768,256]{1,0:T(8,128)(2,1)S(1)}, u32[]{:S(2)}, u32[]{:S(2)}) collective-permute-start(bf16[768,256]{1,0:T(8,128)(2,1)S(1)} %add_convert_fusion.1.x.refs_0_), channel_id=1, source_target_pairs={{0,2},{1,5},{2,0},{3,7},{4,6},{5,1},{6,4},{7,3},{8,10},{9,13},{10,... | collective-permute-start | bytes 1179656 | tf_op jit(solution)/shard_map/ppermute | solution.py:325
  46.3 16.3 %collective-permute-start.17 = (bf16[768,256]{1,0:T(8,128)(2,1)S(1)}, bf16[768,256]{1,0:T(8,128)(2,1)S(1)}, u32[]{:S(2)}, u32[]{:S(2)}) collective-permute-start(bf16[768,256]{1,0:T(8,128)(2,1)S(1)} %add_convert_fusion.y.refs_0_), channel_id=1, source_target_pairs={{0,2},{1,5},{2,0},{3,7},{4,6},{5,1},{6,4},{7,3},{8,10},{9,13},{10,... | collective-permute-start | bytes 1179656 | tf_op jit(solution)/shard_map/ppermute | solution.py:325
  47.6 21.0 %collective-permute-start.11 = (bf16[768,256]{1,0:T(8,128)(2,1)S(1)}, bf16[768,256]{1,0:T(8,128)(2,1)S(1)}, u32[]{:S(2)}, u32[]{:S(2)}) collective-permute-start(bf16[768,256]{1,0:T(8,128)(2,1)S(1)} %add_convert_fusion.1.x.refs_0_), channel_id=1, source_target_pairs={{0,4},{1,3},{2,6},{3,1},{4,0},{5,7},{6,2},{7,5},{8,12},{9,11},{10,... | collective-permute-start | bytes 1179656 | tf_op jit(solution)/shard_map/ppermute | solution.py:325
  54.2 14.4 %collective-permute-start.12 = (bf16[768,256]{1,0:T(8,128)(2,1)S(1)}, bf16[768,256]{1,0:T(8,128)(2,1)S(1)}, u32[]{:S(2)}, u32[]{:S(2)}) collective-permute-start(bf16[768,256]{1,0:T(8,128)(2,1)S(1)} %collective-permute-done.10.refs_1_), channel_id=1, source_target_pairs={{0,4},{1,3},{2,6},{3,1},{4,0},{5,7},{6,2},{7,5},{8,12},{9,11},{10,... | collective-permute-start | bytes 1179656 | tf_op jit(solution)/shard_map/ppermute | solution.py:325
  56.7 13.8 %collective-permute-start.19 = (bf16[768,256]{1,0:T(8,128)(2,1)S(1)}, bf16[768,256]{1,0:T(8,128)(2,1)S(1)}, u32[]{:S(2)}, u32[]{:S(2)}) collective-permute-start(bf16[768,256]{1,0:T(8,128)(2,1)S(1)} %add_convert_fusion.y.refs_0_), channel_id=1, source_target_pairs={{0,4},{1,3},{2,6},{3,1},{4,0},{5,7},{6,2},{7,5},{8,12},{9,11},{10,... | collective-permute-start | bytes 1179656 | tf_op jit(solution)/shard_map/ppermute | solution.py:325
  62.6 9.8 %collective-permute-start.18 = (bf16[768,256]{1,0:T(8,128)(2,1)S(1)}, bf16[768,256]{1,0:T(8,128)(2,1)S(1)}, u32[]{:S(2)}, u32[]{:S(2)}) collective-permute-start(bf16[768,256]{1,0:T(8,128)(2,1)S(1)} %collective-permute-done.17.refs_1_), channel_id=1, source_target_pairs={{0,4},{1,3},{2,6},{3,1},{4,0},{5,7},{6,2},{7,5},{8,12},{9,11},{10,... | collective-permute-start | bytes 1179656 | tf_op jit(solution)/shard_map/ppermute | solution.py:325
  70.4 3.0 %collective-permute-start.13 = (bf16[512,256]{1,0:T(8,128)(2,1)S(1)}, bf16[512,256]{1,0:T(8,128)(2,1)S(1)}, u32[]{:S(2)}, u32[]{:S(2)}) collective-permute-start(bf16[512,256]{1,0:T(8,128)(2,1)S(1)} %get-tuple-element.23), channel_id=1, source_target_pairs={{0,1},{1,0},{2,3},{3,2},{4,5},{5,4},{6,7},{7,6},{8,9},{9,8},{10,11... | collective-permute-start | bytes 786440 | tf_op jit(solution)/shard_map/ppermute | solution.py:318
  72.8 17.1 %copy-start.2 = (f32[512,128]{1,0:T(8,128)S(1)}, f32[512,128]{1,0:T(8,128)}, u32[]{:S(2)}) copy-start(f32[512,128]{1,0:T(8,128)} %rhs.1) | copy-start | bytes 786436
  72.8 6.0 %collective-permute-start.20 = (bf16[512,256]{1,0:T(8,128)(2,1)S(1)}, bf16[512,256]{1,0:T(8,128)(2,1)S(1)}, u32[]{:S(2)}, u32[]{:S(2)}) collective-permute-start(bf16[512,256]{1,0:T(8,128)(2,1)S(1)} %last_part.3), channel_id=1, source_target_pairs={{0,1},{1,0},{2,3},{3,2},{4,5},{5,4},{6,7},{7,6},{8,9},{9,8},{10,11... | collective-permute-start | bytes 786440 | tf_op jit(solution)/shard_map/ppermute | solution.py:318
  73.6 9.9 %collective-permute-start.14 = (bf16[256,128]{1,0:T(8,128)(2,1)S(1)}, bf16[256,128]{1,0:T(8,128)(2,1)S(1)}, u32[]{:S(2)}, u32[]{:S(2)}) collective-permute-start(bf16[256,128]{1,0:T(8,128)(2,1)S(1)} %get-tuple-element.25), channel_id=1, source_target_pairs={{0,8},{8,0},{16,24},{24,16},{1,9},{9,1},{17,25},{25,17},{2,10},{10... | collective-permute-start | bytes 196616 | tf_op jit(solution)/shard_map/ppermute | solution.py:366
  76.2 8.6 %collective-permute-start.15 = (bf16[256,128]{1,0:T(8,128)(2,1)S(1)}, bf16[256,128]{1,0:T(8,128)(2,1)S(1)}, u32[]{:S(2)}, u32[]{:S(2)}) collective-permute-start(bf16[256,128]{1,0:T(8,128)(2,1)S(1)} %get-tuple-element.26), channel_id=1, source_target_pairs={{0,16},{8,24},{16,0},{24,8},{1,17},{9,25},{17,1},{25,9},{2,18},{10... | collective-permute-start | bytes 196616 | tf_op jit(solution)/shard_map/ppermute | solution.py:366
  78.8 6.8 %collective-permute-start.16 = (bf16[256,128]{1,0:T(8,128)(2,1)S(1)}, bf16[256,128]{1,0:T(8,128)(2,1)S(1)}, u32[]{:S(2)}, u32[]{:S(2)}) collective-permute-start(bf16[256,128]{1,0:T(8,128)(2,1)S(1)} %get-tuple-element.27), channel_id=1, source_target_pairs={{0,24},{8,16},{16,8},{24,0},{1,25},{9,17},{17,9},{25,1},{2,26},{10... | collective-permute-start | bytes 196616 | tf_op jit(solution)/shard_map/ppermute | solution.py:366
  79.1 6.5 %collective-permute-start.21 = (bf16[256,128]{1,0:T(8,128)(2,1)S(1)}, bf16[256,128]{1,0:T(8,128)(2,1)S(1)}, u32[]{:S(2)}, u32[]{:S(2)}) collective-permute-start(bf16[256,128]{1,0:T(8,128)(2,1)S(1)} %get-tuple-element.31), channel_id=1, source_target_pairs={{0,8},{8,0},{16,24},{24,16},{1,9},{9,1},{17,25},{25,17},{2,10},{10... | collective-permute-start | bytes 196616 | tf_op jit(solution)/shard_map/ppermute | solution.py:366
  80.0 9.8 %collective-permute-start.22 = (bf16[256,128]{1,0:T(8,128)(2,1)S(1)}, bf16[256,128]{1,0:T(8,128)(2,1)S(1)}, u32[]{:S(2)}, u32[]{:S(2)}) collective-permute-start(bf16[256,128]{1,0:T(8,128)(2,1)S(1)} %get-tuple-element.32), channel_id=1, source_target_pairs={{0,16},{8,24},{16,0},{24,8},{1,17},{9,25},{17,1},{25,9},{2,18},{10... | collective-permute-start | bytes 196616 | tf_op jit(solution)/shard_map/ppermute | solution.py:366
  83.5 6.3 %collective-permute-start.23 = (bf16[256,128]{1,0:T(8,128)(2,1)S(1)}, bf16[256,128]{1,0:T(8,128)(2,1)S(1)}, u32[]{:S(2)}, u32[]{:S(2)}) collective-permute-start(bf16[256,128]{1,0:T(8,128)(2,1)S(1)} %get-tuple-element.33), channel_id=1, source_target_pairs={{0,24},{8,16},{16,8},{24,0},{1,25},{9,17},{17,9},{25,1},{2,26},{10... | collective-permute-start | bytes 196616 | tf_op jit(solution)/shard_map/ppermute | solution.py:366

commit v7 on v6

--- a/solution.py
+++ b/solution.py
@@ -280,8 +280,10 @@
 
 
 def finish_kernel(n, rhs, *refs):
-    groups, out = (refs[:n], refs[n : 2 * n]), refs[2 * n]
-    first, second = (sum((g[...].astype(F32) for g in group[1:]), group[0][...]) for group in groups)
+    groups, out = (refs[:n], refs[n:-1]), refs[-1]
+    first, second = (
+        sum((g[...].astype(F32) for g in group[1:]), group[0][...]) for group in groups
+    )
     rows = first.shape[0]
     low = low_lanes(first.shape)
     out[:rows] = rhs[:rows] - jnp.where(low, first, swap_halves(second))
@@ -296,7 +298,7 @@
     return pl.pallas_call(
         functools.partial(finish_kernel, n),
         out_shape=jax.ShapeDtypeStruct(rhs.shape, F32),
-        in_specs=[VMEM] * (1 + 2 * n),
+        in_specs=[VMEM] * (1 + n + len(groups[1])),
         out_specs=VMEM,
         compiler_params=pltpu.CompilerParams(vmem_limit_bytes=4 << 20),
         name="finish",
@@ -364,6 +366,8 @@
         group = list(split(own, other, leaves))
         for d in range(1, leaves):
             group[d] = lax.ppermute(group[d], "leaf", [(j, j ^ d) for j in range(leaves)])
+        if not c:
+            group = [sum((g.astype(F32) for g in group[1:]), group[0])]
         groups.append(group)
 
     solution = join(*solved, leaves)

time: 90.8 us -> 91.8 us (1.011)
  transfers between devices with their start and end apart: 24 -> 24, of which waited for: 10 -> 11; matrix products, arithmetic and copies ran while one was open for 0% -> 0% of each run, Pallas kernels for 21% -> 21%
where the time goes in v7:
time: 91.8 us; the launch traced here: 91.6 us
  waiting for transfers between devices  32.8 us (36%)
  starting transfers between devices  31.2 us (34%)
  Pallas kernels  22.9 us (25%)
  local copies, waits for them, and re-layouts  3.58 us (4%)
    ppermute x12, waiting for transfers between devices, gather(): pieces.append(lax.ppermute(pieces[p], 'row', pairs))  26.9 us
    ppermute x12, starting transfers between devices, gather(): pieces.append(lax.ppermute(pieces[p], 'row', pairs))  20.2 us
    ppermute x6, starting transfers between devices, on_device(): lax.ppermute(group[d], 'leaf', [(j, j ^ d) for j in range(leaves)])  9.29 us
    pallas_call x4, Pallas kernels, partials(): pl.pallas_call(functools.partial(partial_kernel, n, first, bool(sums)), o...  8.35 us
    pallas_call x2, Pallas kernels, select_rows(): pl.pallas_call(functools.partial(select_kernel, masks, other), out_shape=...  6.65 us
    ppermute x6, waiting for transfers between devices, on_device(): lax.ppermute(group[d], 'leaf', [(j, j ^ d) for j in range(leaves)])  5.94 us
    unnamed x18, local copies, waits for them, and re-layouts  3.58 us
    pallas_call x2, Pallas kernels, pick(): pl.pallas_call(functools.partial(pick_kernel, masks, other), out_shape=ja...  3.15 us
  transfers between devices with their start and end apart: 24, of which 11 were waited for; matrix products, arithmetic and copies ran while one was open for 0% of the time, Pallas kernels for 21%

profile of v7, /device:TPU:0, one launch (start us, length us, event | category | flops | bytes accessed | tf_op | source)
XLA Modules:
  0.0 91.6 jit_solution(16601038568078774985)
XLA Ops:
  0.6 0.0 slice-start
  0.7 0.0 slice-start.1
  0.7 2.6 %pick.3 = bf16[768,3072]{1,0:T(8,128)(2,1)S(1)} custom-call(bf16[768,6144]{1,0:T(8,128)(2,1)} %bitcast.4), custom_call_target="tpu_custom_call" | custom-call | tf_op jit(solution)/shard_map/pick/pallas_call | solution.py:65
  3.2 0.6 collective-permute-start
  3.8 3.5 %copy-done = bf16[1,512,6144]{2,1,0:T(8,128)(2,1)S(1)} copy-done((bf16[1,512,6144]{2,1,0:T(8,128)(2,1)S(1)}, bf16[1,512,6144]{2,1,0:T(8,128)(2,1)}, u32[]{:S(2)}) %copy-start) | copy-done | bytes 6291480
  7.3 3.2 %select_rows.3 = bf16[512,3072]{1,0:T(8,128)(2,1)S(1)} custom-call(s32[1,512]{1,0:T(1,128)S(1)} %copy-done.3, bf16[512,6144]{1,0:T(8,128)(2,1)S(1)} %bitcast.8), custom_call_target="tpu_custom_call" | custom-call | tf_op jit(solution)/shard_map/select_rows/pallas_call | solution.py:100
  10.6 0.1 collective-permute-start.9
  10.7 1.3 %chunk.2.refs_0_ = bf16[768,256]{1,0:T(8,128)(2,1)S(1)} custom-call(bf16[768,512]{1,0:T(8,128)(2,1)} %bitcast.12), custom_call_target="tpu_custom_call" | custom-call | tf_op jit(solution)/shard_map/chunk/pallas_call | solution.py:213
  11.9 2.8 %collective-permute-start.1 = (bf16[768,256]{1,0:T(8,128)(2,1)S(1)}, bf16[768,256]{1,0:T(8,128)(2,1)S(1)}, u32[]{:S(2)}, u32[]{:S(2)}) collective-permute-start(bf16[768,256]{1,0:T(8,128)(2,1)S(1)} %chunk.2.refs_0_), channel_id=1, source_target_pairs={{0,2},{1,5},{2,0},{3,7},{4,6},{5,1},{6,4},{7,3},{8,10},{9,13},{10,... | collective-permute-start | bytes 1179656 | tf_op jit(solution)/shard_map/ppermute | solution.py:327
  14.8 1.5 %collective-permute-start.2 = (bf16[768,256]{1,0:T(8,128)(2,1)S(1)}, bf16[768,256]{1,0:T(8,128)(2,1)S(1)}, u32[]{:S(2)}, u32[]{:S(2)}) collective-permute-start(bf16[768,256]{1,0:T(8,128)(2,1)S(1)} %chunk.2.refs_0_), channel_id=1, source_target_pairs={{0,4},{1,3},{2,6},{3,1},{4,0},{5,7},{6,2},{7,5},{8,12},{9,11},{10,... | collective-permute-start | bytes 1179656 | tf_op jit(solution)/shard_map/ppermute | solution.py:327
  16.3 0.2 chunk.3.refs_0_
  16.5 0.6 collective-permute-start.5
  17.1 6.7 %collective-permute-done.1.refs_1_ = bf16[768,256]{1,0:T(8,128)(2,1)S(1)} collective-permute-done((bf16[768,256]{1,0:T(8,128)(2,1)S(1)}, bf16[768,256]{1,0:T(8,128)(2,1)S(1)}, u32[]{:S(2)}, u32[]{:S(2)}) %collective-permute-start.1) | collective-permute-done | bytes 393248 | tf_op jit(solution)/shard_map/ppermute | solution.py:327
  23.8 2.4 %collective-permute-start.3 = (bf16[768,256]{1,0:T(8,128)(2,1)S(1)}, bf16[768,256]{1,0:T(8,128)(2,1)S(1)}, u32[]{:S(2)}, u32[]{:S(2)}) collective-permute-start(bf16[768,256]{1,0:T(8,128)(2,1)S(1)} %collective-permute-done.1.refs_1_), channel_id=1, source_target_pairs={{0,4},{1,3},{2,6},{3,1},{4,0},{5,7},{6,2},{7,5},{8,12},{9,11},{10,... | collective-permute-start | bytes 1179656 | tf_op jit(solution)/shard_map/ppermute | solution.py:327
  26.1 0.6 collective-permute-done.2.refs_2_
  26.7 1.5 %collective-permute-start.6 = (bf16[768,256]{1,0:T(8,128)(2,1)S(1)}, bf16[768,256]{1,0:T(8,128)(2,1)S(1)}, u32[]{:S(2)}, u32[]{:S(2)}) collective-permute-start(bf16[768,256]{1,0:T(8,128)(2,1)S(1)} %chunk.3.refs_0_), channel_id=1, source_target_pairs={{0,4},{1,3},{2,6},{3,1},{4,0},{5,7},{6,2},{7,5},{8,12},{9,11},{10,... | collective-permute-start | bytes 1179656 | tf_op jit(solution)/shard_map/ppermute | solution.py:327
  28.3 3.5 %collective-permute-done.5.refs_1_ = bf16[768,256]{1,0:T(8,128)(2,1)S(1)} collective-permute-done((bf16[768,256]{1,0:T(8,128)(2,1)S(1)}, bf16[768,256]{1,0:T(8,128)(2,1)S(1)}, u32[]{:S(2)}, u32[]{:S(2)}) %collective-permute-start.5) | collective-permute-done | bytes 393248 | tf_op jit(solution)/shard_map/ppermute | solution.py:327
  31.8 1.8 %collective-permute-start.7 = (bf16[768,256]{1,0:T(8,128)(2,1)S(1)}, bf16[768,256]{1,0:T(8,128)(2,1)S(1)}, u32[]{:S(2)}, u32[]{:S(2)}) collective-permute-start(bf16[768,256]{1,0:T(8,128)(2,1)S(1)} %collective-permute-done.5.refs_1_), channel_id=1, source_target_pairs={{0,4},{1,3},{2,6},{3,1},{4,0},{5,7},{6,2},{7,5},{8,12},{9,11},{10,... | collective-permute-start | bytes 1179656 | tf_op jit(solution)/shard_map/ppermute | solution.py:327
  33.5 0.6 pick.2.keep
  34.1 0.0 collective-permute-done.3.refs_3_
  34.2 2.6 %partials.4 = (f32[768,256]{1,0:T(8,128)S(1)}, bf16[768,256]{1,0:T(8,128)(2,1)S(1)}) custom-call(bf16[768,3072]{1,0:T(8,128)(2,1)S(1)} %pick.2.keep, bf16[768,3072]{1,0:T(8,128)(2,1)S(1)} %collective-permute-done.swap, bf16[768,256]{1,0:T(8,128)(2,1)S(1)} %chunk.2.refs_0_, bf16[768,256]{1,0:T(8,128)(2,1)S(1)} %collective-permute-done.1.refs_1_, ...), custom_call_target="tpu_custom_call" | custom-call | tf_op jit(solution)/shard_map/partials/pallas_call | solution.py:131
  36.8 0.0 slice-start.3
  36.8 0.0 slice-start.4
  36.8 0.1 collective-permute-start.4
  36.9 0.1 collective-permute-done.6.refs_2_
  37.0 4.2 %collective-permute-done.7.refs_3_ = bf16[768,256]{1,0:T(8,128)(2,1)S(1)} collective-permute-done((bf16[768,256]{1,0:T(8,128)(2,1)S(1)}, bf16[768,256]{1,0:T(8,128)(2,1)S(1)}, u32[]{:S(2)}, u32[]{:S(2)}) %collective-permute-start.7) | collective-permute-done | bytes 393248 | tf_op jit(solution)/shard_map/ppermute | solution.py:327
  41.2 2.6 %partials.5 = (f32[768,256]{1,0:T(8,128)S(1)}, bf16[768,256]{1,0:T(8,128)(2,1)S(1)}) custom-call(bf16[768,3072]{1,0:T(8,128)(2,1)S(1)} %pick.2.keep, bf16[768,3072]{1,0:T(8,128)(2,1)S(1)} %collective-permute-done.swap, bf16[768,256]{1,0:T(8,128)(2,1)S(1)} %chunk.3.refs_0_, bf16[768,256]{1,0:T(8,128)(2,1)S(1)} %collective-permute-done.5.refs_1_, ...), custom_call_target="tpu_custom_call" | custom-call | tf_op jit(solution)/shard_map/partials/pallas_call | solution.py:131
  43.8 0.3 collective-permute-start.8
  44.1 0.0 collective-permute-done.4
  44.1 0.1 add_convert_fusion.1.x.refs_0_
  44.2 2.1 %collective-permute-start.10 = (bf16[768,256]{1,0:T(8,128)(2,1)S(1)}, bf16[768,256]{1,0:T(8,128)(2,1)S(1)}, u32[]{:S(2)}, u32[]{:S(2)}) collective-permute-start(bf16[768,256]{1,0:T(8,128)(2,1)S(1)} %add_convert_fusion.1.x.refs_0_), channel_id=1, source_target_pairs={{0,2},{1,5},{2,0},{3,7},{4,6},{5,1},{6,4},{7,3},{8,10},{9,13},{10,... | collective-permute-start | bytes 1179656 | tf_op jit(solution)/shard_map/ppermute | solution.py:327
  46.2 0.1 add_convert_fusion.y.refs_0_
  46.3 1.3 %collective-permute-start.17 = (bf16[768,256]{1,0:T(8,128)(2,1)S(1)}, bf16[768,256]{1,0:T(8,128)(2,1)S(1)}, u32[]{:S(2)}, u32[]{:S(2)}) collective-permute-start(bf16[768,256]{1,0:T(8,128)(2,1)S(1)} %add_convert_fusion.y.refs_0_), channel_id=1, source_target_pairs={{0,2},{1,5},{2,0},{3,7},{4,6},{5,1},{6,4},{7,3},{8,10},{9,13},{10,... | collective-permute-start | bytes 1179656 | tf_op jit(solution)/shard_map/ppermute | solution.py:327
  47.6 1.3 %collective-permute-start.11 = (bf16[768,256]{1,0:T(8,128)(2,1)S(1)}, bf16[768,256]{1,0:T(8,128)(2,1)S(1)}, u32[]{:S(2)}, u32[]{:S(2)}) collective-permute-start(bf16[768,256]{1,0:T(8,128)(2,1)S(1)} %add_convert_fusion.1.x.refs_0_), channel_id=1, source_target_pairs={{0,4},{1,3},{2,6},{3,1},{4,0},{5,7},{6,2},{7,5},{8,12},{9,11},{10,... | collective-permute-start | bytes 1179656 | tf_op jit(solution)/shard_map/ppermute | solution.py:327
  48.9 5.3 %collective-permute-done.10.refs_1_ = bf16[768,256]{1,0:T(8,128)(2,1)S(1)} collective-permute-done((bf16[768,256]{1,0:T(8,128)(2,1)S(1)}, bf16[768,256]{1,0:T(8,128)(2,1)S(1)}, u32[]{:S(2)}, u32[]{:S(2)}) %collective-permute-start.10) | collective-permute-done | bytes 393248 | tf_op jit(solution)/shard_map/ppermute | solution.py:327
  54.2 2.5 %collective-permute-start.12 = (bf16[768,256]{1,0:T(8,128)(2,1)S(1)}, bf16[768,256]{1,0:T(8,128)(2,1)S(1)}, u32[]{:S(2)}, u32[]{:S(2)}) collective-permute-start(bf16[768,256]{1,0:T(8,128)(2,1)S(1)} %collective-permute-done.10.refs_1_), channel_id=1, source_target_pairs={{0,4},{1,3},{2,6},{3,1},{4,0},{5,7},{6,2},{7,5},{8,12},{9,11},{10,... | collective-permute-start | bytes 1179656 | tf_op jit(solution)/shard_map/ppermute | solution.py:327
  56.7 0.0 collective-permute-start.19
  56.7 5.9 %collective-permute-done.17.refs_1_ = bf16[768,256]{1,0:T(8,128)(2,1)S(1)} collective-permute-done((bf16[768,256]{1,0:T(8,128)(2,1)S(1)}, bf16[768,256]{1,0:T(8,128)(2,1)S(1)}, u32[]{:S(2)}, u32[]{:S(2)}) %collective-permute-start.17) | collective-permute-done | bytes 393248 | tf_op jit(solution)/shard_map/ppermute | solution.py:327
  62.6 2.5 %collective-permute-start.18 = (bf16[768,256]{1,0:T(8,128)(2,1)S(1)}, bf16[768,256]{1,0:T(8,128)(2,1)S(1)}, u32[]{:S(2)}, u32[]{:S(2)}) collective-permute-start(bf16[768,256]{1,0:T(8,128)(2,1)S(1)} %collective-permute-done.17.refs_1_), channel_id=1, source_target_pairs={{0,4},{1,3},{2,6},{3,1},{4,0},{5,7},{6,2},{7,5},{8,12},{9,11},{10,... | collective-permute-start | bytes 1179656 | tf_op jit(solution)/shard_map/ppermute | solution.py:327
  65.1 3.4 %select_rows.2.keep.block = bf16[512,3072]{1,0:T(8,128)(2,1)S(1)} custom-call(s32[1,512]{1,0:T(1,128)S(1)} %copy-done.3, bf16[512,6144]{1,0:T(8,128)(2,1)S(1)} %bitcast.11), custom_call_target="tpu_custom_call" | custom-call | tf_op jit(solution)/shard_map/select_rows/pallas_call | solution.py:100
  68.5 0.0 collective-permute-done.11.refs_2_
  68.6 0.0 collective-permute-done.12.refs_3_
  68.6 1.8 %partials.6 = (f32[512,256]{1,0:T(8,128)S(1)}, bf16[512,256]{1,0:T(8,128)(2,1)S(1)}) custom-call(bf16[512,3072]{1,0:T(8,128)(2,1)S(1)} %select_rows.2.keep.block, bf16[512,3072]{1,0:T(8,128)(2,1)S(1)} %collective-permute-done.9.swap.block, bf16[768,256]{1,0:T(8,128)(2,1)S(1)} %add_convert_fusion.1.x.refs_0_, ...), custom_call_target="tpu_custom_call" | custom-call | tf_op jit(solution)/shard_map/partials/pallas_call | solution.py:131
  70.4 0.1 collective-permute-start.13
  70.4 0.0 collective-permute-done.19.refs_2_
  70.5 1.4 %partials.7 = (f32[512,256]{1,0:T(8,128)S(1)}, f32[512,256]{1,0:T(8,128)S(1)}) custom-call(bf16[512,3072]{1,0:T(8,128)(2,1)S(1)} %select_rows.2.keep.block, bf16[512,3072]{1,0:T(8,128)(2,1)S(1)} %collective-permute-done.9.swap.block, bf16[768,256]{1,0:T(8,128)(2,1)S(1)} %add_convert_fusion.y.refs_0_, bf16[768,256]{1,0:T(8,128)(2,1)S(1)} %collective-permute-done.17.refs_1_, ...), custom_call_target="tpu_custom_call" | custom-call | tf_op jit(solution)/shard_map/partials/pallas_call | solution.py:131
  71.8 0.5 collective-permute-done.18.piece
  72.4 0.4 last_part.3
  72.8 0.0 copy-start.2
  72.8 0.6 collective-permute-start.20
  73.3 0.0 collective-permute-done.13.other
  73.3 0.3 split.2
  73.6 4.2 %collective-permute-start.16 = (bf16[256,128]{1,0:T(8,128)(2,1)S(1)}, bf16[256,128]{1,0:T(8,128)(2,1)S(1)}, u32[]{:S(2)}, u32[]{:S(2)}) collective-permute-start(bf16[256,128]{1,0:T(8,128)(2,1)S(1)} %get-tuple-element.27), channel_id=1, source_target_pairs={{0,24},{8,16},{16,8},{24,0},{1,25},{9,17},{17,9},{25,1},{2,26},{10... | collective-permute-start | bytes 196616 | tf_op jit(solution)/shard_map/ppermute | solution.py:368
  77.8 0.6 collective-permute-start.14
  78.4 1.2 %join.1 = bf16[768,512]{1,0:T(8,128)(2,1)} custom-call(bf16[768,256]{1,0:T(8,128)(2,1)S(1)} %add_convert_fusion.1.x.refs_0_, bf16[768,256]{1,0:T(8,128)(2,1)S(1)} %add_convert_fusion.y.refs_0_), custom_call_target="tpu_custom_call" | custom-call | tf_op jit(solution)/shard_map/join/pallas_call | solution.py:238
  79.7 0.4 last_part.2.own
  80.0 0.3 split.3
  80.3 1.5 %collective-permute-start.21 = (bf16[256,128]{1,0:T(8,128)(2,1)S(1)}, bf16[256,128]{1,0:T(8,128)(2,1)S(1)}, u32[]{:S(2)}, u32[]{:S(2)}) collective-permute-start(bf16[256,128]{1,0:T(8,128)(2,1)S(1)} %get-tuple-element.31), channel_id=1, source_target_pairs={{0,8},{8,0},{16,24},{24,16},{1,9},{9,1},{17,25},{25,17},{2,10},{10... | collective-permute-start | bytes 196616 | tf_op jit(solution)/shard_map/ppermute | solution.py:368
  81.8 2.9 %collective-permute-start.22 = (bf16[256,128]{1,0:T(8,128)(2,1)S(1)}, bf16[256,128]{1,0:T(8,128)(2,1)S(1)}, u32[]{:S(2)}, u32[]{:S(2)}) collective-permute-start(bf16[256,128]{1,0:T(8,128)(2,1)S(1)} %get-tuple-element.32), channel_id=1, source_target_pairs={{0,16},{8,24},{16,0},{24,8},{1,17},{9,25},{17,1},{25,9},{2,18},{10... | collective-permute-start | bytes 196616 | tf_op jit(solution)/shard_map/ppermute | solution.py:368
  84.7 0.1 collective-permute-start.23
  84.8 0.8 collective-permute-done.21.refs_2_
  85.6 3.1 %collective-permute-done.22.refs_3_ = bf16[256,128]{1,0:T(8,128)(2,1)S(1)} collective-permute-done((bf16[256,128]{1,0:T(8,128)(2,1)S(1)}, bf16[256,128]{1,0:T(8,128)(2,1)S(1)}, u32[]{:S(2)}, u32[]{:S(2)}) %collective-permute-start.22) | collective-permute-done | bytes 65568 | tf_op jit(solution)/shard_map/ppermute | solution.py:368
  88.7 2.1 %collective-permute-done.23.refs_4_ = bf16[256,128]{1,0:T(8,128)(2,1)S(1)} collective-permute-done((bf16[256,128]{1,0:T(8,128)(2,1)S(1)}, bf16[256,128]{1,0:T(8,128)(2,1)S(1)}, u32[]{:S(2)}, u32[]{:S(2)}) %collective-permute-start.23) | collective-permute-done | bytes 65568 | tf_op jit(solution)/shard_map/ppermute | solution.py:368
  90.8 0.8 finish.1
  (23 shorter events, 0.1 us)
Async XLA Ops:
  0.6 3.2 %copy-start.3 = (s32[1,512]{1,0:T(1,128)S(1)}, s32[1,512]{1,0:T(1,128)}, u32[]{:S(2)}) copy-start(s32[1,512]{1,0:T(1,128)} %places.3) | copy-start | bytes 6148
  0.6 32.9 %slice-start = ((s8[9437184]{0:T(1024)(128)(4,1)}), s8[4194304]{0:T(1024)(128)(4,1)S(1)}, s32[]{:S(2)}) async-start(s8[9437184]{0:T(1024)(128)(4,1)} %bitcast.5), calls=%async_computation | async-start | bytes 8388608
  0.7 32.9 %slice-start.1 = ((s8[9437184]{0:T(1024)(128)(4,1)}), s8[4194304]{0:T(1024)(128)(4,1)S(1)}, s32[]{:S(2)}) async-start(s8[9437184]{0:T(1024)(128)(4,1)} %bitcast.5), calls=%async_computation.1 | async-start | bytes 8388608
  3.2 30.9 %collective-permute-start = (bf16[768,3072]{1,0:T(8,128)(2,1)S(1)}, bf16[768,3072]{1,0:T(8,128)(2,1)S(1)}, u32[]{:S(2)}, u32[]{:S(2)}) collective-permute-start(bf16[768,3072]{1,0:T(8,128)(2,1)S(1)} %pick.3), channel_id=1, source_target_pairs={{0,1},{1,0},{2,3},{3,2},{4,5},{5,4},{6,7},{7,6},{8,9},{9,8},{10,11... | collective-permute-start | bytes 14155784 | tf_op jit(solution)/shard_map/ppermute | solution.py:320
  3.8 3.5 %copy-start = (bf16[1,512,6144]{2,1,0:T(8,128)(2,1)S(1)}, bf16[1,512,6144]{2,1,0:T(8,128)(2,1)}, u32[]{:S(2)}) copy-start(bf16[1,512,6144]{2,1,0:T(8,128)(2,1)} %param.7) | copy-start | bytes 18874372
  7.3 9.0 %copy-start.1 = (bf16[1,768,512]{2,1,0:T(8,128)(2,1)S(1)}, bf16[1,768,512]{2,1,0:T(8,128)(2,1)}, u32[]{:S(2)}) copy-start(bf16[1,768,512]{2,1,0:T(8,128)(2,1)} %param.6) | copy-start | bytes 2359300
  7.3 26.2 %slice-start.2 = ((s8[9437184]{0:T(1024)(128)(4,1)}), s8[1048576]{0:T(1024)(128)(4,1)S(1)}, s32[]{:S(2)}) async-start(s8[9437184]{0:T(1024)(128)(4,1)} %bitcast.5), calls=%async_computation.2 | async-start | bytes 2097152
  10.6 58.0 %collective-permute-start.9 = (bf16[512,3072]{1,0:T(8,128)(2,1)S(1)}, bf16[512,3072]{1,0:T(8,128)(2,1)S(1)}, u32[]{:S(2)}, u32[]{:S(2)}) collective-permute-start(bf16[512,3072]{1,0:T(8,128)(2,1)S(1)} %select_rows.3), channel_id=1, source_target_pairs={{0,1},{1,0},{2,3},{3,2},{4,5},{5,4},{6,7},{7,6},{8,9},{9,8},{10,11... | collective-permute-start | bytes 9437192 | tf_op jit(solution)/shard_map/ppermute | solution.py:320
  11.9 11.8 %collective-permute-start.1 = (bf16[768,256]{1,0:T(8,128)(2,1)S(1)}, bf16[768,256]{1,0:T(8,128)(2,1)S(1)}, u32[]{:S(2)}, u32[]{:S(2)}) collective-permute-start(bf16[768,256]{1,0:T(8,128)(2,1)S(1)} %chunk.2.refs_0_), channel_id=1, source_target_pairs={{0,2},{1,5},{2,0},{3,7},{4,6},{5,1},{6,4},{7,3},{8,10},{9,13},{10,... | collective-permute-start | bytes 1179656 | tf_op jit(solution)/shard_map/ppermute | solution.py:327
  14.8 12.0 %collective-permute-start.2 = (bf16[768,256]{1,0:T(8,128)(2,1)S(1)}, bf16[768,256]{1,0:T(8,128)(2,1)S(1)}, u32[]{:S(2)}, u32[]{:S(2)}) collective-permute-start(bf16[768,256]{1,0:T(8,128)(2,1)S(1)} %chunk.2.refs_0_), channel_id=1, source_target_pairs={{0,4},{1,3},{2,6},{3,1},{4,0},{5,7},{6,2},{7,5},{8,12},{9,11},{10,... | collective-permute-start | bytes 1179656 | tf_op jit(solution)/shard_map/ppermute | solution.py:327
  16.5 15.3 %collective-permute-start.5 = (bf16[768,256]{1,0:T(8,128)(2,1)S(1)}, bf16[768,256]{1,0:T(8,128)(2,1)S(1)}, u32[]{:S(2)}, u32[]{:S(2)}) collective-permute-start(bf16[768,256]{1,0:T(8,128)(2,1)S(1)} %chunk.3.refs_0_), channel_id=1, source_target_pairs={{0,2},{1,5},{2,0},{3,7},{4,6},{5,1},{6,4},{7,3},{8,10},{9,13},{10,... | collective-permute-start | bytes 1179656 | tf_op jit(solution)/shard_map/ppermute | solution.py:327
  23.8 10.4 %collective-permute-start.3 = (bf16[768,256]{1,0:T(8,128)(2,1)S(1)}, bf16[768,256]{1,0:T(8,128)(2,1)S(1)}, u32[]{:S(2)}, u32[]{:S(2)}) collective-permute-start(bf16[768,256]{1,0:T(8,128)(2,1)S(1)} %collective-permute-done.1.refs_1_), channel_id=1, source_target_pairs={{0,4},{1,3},{2,6},{3,1},{4,0},{5,7},{6,2},{7,5},{8,12},{9,11},{10,... | collective-permute-start | bytes 1179656 | tf_op jit(solution)/shard_map/ppermute | solution.py:327
  26.7 10.2 %collective-permute-start.6 = (bf16[768,256]{1,0:T(8,128)(2,1)S(1)}, bf16[768,256]{1,0:T(8,128)(2,1)S(1)}, u32[]{:S(2)}, u32[]{:S(2)}) collective-permute-start(bf16[768,256]{1,0:T(8,128)(2,1)S(1)} %chunk.3.refs_0_), channel_id=1, source_target_pairs={{0,4},{1,3},{2,6},{3,1},{4,0},{5,7},{6,2},{7,5},{8,12},{9,11},{10,... | collective-permute-start | bytes 1179656 | tf_op jit(solution)/shard_map/ppermute | solution.py:327
  31.8 9.4 %collective-permute-start.7 = (bf16[768,256]{1,0:T(8,128)(2,1)S(1)}, bf16[768,256]{1,0:T(8,128)(2,1)S(1)}, u32[]{:S(2)}, u32[]{:S(2)}) collective-permute-start(bf16[768,256]{1,0:T(8,128)(2,1)S(1)} %collective-permute-done.5.refs_1_), channel_id=1, source_target_pairs={{0,4},{1,3},{2,6},{3,1},{4,0},{5,7},{6,2},{7,5},{8,12},{9,11},{10,... | collective-permute-start | bytes 1179656 | tf_op jit(solution)/shard_map/ppermute | solution.py:327
  36.8 28.4 %slice-start.3 = ((s8[6291456]{0:T(1024)(128)(4,1)}), s8[4194304]{0:T(1024)(128)(4,1)S(1)}, s32[]{:S(2)}) async-start(s8[6291456]{0:T(1024)(128)(4,1)} %bitcast.9), calls=%async_computation.3 | async-start | bytes 8388608
  36.8 28.3 %slice-start.4 = ((s8[6291456]{0:T(1024)(128)(4,1)}), s8[2097152]{0:T(1024)(128)(4,1)S(1)}, s32[]{:S(2)}) async-start(s8[6291456]{0:T(1024)(128)(4,1)} %bitcast.9), calls=%async_computation.4 | async-start | bytes 4194304
  36.8 7.3 %collective-permute-start.4 = (bf16[768,256]{1,0:T(8,128)(2,1)S(1)}, bf16[768,256]{1,0:T(8,128)(2,1)S(1)}, u32[]{:S(2)}, u32[]{:S(2)}) collective-permute-start(bf16[768,256]{1,0:T(8,128)(2,1)S(1)} %get-tuple-element.19), channel_id=1, source_target_pairs={{0,1},{1,0},{2,3},{3,2},{4,5},{5,4},{6,7},{7,6},{8,9},{9,8},{10,11... | collective-permute-start | bytes 1179656 | tf_op jit(solution)/shard_map/ppermute | solution.py:320
  43.8 2.5 %collective-permute-start.8 = (bf16[768,256]{1,0:T(8,128)(2,1)S(1)}, bf16[768,256]{1,0:T(8,128)(2,1)S(1)}, u32[]{:S(2)}, u32[]{:S(2)}) collective-permute-start(bf16[768,256]{1,0:T(8,128)(2,1)S(1)} %get-tuple-element.21), channel_id=1, source_target_pairs={{0,1},{1,0},{2,3},{3,2},{4,5},{5,4},{6,7},{7,6},{8,9},{9,8},{10,11... | collective-permute-start | bytes 1179656 | tf_op jit(solution)/shard_map/ppermute | solution.py:320
  44.2 10.0 %collective-permute-start.10 = (bf16[768,256]{1,0:T(8,128)(2,1)S(1)}, bf16[768,256]{1,0:T(8,128)(2,1)S(1)}, u32[]{:S(2)}, u32[]{:S(2)}) collective-permute-start(bf16[768,256]{1,0:T(8,128)(2,1)S(1)} %add_convert_fusion.1.x.refs_0_), channel_id=1, source_target_pairs={{0,2},{1,5},{2,0},{3,7},{4,6},{5,1},{6,4},{7,3},{8,10},{9,13},{10,... | collective-permute-start | bytes 1179656 | tf_op jit(solution)/shard_map/ppermute | solution.py:327
  46.3 16.3 %collective-permute-start.17 = (bf16[768,256]{1,0:T(8,128)(2,1)S(1)}, bf16[768,256]{1,0:T(8,128)(2,1)S(1)}, u32[]{:S(2)}, u32[]{:S(2)}) collective-permute-start(bf16[768,256]{1,0:T(8,128)(2,1)S(1)} %add_convert_fusion.y.refs_0_), channel_id=1, source_target_pairs={{0,2},{1,5},{2,0},{3,7},{4,6},{5,1},{6,4},{7,3},{8,10},{9,13},{10,... | collective-permute-start | bytes 1179656 | tf_op jit(solution)/shard_map/ppermute | solution.py:327
  47.6 21.0 %collective-permute-start.11 = (bf16[768,256]{1,0:T(8,128)(2,1)S(1)}, bf16[768,256]{1,0:T(8,128)(2,1)S(1)}, u32[]{:S(2)}, u32[]{:S(2)}) collective-permute-start(bf16[768,256]{1,0:T(8,128)(2,1)S(1)} %add_convert_fusion.1.x.refs_0_), channel_id=1, source_target_pairs={{0,4},{1,3},{2,6},{3,1},{4,0},{5,7},{6,2},{7,5},{8,12},{9,11},{10,... | collective-permute-start | bytes 1179656 | tf_op jit(solution)/shard_map/ppermute | solution.py:327
  54.2 14.4 %collective-permute-start.12 = (bf16[768,256]{1,0:T(8,128)(2,1)S(1)}, bf16[768,256]{1,0:T(8,128)(2,1)S(1)}, u32[]{:S(2)}, u32[]{:S(2)}) collective-permute-start(bf16[768,256]{1,0:T(8,128)(2,1)S(1)} %collective-permute-done.10.refs_1_), channel_id=1, source_target_pairs={{0,4},{1,3},{2,6},{3,1},{4,0},{5,7},{6,2},{7,5},{8,12},{9,11},{10,... | collective-permute-start | bytes 1179656 | tf_op jit(solution)/shard_map/ppermute | solution.py:327
  56.7 13.8 %collective-permute-start.19 = (bf16[768,256]{1,0:T(8,128)(2,1)S(1)}, bf16[768,256]{1,0:T(8,128)(2,1)S(1)}, u32[]{:S(2)}, u32[]{:S(2)}) collective-permute-start(bf16[768,256]{1,0:T(8,128)(2,1)S(1)} %add_convert_fusion.y.refs_0_), channel_id=1, source_target_pairs={{0,4},{1,3},{2,6},{3,1},{4,0},{5,7},{6,2},{7,5},{8,12},{9,11},{10,... | collective-permute-start | bytes 1179656 | tf_op jit(solution)/shard_map/ppermute | solution.py:327
  62.6 9.8 %collective-permute-start.18 = (bf16[768,256]{1,0:T(8,128)(2,1)S(1)}, bf16[768,256]{1,0:T(8,128)(2,1)S(1)}, u32[]{:S(2)}, u32[]{:S(2)}) collective-permute-start(bf16[768,256]{1,0:T(8,128)(2,1)S(1)} %collective-permute-done.17.refs_1_), channel_id=1, source_target_pairs={{0,4},{1,3},{2,6},{3,1},{4,0},{5,7},{6,2},{7,5},{8,12},{9,11},{10,... | collective-permute-start | bytes 1179656 | tf_op jit(solution)/shard_map/ppermute | solution.py:327
  70.4 3.0 %collective-permute-start.13 = (bf16[512,256]{1,0:T(8,128)(2,1)S(1)}, bf16[512,256]{1,0:T(8,128)(2,1)S(1)}, u32[]{:S(2)}, u32[]{:S(2)}) collective-permute-start(bf16[512,256]{1,0:T(8,128)(2,1)S(1)} %get-tuple-element.23), channel_id=1, source_target_pairs={{0,1},{1,0},{2,3},{3,2},{4,5},{5,4},{6,7},{7,6},{8,9},{9,8},{10,11... | collective-permute-start | bytes 786440 | tf_op jit(solution)/shard_map/ppermute | solution.py:320
  72.8 18.0 %copy-start.2 = (f32[512,128]{1,0:T(8,128)S(1)}, f32[512,128]{1,0:T(8,128)}, u32[]{:S(2)}) copy-start(f32[512,128]{1,0:T(8,128)} %rhs.1) | copy-start | bytes 786436
  72.8 7.3 %collective-permute-start.20 = (bf16[512,256]{1,0:T(8,128)(2,1)S(1)}, bf16[512,256]{1,0:T(8,128)(2,1)S(1)}, u32[]{:S(2)}, u32[]{:S(2)}) collective-permute-start(bf16[512,256]{1,0:T(8,128)(2,1)S(1)} %last_part.3), channel_id=1, source_target_pairs={{0,1},{1,0},{2,3},{3,2},{4,5},{5,4},{6,7},{7,6},{8,9},{9,8},{10,11... | collective-permute-start | bytes 786440 | tf_op jit(solution)/shard_map/ppermute | solution.py:320
  73.6 11.1 %collective-permute-start.16 = (bf16[256,128]{1,0:T(8,128)(2,1)S(1)}, bf16[256,128]{1,0:T(8,128)(2,1)S(1)}, u32[]{:S(2)}, u32[]{:S(2)}) collective-permute-start(bf16[256,128]{1,0:T(8,128)(2,1)S(1)} %get-tuple-element.27), channel_id=1, source_target_pairs={{0,24},{8,16},{16,8},{24,0},{1,25},{9,17},{17,9},{25,1},{2,26},{10... | collective-permute-start | bytes 196616 | tf_op jit(solution)/shard_map/ppermute | solution.py:368
  77.8 7.0 %collective-permute-start.15 = (bf16[256,128]{1,0:T(8,128)(2,1)S(1)}, bf16[256,128]{1,0:T(8,128)(2,1)S(1)}, u32[]{:S(2)}, u32[]{:S(2)}) collective-permute-start(bf16[256,128]{1,0:T(8,128)(2,1)S(1)} %get-tuple-element.26), channel_id=1, source_target_pairs={{0,16},{8,24},{16,0},{24,8},{1,17},{9,25},{17,1},{25,9},{2,18},{10... | collective-permute-start | bytes 196616 | tf_op jit(solution)/shard_map/ppermute | solution.py:368
  77.8 7.0 %collective-permute-start.14 = (bf16[256,128]{1,0:T(8,128)(2,1)S(1)}, bf16[256,128]{1,0:T(8,128)(2,1)S(1)}, u32[]{:S(2)}, u32[]{:S(2)}) collective-permute-start(bf16[256,128]{1,0:T(8,128)(2,1)S(1)} %get-tuple-element.25), channel_id=1, source_target_pairs={{0,8},{8,0},{16,24},{24,16},{1,9},{9,1},{17,25},{25,17},{2,10},{10... | collective-permute-start | bytes 196616 | tf_op jit(solution)/shard_map/ppermute | solution.py:368
  80.3 5.3 %collective-permute-start.21 = (bf16[256,128]{1,0:T(8,128)(2,1)S(1)}, bf16[256,128]{1,0:T(8,128)(2,1)S(1)}, u32[]{:S(2)}, u32[]{:S(2)}) collective-permute-start(bf16[256,128]{1,0:T(8,128)(2,1)S(1)} %get-tuple-element.31), channel_id=1, source_target_pairs={{0,8},{8,0},{16,24},{24,16},{1,9},{9,1},{17,25},{25,17},{2,10},{10... | collective-permute-start | bytes 196616 | tf_op jit(solution)/shard_map/ppermute | solution.py:368
  81.8 6.9 %collective-permute-start.22 = (bf16[256,128]{1,0:T(8,128)(2,1)S(1)}, bf16[256,128]{1,0:T(8,128)(2,1)S(1)}, u32[]{:S(2)}, u32[]{:S(2)}) collective-permute-start(bf16[256,128]{1,0:T(8,128)(2,1)S(1)} %get-tuple-element.32), channel_id=1, source_target_pairs={{0,16},{8,24},{16,0},{24,8},{1,17},{9,25},{17,1},{25,9},{2,18},{10... | collective-permute-start | bytes 196616 | tf_op jit(solution)/shard_map/ppermute | solution.py:368
  84.7 6.1 %collective-permute-start.23 = (bf16[256,128]{1,0:T(8,128)(2,1)S(1)}, bf16[256,128]{1,0:T(8,128)(2,1)S(1)}, u32[]{:S(2)}, u32[]{:S(2)}) collective-permute-start(bf16[256,128]{1,0:T(8,128)(2,1)S(1)} %get-tuple-element.33), channel_id=1, source_target_pairs={{0,24},{8,16},{16,8},{24,0},{1,25},{9,17},{17,9},{25,1},{2,26},{10... | collective-permute-start | bytes 196616 | tf_op jit(solution)/shard_map/ppermute | solution.py:368
